TPU v7x, 128 devices: a whole 4x4x4 slice. The times are simulated.
128 devices in a mesh: cap: 16 (over y, x), tile: 8 (over z, core).
Axes of the slice: x: 4, y: 4, z: 4, core: 2. Of those that a mesh axis runs over, the one named last changes fastest.
Arguments:
- load: float32 [3, 32, 1536, 128], P(None, 'cap', 'tile'), may hold values from -6 to 6
- previous: float32 [3, 32, 1536, 128], P(None, 'cap', 'tile'), may hold values from -4 to 4
- stress_old: float32 [12, 32, 1536, 128], P(None, 'cap', 'tile'), may hold values from -6 to 6
- shear_modulus: float32 [32, 1536, 128], P('cap', 'tile'), may hold values from 0.5 to 5
- relaxation: float32 [32, 1536, 128], P('cap', 'tile'), may hold values from 0.05 to 2
- density_jump: float32 [32], P('cap'), may hold values from 0.2 to 2
- element_stiffness: float32 [12, 12], replicated, may hold values from -2.9 to 3.4, as said below
- degree_slots: int32 [768], replicated, may hold values from 0 to 767, each once
Outputs:
- displacement: float32 [3, 32, 1536, 128], P(None, 'cap', 'tile')
- stress_new: float32 [12, 32, 1536, 128], P(None, 'cap', 'tile')
- potential_coeffs: float32 [768, 32, 256], P('tile', 'cap')
Inputs may be any that keep to these rules, and one draw needn't show every extreme that they name: `element_stiffness`: symmetric positive definite. `degree_slots`: each degree 0 to 767 sits in exactly one slot.
All inputs are finite; a program needn't handle non-finite values.
Results may differ from a plain program's by a relative error of at most 0.00013.
Values sent between devices are 32-bit elements; how exact they have to be, the bound alone decides.
No kernel may reach another device: no remote copies, remote signals or barrier semaphores. Data moves between devices by JAX's collectives and lax.ppermute only.
A program may use at most 128 MiB of HBM per device.

v0:
```python
import functools
import math

import jax
import jax.numpy as jnp
from jax import lax
from jax.sharding import Mesh
from jax.sharding import PartitionSpec as P

HRING = 1536
LDEG = 768
ITERS = 6
TILE = ("tile_0", "tile_1")
CAP = ("cap_0", "cap_1")
CAP_TILE = ("cap_0", "cap_1", "tile_0", "tile_1")


precise = lax.Precision.HIGHEST
rotation_gain = 2.0
gravity_gain = 0.2


def from_behind(block, axis, distance):
    devices = range(lax.axis_size(axis))
    route = [((i - distance) % len(devices), i) for i in devices]
    return lax.ppermute(block, axis, route)


def from_behind_2(block, axis, distance):
    devices = range(lax.axis_size(axis))
    route = [(i - distance, i) for i in devices if i - distance in devices]
    return lax.ppermute(block, axis, route)


def by_axis(shard, axes):
    return functools.reduce(lax.psum, axes, shard)


def split_up(shard, dim, length):
    before, after = (shard.shape[:dim], shard.shape[dim + 1 :])
    return jnp.moveaxis(shard.reshape(*before, length, -1, *after), dim, 0)


def sum_at_owner(shard, axis, dim):
    length = lax.axis_size(axis)
    tiles = lax.all_to_all(split_up(shard, dim, length), axis, 0, 0, tiled=True)
    return jnp.sum(tiles, axis=0)


def sent_to_all(shard, axis):
    length = lax.axis_size(axis)
    return lax.all_to_all(
        jnp.broadcast_to(shard[None], (length, *shard.shape)), axis, 0, 0, tiled=True
    )


def joined_along(tiles, dim):
    dims = list(tiles.shape[1:])
    dims[dim] *= tiles.shape[0]
    return jnp.moveaxis(tiles, 0, dim).reshape(dims)


def gather_directly(shard, axis, dim):
    tiles = sent_to_all(shard, axis)
    return joined_along(tiles, dim)


def radius_rows(amount, layers):
    positions = jnp.arange(amount, dtype=jnp.int32).astype(jnp.float32)
    return 1.0 - 0.45 * (positions + 0.5) / layers


def cycle_basis(degrees, columns):
    windings = degrees[:, None] * columns[None, :] % HRING
    angles = windings.astype(jnp.float32) * (2.0 * math.pi / HRING)
    return (jnp.cos(angles), jnp.sin(angles))


def green_kernel(degrees, target_radius, source_radius):
    degree_float = degrees.astype(jnp.float32)
    distance = jnp.abs(jnp.log(target_radius)[:, None] - jnp.log(source_radius)[None, :])
    return (
        jnp.exp(-degree_float[:, None, None] * distance[None])
        / jnp.sqrt(2.0 * degree_float + 1.0)[:, None, None]
    )


def rotation_term(degrees, radius_list, moment):
    selector = (degrees == 2).astype(jnp.float32)
    return (
        rotation_gain
        * selector[:, None, None]
        * (radius_list**2)[None, :, None]
        * moment[:, None, :]
    )


def extend_field(nodal_field):
    edge_column = from_behind(nodal_field[:, :, :1, :], TILE, -1)
    widened = jnp.concatenate([nodal_field, edge_column], axis=2)
    bottom = from_behind_2(widened[:, :1], CAP, -1)
    return jnp.concatenate([widened, bottom], axis=1)


def corner_values(extended):
    shallow = extended[:, :-1]
    deeper = extended[:, 1:]
    stacked = jnp.stack(
        [shallow[:, :, :-1], shallow[:, :, 1:], deeper[:, :, :-1], deeper[:, :, 1:]], axis=1
    )
    return stacked.reshape((12,) + stacked.shape[2:])


def element_forces(nodal_field, stiffness, effective):
    values = corner_values(extend_field(nodal_field))
    return effective[None] * jnp.einsum("ab,brhs->arhs", stiffness, values, precision=precise)


def place_corner(portion, top_pad, left_pad):
    return jnp.pad(portion, ((0, 0), (top_pad, 1 - top_pad), (left_pad, 1 - left_pad), (0, 0)))


def fold_forces(forces):
    grouped = forces.reshape((3, 4) + forces.shape[1:])
    row_count = forces.shape[1]
    col_count = forces.shape[2]
    padded_sum = place_corner(grouped[:, 0], 0, 0) + place_corner(grouped[:, 1], 0, 1)
    padded_sum = padded_sum + place_corner(grouped[:, 2], 1, 0) + place_corner(grouped[:, 3], 1, 1)
    spill_column = from_behind(padded_sum[:, :, col_count:, :], TILE, 1)
    interior = padded_sum[:, :, :col_count, :] + jnp.pad(
        spill_column, ((0, 0), (0, 0), (0, col_count - 1), (0, 0))
    )
    spill_row = from_behind_2(interior[:, row_count:], CAP, 1)
    return interior[:, :row_count] + jnp.pad(
        spill_row, ((0, 0), (0, row_count - 1), (0, 0), (0, 0))
    )


def joint_sums(vector, applied):
    return (
        by_axis(jnp.sum(vector * vector), CAP_TILE),
        by_axis(jnp.sum(vector * applied), CAP_TILE),
    )


def body(
    load,
    previous,
    stress_old,
    shear_modulus,
    relaxation,
    density_jump,
    element_stiffness,
    degree_slots,
):
    effective = shear_modulus / (1.0 + 0.5 * relaxation)
    carried_share = relaxation / (1.0 + 0.5 * relaxation)
    retained = (1.0 - 0.5 * relaxation) / (1.0 + 0.5 * relaxation)
    sections = load.shape[3]
    depth_rows = load.shape[1]
    cycle_cols = load.shape[2]
    cap_count = lax.axis_size(CAP)
    tile_count = lax.axis_size(TILE)
    layers = depth_rows * cap_count
    slot_count = LDEG // tile_count
    cap_place = lax.axis_index(CAP)
    tile_place = lax.axis_index(TILE)
    columns = tile_place * cycle_cols + jnp.arange(cycle_cols, dtype=jnp.int32)
    weighted = previous[0] * density_jump[:, None, None]
    normalizer = math.sqrt(2.0 / HRING)
    start_forces = element_forces(previous, element_stiffness, effective)
    residual = fold_forces(carried_share[None] * stress_old - start_forces) + load
    degrees = degree_slots
    cosine, sine_table = cycle_basis(degrees, columns)
    first_half = jnp.einsum("kh,rhs->krs", cosine, weighted, precision=precise)
    second_half = jnp.einsum("kh,rhs->krs", sine_table, weighted, precision=precise)
    coefficients = sum_at_owner(
        jnp.concatenate([first_half, second_half], axis=2) * normalizer, TILE, 0
    )
    own_degrees = lax.dynamic_slice_in_dim(degree_slots, tile_place * slot_count, slot_count, 0)
    quarter = slot_count // cap_count
    item_degrees = lax.dynamic_slice_in_dim(own_degrees, cap_place * quarter, quarter, 0)
    radius_all = radius_rows(layers, layers)
    columns_part = lax.all_to_all(coefficients, CAP, split_axis=0, concat_axis=1, tiled=True)
    kernel = green_kernel(item_degrees, radius_all, radius_all)
    result = jnp.einsum("kij,kjs->kis", kernel, columns_part, precision=precise)
    moment = jnp.einsum("j,kjs->ks", radius_all**4 / layers, columns_part, precision=precise)
    profiles = result + rotation_term(item_degrees, radius_all, moment)
    potential = lax.all_to_all(profiles, CAP, split_axis=1, concat_axis=0, tiled=True)
    portion = gather_directly(potential, TILE, 0)
    degrees = degree_slots
    cosine, sine_table = cycle_basis(degrees, columns)
    running = jnp.einsum("krs,kh->rhs", portion[:, :, :sections], cosine, precision=precise)
    surface_field = running + jnp.einsum(
        "krs,kh->rhs", portion[:, :, sections:], sine_table, precision=precise
    )
    gravity_force = gravity_gain * density_jump[:, None, None] * surface_field
    residual = residual + jnp.concatenate([gravity_force[None], jnp.zeros_like(load[1:])], axis=0)
    forces = element_forces(residual, element_stiffness, effective)
    applied = fold_forces(forces)
    norm_now, product = joint_sums(residual, applied)
    step_size = norm_now / product

    def iterate(counter, carry_state):
        (
            solution,
            residual,
            direction,
            applied_dir,
            direction_forces,
            elastic,
            norm_now,
            step_size,
        ) = carry_state
        solution = solution + step_size * direction
        residual = residual - step_size * applied_dir
        elastic = elastic + step_size * direction_forces
        forces = element_forces(residual, element_stiffness, effective)
        applied = fold_forces(forces)
        norm_next, product = joint_sums(residual, applied)
        growth = norm_next / norm_now
        step_size = norm_next / (product - growth * norm_next / step_size)
        direction = residual + growth * direction
        applied_dir = applied + growth * applied_dir
        direction_forces = forces + growth * direction_forces
        return (
            solution,
            residual,
            direction,
            applied_dir,
            direction_forces,
            elastic,
            norm_next,
            step_size,
        )

    start_state = (previous, residual, residual, applied, forces, start_forces, norm_now, step_size)
    final_state = lax.fori_loop(0, ITERS - 1, iterate, start_state)
    solution = final_state[0] + final_state[7] * final_state[2]
    elastic = final_state[5] + final_state[7] * final_state[4]
    stress_new = retained[None] * stress_old + elastic
    return (solution, stress_new, potential)


def solution(mesh):
    torus = Mesh(mesh.devices.reshape(4, 4, 4, 2), ("cap_0", "cap_1", "tile_0", "tile_1"))
    return jax.shard_map(
        body,
        mesh=torus,
        in_specs=(
            P(None, CAP, TILE, None),
            P(None, CAP, TILE, None),
            P(None, CAP, TILE, None),
            P(CAP, TILE, None),
            P(CAP, TILE, None),
            P(CAP),
            P(),
            P(),
        ),
        out_specs=(P(None, CAP, TILE, None), P(None, CAP, TILE, None), P(TILE, CAP, None)),
        check_vma=False,
    )
```

profile of v0, /device:TPU:1, one launch (start us, length us, event | category | flops | bytes accessed | tf_op | source)
XLA Modules:
  0.0 585.1 jit_solution(14023895264266373132)
XLA Ops:
  2.5 4.4 fusion.20
  6.9 3.8 fusion.22
  12.0 6.9 %all-to-all-start = ((f32[8,96,2,256]{3,1,2,0:T(8,128)}), f32[8,96,2,256]{3,1,2,0:T(8,128)S(1)}, u32[]{:S(2)}, u32[]{:S(2)}) async-start(f32[8,96,2,256]{3,1,2,0:T(8,128)} %maximum_multiply_fusion), calls=%async_computation | async-start | bytes 3145728 | tf_op jit(solution)/shard_map/all_to_all | solution.py:46
  20.2 19.5 %all-to-all-done = f32[8,96,2,256]{3,1,2,0:T(8,128)S(1)} async-done(((f32[8,96,2,256]{3,1,2,0:T(8,128)}), f32[8,96,2,256]{3,1,2,0:T(8,128)S(1)}, u32[]{:S(2)}, u32[]{:S(2)}) %all-to-all-start) | async-done | bytes 1572896 | tf_op jit(solution)/shard_map/all_to_all | solution.py:46
  40.6 6.8 %all-to-all-start.1 = ((f32[96,2,256]{2,1,0:T(2,128)}), f32[96,2,256]{2,1,0:T(2,128)S(1)}, u32[]{:S(2)}, u32[]{:S(2)}) async-start(f32[96,2,256]{2,1,0:T(2,128)} %copy.149), calls=%async_computation.1 | async-start | bytes 393216 | tf_op jit(solution)/shard_map/all_to_all | solution.py:184
  49.3 5.4 all-to-all-done.1
  56.3 3.5 all-to-all-start.2
  60.2 7.1 %all-to-all-done.2 = f32[6,32,256]{2,0,1:T(8,128)S(1)} async-done(((f32[6,32,256]{2,0,1:T(8,128)}), f32[6,32,256]{2,0,1:T(8,128)S(1)}, u32[]{:S(2)}, u32[]{:S(2)}) %all-to-all-start.2) | async-done | bytes 196640 | tf_op jit(solution)/shard_map/all_to_all | solution.py:189
  69.5 7.7 %all-to-all-start.3 = ((f32[8,96,2,256]{3,1,2,0:T(8,128)}), f32[8,96,2,256]{3,1,2,0:T(8,128)}, u32[]{:S(2)}, u32[]{:S(2)}) async-start(f32[8,96,2,256]{3,1,2,0:T(8,128)} %broadcast_in_dim.7), calls=%async_computation.3 | async-start | bytes 3145728 | tf_op jit(solution)/shard_map/all_to_all | solution.py:52
  77.2 4.8 fusion.9
  85.8 8.7 %collective-permute-done.6 = f32[3,3,1,128]{3,2,1,0:T(1,128)S(1)} collective-permute-done((f32[3,3,1,128]{3,2,1,0:T(1,128)S(1)}, f32[3,3,1,128]{3,2,1,0:T(1,128)S(1)}, u32[]{:S(2)}, u32[]{:S(2)}) %collective-permute-start.6) | collective-permute-done | bytes 4640 | tf_op jit(solution)/shard_map/ppermute | solution.py:26
  107.5 3.7 collective-permute-done.8
  115.9 4.7 collective-permute-done.9
  121.2 4.9 fusion.7
  137.5 13.8 %all-reduce.25 = (f32[]{:T(128)}, f32[]{:T(128)}) all-reduce(f32[]{:T(128)} %get-tuple-element.174, f32[]{:T(128)} %get-tuple-element.173), channel_id=1, replica_groups=mesh['cap_0'=4,'cap_1'=4,'tile_0'=4,'tile_1'=2] {'cap_0'}, use_global_device_ids=true, to_apply=%region_2.3 | all-reduce | flops 2 | bytes 16 | tf_op jit(solution)/shard_map/psum | solution.py:36
  151.3 6.6 %all-reduce.24 = (f32[]{:T(128)}, f32[]{:T(128)}) all-reduce(f32[]{:T(128)} %get-tuple-element.209, f32[]{:T(128)} %get-tuple-element.210), channel_id=1, replica_groups=mesh['cap_0'=4,'cap_1'=4,'tile_0'=4,'tile_1'=2] {'cap_1'}, use_global_device_ids=true, to_apply=%region_3.4 | all-reduce | flops 2 | bytes 16 | tf_op jit(solution)/shard_map/psum | solution.py:36
  157.9 7.5 %all-reduce.23 = (f32[]{:T(128)}, f32[]{:T(128)}) all-reduce(f32[]{:T(128)} %get-tuple-element.207, f32[]{:T(128)} %get-tuple-element.208), channel_id=1, replica_groups=mesh['cap_0'=4,'cap_1'=4,'tile_0'=4,'tile_1'=2] {'tile_0'}, use_global_device_ids=true, to_apply=%region_4.5 | all-reduce | flops 2 | bytes 16 | tf_op jit(solution)/shard_map/psum | solution.py:36
  165.5 11.4 %all-reduce.26 = (f32[]{:T(128)}, f32[]{:T(128)}) all-reduce(f32[]{:T(128)} %get-tuple-element.205, f32[]{:T(128)} %get-tuple-element.206), channel_id=1, replica_groups=mesh['cap_0'=4,'cap_1'=4,'tile_0'=4,'tile_1'=2] {'tile_1'}, use_global_device_ids=true, to_apply=%region_5.6 | all-reduce | flops 2 | bytes 16 | tf_op jit(solution)/shard_map/psum | solution.py:36
  178.2 399.1 %while.26 = (s32[]{:T(128)}, f32[3,2,192,128]{3,2,1,0:T(8,128)S(1)}, f32[3,2,192,128]{3,2,1,0:T(8,128)S(1)}, f32[3,2,192,128]{3,2,1,0:T(8,128)S(1)}, f32[3,2,192...) while((s32[]{:T(128)}, ...), condition=%wide.region_22.23_spmd, body=%wide.region_11.22_spmd.sunk | while | flops 93275520 | bytes 65152024 | solution.py:238
  182.8 8.6 %collective-permute-done.1 = f32[3,1,193,128]{3,2,1,0:T(8,128)S(1)} collective-permute-done((f32[3,1,193,128]{3,2,1,0:T(8,128)S(1)}, f32[3,1,193,128]{3,2,1,0:T(8,128)S(1)}, u32[]{:S(2)}, u32[]{:S(2)}) %collective-permute-start.1) | collective-permute-done | bytes 296480 | tf_op jit(solution)/shard_map/while/body/eval_jaxpr/ppermute | solution.py:32
  191.8 5.8 multiply_bitcast_fusion.2
  202.5 3.4 collective-permute-start.3
  206.6 4.0 collective-permute-done.3
  211.4 10.8 %all-reduce.31 = (f32[]{:T(128)}, f32[]{:T(128)}) all-reduce(f32[]{:T(128)} %get-tuple-element.340, f32[]{:T(128)} %get-tuple-element.341), channel_id=1, replica_groups=mesh['cap_0'=4,'cap_1'=4,'tile_0'=4,'tile_1'=2] {'cap_0'}, use_global_device_ids=true, to_apply=%region_13.13 | all-reduce | flops 2 | bytes 16 | tf_op jit(solution)/shard_map/while/body/eval_jaxpr/psum | solution.py:36
  222.2 6.6 %all-reduce.32 = (f32[]{:T(128)}, f32[]{:T(128)}) all-reduce(f32[]{:T(128)} %get-tuple-element.342, f32[]{:T(128)} %get-tuple-element.343), channel_id=1, replica_groups=mesh['cap_0'=4,'cap_1'=4,'tile_0'=4,'tile_1'=2] {'cap_1'}, use_global_device_ids=true, to_apply=%region_14.14 | all-reduce | flops 2 | bytes 16 | tf_op jit(solution)/shard_map/while/body/eval_jaxpr/psum | solution.py:36
  228.8 9.3 %all-reduce.33 = (f32[]{:T(128)}, f32[]{:T(128)}) all-reduce(f32[]{:T(128)} %get-tuple-element.344, f32[]{:T(128)} %get-tuple-element.345), channel_id=1, replica_groups=mesh['cap_0'=4,'cap_1'=4,'tile_0'=4,'tile_1'=2] {'tile_0'}, use_global_device_ids=true, to_apply=%region_15.15 | all-reduce | flops 2 | bytes 16 | tf_op jit(solution)/shard_map/while/body/eval_jaxpr/psum | solution.py:36
  238.1 9.6 %all-reduce.34 = (f32[]{:T(128)}, f32[]{:T(128)}) all-reduce(f32[]{:T(128)} %get-tuple-element.346, f32[]{:T(128)} %get-tuple-element.347), channel_id=1, replica_groups=mesh['cap_0'=4,'cap_1'=4,'tile_0'=4,'tile_1'=2] {'tile_1'}, use_global_device_ids=true, to_apply=%region_16.16 | all-reduce | flops 2 | bytes 16 | tf_op jit(solution)/shard_map/while/body/eval_jaxpr/psum | solution.py:36
  250.4 7.2 %multiply_add_fusion.10 = (f32[12,2,192,128]{3,0,2,1:T(8,128)}, f32[12,2,192,128]{3,0,2,1:T(8,128)}) fusion(f32[12,2,192,128]{3,0,2,1:T(8,128)} %get-tuple-element.373, f32[12,2,192,128]{3,0,2,1:T(8,128)} %get-tuple-element.372, f32[]{:T(128)S(6)} %copy.228, f32[12,2,192,128]{3,0,2,1:T(8,128)} %copy-done, f32[]{:T(128)S(6)} %div.91), kind=kLoop, calls=%fused_computation.2.clone.1 | loop fusion | flops 2359296 | bytes 11796488 | tf_op jit(solution)/shard_map/while/body/eval_jaxpr/add | solution.py:217
  262.6 9.2 %collective-permute-done.1 = f32[3,1,193,128]{3,2,1,0:T(8,128)S(1)} collective-permute-done((f32[3,1,193,128]{3,2,1,0:T(8,128)S(1)}, f32[3,1,193,128]{3,2,1,0:T(8,128)S(1)}, u32[]{:S(2)}, u32[]{:S(2)}) %collective-permute-start.1) | collective-permute-done | bytes 296480 | tf_op jit(solution)/shard_map/while/body/eval_jaxpr/ppermute | solution.py:32
  272.1 5.8 multiply_bitcast_fusion.2
  282.8 3.4 collective-permute-start.3
  286.8 3.4 collective-permute-done.3
  291.1 11.4 %all-reduce.31 = (f32[]{:T(128)}, f32[]{:T(128)}) all-reduce(f32[]{:T(128)} %get-tuple-element.340, f32[]{:T(128)} %get-tuple-element.341), channel_id=1, replica_groups=mesh['cap_0'=4,'cap_1'=4,'tile_0'=4,'tile_1'=2] {'cap_0'}, use_global_device_ids=true, to_apply=%region_13.13 | all-reduce | flops 2 | bytes 16 | tf_op jit(solution)/shard_map/while/body/eval_jaxpr/psum | solution.py:36
  302.5 6.6 %all-reduce.32 = (f32[]{:T(128)}, f32[]{:T(128)}) all-reduce(f32[]{:T(128)} %get-tuple-element.342, f32[]{:T(128)} %get-tuple-element.343), channel_id=1, replica_groups=mesh['cap_0'=4,'cap_1'=4,'tile_0'=4,'tile_1'=2] {'cap_1'}, use_global_device_ids=true, to_apply=%region_14.14 | all-reduce | flops 2 | bytes 16 | tf_op jit(solution)/shard_map/while/body/eval_jaxpr/psum | solution.py:36
  309.1 9.7 %all-reduce.33 = (f32[]{:T(128)}, f32[]{:T(128)}) all-reduce(f32[]{:T(128)} %get-tuple-element.344, f32[]{:T(128)} %get-tuple-element.345), channel_id=1, replica_groups=mesh['cap_0'=4,'cap_1'=4,'tile_0'=4,'tile_1'=2] {'tile_0'}, use_global_device_ids=true, to_apply=%region_15.15 | all-reduce | flops 2 | bytes 16 | tf_op jit(solution)/shard_map/while/body/eval_jaxpr/psum | solution.py:36
  318.8 8.5 %all-reduce.34 = (f32[]{:T(128)}, f32[]{:T(128)}) all-reduce(f32[]{:T(128)} %get-tuple-element.346, f32[]{:T(128)} %get-tuple-element.347), channel_id=1, replica_groups=mesh['cap_0'=4,'cap_1'=4,'tile_0'=4,'tile_1'=2] {'tile_1'}, use_global_device_ids=true, to_apply=%region_16.16 | all-reduce | flops 2 | bytes 16 | tf_op jit(solution)/shard_map/while/body/eval_jaxpr/psum | solution.py:36
  330.0 7.2 %multiply_add_fusion.10 = (f32[12,2,192,128]{3,0,2,1:T(8,128)}, f32[12,2,192,128]{3,0,2,1:T(8,128)}) fusion(f32[12,2,192,128]{3,0,2,1:T(8,128)} %get-tuple-element.373, f32[12,2,192,128]{3,0,2,1:T(8,128)} %get-tuple-element.372, f32[]{:T(128)S(6)} %copy.228, f32[12,2,192,128]{3,0,2,1:T(8,128)} %copy-done, f32[]{:T(128)S(6)} %div.91), kind=kLoop, calls=%fused_computation.2.clone.1 | loop fusion | flops 2359296 | bytes 11796488 | tf_op jit(solution)/shard_map/while/body/eval_jaxpr/add | solution.py:217
  342.2 9.8 %collective-permute-done.1 = f32[3,1,193,128]{3,2,1,0:T(8,128)S(1)} collective-permute-done((f32[3,1,193,128]{3,2,1,0:T(8,128)S(1)}, f32[3,1,193,128]{3,2,1,0:T(8,128)S(1)}, u32[]{:S(2)}, u32[]{:S(2)}) %collective-permute-start.1) | collective-permute-done | bytes 296480 | tf_op jit(solution)/shard_map/while/body/eval_jaxpr/ppermute | solution.py:32
  352.3 5.8 multiply_bitcast_fusion.2
  362.2 3.4 collective-permute-start.3
  366.2 3.3 collective-permute-done.3
  370.3 10.2 %all-reduce.31 = (f32[]{:T(128)}, f32[]{:T(128)}) all-reduce(f32[]{:T(128)} %get-tuple-element.340, f32[]{:T(128)} %get-tuple-element.341), channel_id=1, replica_groups=mesh['cap_0'=4,'cap_1'=4,'tile_0'=4,'tile_1'=2] {'cap_0'}, use_global_device_ids=true, to_apply=%region_13.13 | all-reduce | flops 2 | bytes 16 | tf_op jit(solution)/shard_map/while/body/eval_jaxpr/psum | solution.py:36
  380.6 6.9 %all-reduce.32 = (f32[]{:T(128)}, f32[]{:T(128)}) all-reduce(f32[]{:T(128)} %get-tuple-element.342, f32[]{:T(128)} %get-tuple-element.343), channel_id=1, replica_groups=mesh['cap_0'=4,'cap_1'=4,'tile_0'=4,'tile_1'=2] {'cap_1'}, use_global_device_ids=true, to_apply=%region_14.14 | all-reduce | flops 2 | bytes 16 | tf_op jit(solution)/shard_map/while/body/eval_jaxpr/psum | solution.py:36
  387.4 11.0 %all-reduce.33 = (f32[]{:T(128)}, f32[]{:T(128)}) all-reduce(f32[]{:T(128)} %get-tuple-element.344, f32[]{:T(128)} %get-tuple-element.345), channel_id=1, replica_groups=mesh['cap_0'=4,'cap_1'=4,'tile_0'=4,'tile_1'=2] {'tile_0'}, use_global_device_ids=true, to_apply=%region_15.15 | all-reduce | flops 2 | bytes 16 | tf_op jit(solution)/shard_map/while/body/eval_jaxpr/psum | solution.py:36
  398.4 8.8 %all-reduce.34 = (f32[]{:T(128)}, f32[]{:T(128)}) all-reduce(f32[]{:T(128)} %get-tuple-element.346, f32[]{:T(128)} %get-tuple-element.347), channel_id=1, replica_groups=mesh['cap_0'=4,'cap_1'=4,'tile_0'=4,'tile_1'=2] {'tile_1'}, use_global_device_ids=true, to_apply=%region_16.16 | all-reduce | flops 2 | bytes 16 | tf_op jit(solution)/shard_map/while/body/eval_jaxpr/psum | solution.py:36
  409.8 7.2 %multiply_add_fusion.10 = (f32[12,2,192,128]{3,0,2,1:T(8,128)}, f32[12,2,192,128]{3,0,2,1:T(8,128)}) fusion(f32[12,2,192,128]{3,0,2,1:T(8,128)} %get-tuple-element.373, f32[12,2,192,128]{3,0,2,1:T(8,128)} %get-tuple-element.372, f32[]{:T(128)S(6)} %copy.228, f32[12,2,192,128]{3,0,2,1:T(8,128)} %copy-done, f32[]{:T(128)S(6)} %div.91), kind=kLoop, calls=%fused_computation.2.clone.1 | loop fusion | flops 2359296 | bytes 11796488 | tf_op jit(solution)/shard_map/while/body/eval_jaxpr/add | solution.py:217
  422.1 9.2 %collective-permute-done.1 = f32[3,1,193,128]{3,2,1,0:T(8,128)S(1)} collective-permute-done((f32[3,1,193,128]{3,2,1,0:T(8,128)S(1)}, f32[3,1,193,128]{3,2,1,0:T(8,128)S(1)}, u32[]{:S(2)}, u32[]{:S(2)}) %collective-permute-start.1) | collective-permute-done | bytes 296480 | tf_op jit(solution)/shard_map/while/body/eval_jaxpr/ppermute | solution.py:32
  431.7 5.8 multiply_bitcast_fusion.2
  441.8 3.4 collective-permute-start.3
  450.0 10.8 %all-reduce.31 = (f32[]{:T(128)}, f32[]{:T(128)}) all-reduce(f32[]{:T(128)} %get-tuple-element.340, f32[]{:T(128)} %get-tuple-element.341), channel_id=1, replica_groups=mesh['cap_0'=4,'cap_1'=4,'tile_0'=4,'tile_1'=2] {'cap_0'}, use_global_device_ids=true, to_apply=%region_13.13 | all-reduce | flops 2 | bytes 16 | tf_op jit(solution)/shard_map/while/body/eval_jaxpr/psum | solution.py:36
  460.8 6.8 %all-reduce.32 = (f32[]{:T(128)}, f32[]{:T(128)}) all-reduce(f32[]{:T(128)} %get-tuple-element.342, f32[]{:T(128)} %get-tuple-element.343), channel_id=1, replica_groups=mesh['cap_0'=4,'cap_1'=4,'tile_0'=4,'tile_1'=2] {'cap_1'}, use_global_device_ids=true, to_apply=%region_14.14 | all-reduce | flops 2 | bytes 16 | tf_op jit(solution)/shard_map/while/body/eval_jaxpr/psum | solution.py:36
  467.6 10.9 %all-reduce.33 = (f32[]{:T(128)}, f32[]{:T(128)}) all-reduce(f32[]{:T(128)} %get-tuple-element.344, f32[]{:T(128)} %get-tuple-element.345), channel_id=1, replica_groups=mesh['cap_0'=4,'cap_1'=4,'tile_0'=4,'tile_1'=2] {'tile_0'}, use_global_device_ids=true, to_apply=%region_15.15 | all-reduce | flops 2 | bytes 16 | tf_op jit(solution)/shard_map/while/body/eval_jaxpr/psum | solution.py:36
  478.4 8.8 %all-reduce.34 = (f32[]{:T(128)}, f32[]{:T(128)}) all-reduce(f32[]{:T(128)} %get-tuple-element.346, f32[]{:T(128)} %get-tuple-element.347), channel_id=1, replica_groups=mesh['cap_0'=4,'cap_1'=4,'tile_0'=4,'tile_1'=2] {'tile_1'}, use_global_device_ids=true, to_apply=%region_16.16 | all-reduce | flops 2 | bytes 16 | tf_op jit(solution)/shard_map/while/body/eval_jaxpr/psum | solution.py:36
  489.8 7.2 %multiply_add_fusion.10 = (f32[12,2,192,128]{3,0,2,1:T(8,128)}, f32[12,2,192,128]{3,0,2,1:T(8,128)}) fusion(f32[12,2,192,128]{3,0,2,1:T(8,128)} %get-tuple-element.373, f32[12,2,192,128]{3,0,2,1:T(8,128)} %get-tuple-element.372, f32[]{:T(128)S(6)} %copy.228, f32[12,2,192,128]{3,0,2,1:T(8,128)} %copy-done, f32[]{:T(128)S(6)} %div.91), kind=kLoop, calls=%fused_computation.2.clone.1 | loop fusion | flops 2359296 | bytes 11796488 | tf_op jit(solution)/shard_map/while/body/eval_jaxpr/add | solution.py:217
  502.0 9.8 %collective-permute-done.1 = f32[3,1,193,128]{3,2,1,0:T(8,128)S(1)} collective-permute-done((f32[3,1,193,128]{3,2,1,0:T(8,128)S(1)}, f32[3,1,193,128]{3,2,1,0:T(8,128)S(1)}, u32[]{:S(2)}, u32[]{:S(2)}) %collective-permute-start.1) | collective-permute-done | bytes 296480 | tf_op jit(solution)/shard_map/while/body/eval_jaxpr/ppermute | solution.py:32
  512.2 5.8 multiply_bitcast_fusion.2
  522.0 3.4 collective-permute-start.3
  526.1 3.3 collective-permute-done.3
  530.2 10.2 %all-reduce.31 = (f32[]{:T(128)}, f32[]{:T(128)}) all-reduce(f32[]{:T(128)} %get-tuple-element.340, f32[]{:T(128)} %get-tuple-element.341), channel_id=1, replica_groups=mesh['cap_0'=4,'cap_1'=4,'tile_0'=4,'tile_1'=2] {'cap_0'}, use_global_device_ids=true, to_apply=%region_13.13 | all-reduce | flops 2 | bytes 16 | tf_op jit(solution)/shard_map/while/body/eval_jaxpr/psum | solution.py:36
  540.4 6.9 %all-reduce.32 = (f32[]{:T(128)}, f32[]{:T(128)}) all-reduce(f32[]{:T(128)} %get-tuple-element.342, f32[]{:T(128)} %get-tuple-element.343), channel_id=1, replica_groups=mesh['cap_0'=4,'cap_1'=4,'tile_0'=4,'tile_1'=2] {'cap_1'}, use_global_device_ids=true, to_apply=%region_14.14 | all-reduce | flops 2 | bytes 16 | tf_op jit(solution)/shard_map/while/body/eval_jaxpr/psum | solution.py:36
  547.3 11.0 %all-reduce.33 = (f32[]{:T(128)}, f32[]{:T(128)}) all-reduce(f32[]{:T(128)} %get-tuple-element.344, f32[]{:T(128)} %get-tuple-element.345), channel_id=1, replica_groups=mesh['cap_0'=4,'cap_1'=4,'tile_0'=4,'tile_1'=2] {'tile_0'}, use_global_device_ids=true, to_apply=%region_15.15 | all-reduce | flops 2 | bytes 16 | tf_op jit(solution)/shard_map/while/body/eval_jaxpr/psum | solution.py:36
  558.3 8.8 %all-reduce.34 = (f32[]{:T(128)}, f32[]{:T(128)}) all-reduce(f32[]{:T(128)} %get-tuple-element.346, f32[]{:T(128)} %get-tuple-element.347), channel_id=1, replica_groups=mesh['cap_0'=4,'cap_1'=4,'tile_0'=4,'tile_1'=2] {'tile_1'}, use_global_device_ids=true, to_apply=%region_16.16 | all-reduce | flops 2 | bytes 16 | tf_op jit(solution)/shard_map/while/body/eval_jaxpr/psum | solution.py:36
  569.7 7.2 %multiply_add_fusion.10 = (f32[12,2,192,128]{3,0,2,1:T(8,128)}, f32[12,2,192,128]{3,0,2,1:T(8,128)}) fusion(f32[12,2,192,128]{3,0,2,1:T(8,128)} %get-tuple-element.373, f32[12,2,192,128]{3,0,2,1:T(8,128)} %get-tuple-element.372, f32[]{:T(128)S(6)} %copy.228, f32[12,2,192,128]{3,0,2,1:T(8,128)} %copy-done, f32[]{:T(128)S(6)} %div.91), kind=kLoop, calls=%fused_computation.2.clone.1 | loop fusion | flops 2359296 | bytes 11796488 | tf_op jit(solution)/shard_map/while/body/eval_jaxpr/add | solution.py:217
  578.2 6.4 %fusion.11 = f32[12,2,192,128]{3,2,1,0:T(8,128)} fusion(f32[12,2,192,128]{3,0,2,1:T(8,128)} %get-tuple-element.147, f32[12,2,192,128]{3,0,2,1:T(8,128)} %get-tuple-element.148, f32[12,2,192,128]{3,2,1,0:T(8,128)} %param.12, f32[]{:T(128)} %get-tuple-element.145, f32[2,192,128]{2,1,0:T(8,128)} %get-tuple-element.240), kind=kLoop, calls=%fused_computation.36 | loop fusion | flops 2359296 | bytes 9633796 | tf_op jit(solution)/shard_map/add | solution.py:241
  (206 shorter events, 101.4 us)
Async XLA Ops:
  0.6 6.3 %copy-start.11 = (f32[2]{0:T(128)S(1)}, f32[2]{0:T(128)}, u32[]{:S(2)}) copy-start(f32[2]{0:T(128)} %param.15) | copy-start | bytes 28
  12.0 7.0 %copy-start.10 = (s32[768]{0:T(1024)S(1)}, s32[768]{0:T(1024)}, u32[]{:S(2)}) copy-start(s32[768]{0:T(1024)} %param.17) | copy-start | bytes 9220
  12.0 7.3 %copy-start.8 = (f32[2,192,128]{2,1,0:T(8,128)S(1)}, f32[2,192,128]{2,1,0:T(8,128)}, u32[]{:S(2)}) copy-start(f32[2,192,128]{2,1,0:T(8,128)} %param.14) | copy-start | bytes 589828
  12.0 7.3 %copy-start.9 = (f32[2,192,128]{2,1,0:T(8,128)S(1)}, f32[2,192,128]{2,1,0:T(8,128)}, u32[]{:S(2)}) copy-start(f32[2,192,128]{2,1,0:T(8,128)} %param.13) | copy-start | bytes 589828
  12.0 27.7 %all-to-all-start = ((f32[8,96,2,256]{3,1,2,0:T(8,128)}), f32[8,96,2,256]{3,1,2,0:T(8,128)S(1)}, u32[]{:S(2)}, u32[]{:S(2)}) async-start(f32[8,96,2,256]{3,1,2,0:T(8,128)} %maximum_multiply_fusion), calls=%async_computation | async-start | bytes 3145728 | tf_op jit(solution)/shard_map/all_to_all | solution.py:46
  19.0 29.0 %collective-permute-start.4 = (f32[3,2,1,128]{3,2,1,0:T(1,128)S(1)}, f32[3,2,1,128]{3,2,1,0:T(1,128)S(1)}, u32[]{:S(2)}, u32[]{:S(2)}) collective-permute-start(f32[3,2,1,128]{3,2,1,0:T(1,128)S(1)} %slice.174), channel_id=1, source_target_pairs={{1,0},{2,1},{3,2},{4,3},{5,4},{6,5},{7,6},{0,7},{9,8},{10,9},{11,1... | collective-permute-start | bytes 9224 | tf_op jit(solution)/shard_map/ppermute | solution.py:26
  40.6 14.1 %all-to-all-start.1 = ((f32[96,2,256]{2,1,0:T(2,128)}), f32[96,2,256]{2,1,0:T(2,128)S(1)}, u32[]{:S(2)}, u32[]{:S(2)}) async-start(f32[96,2,256]{2,1,0:T(2,128)} %copy.149), calls=%async_computation.1 | async-start | bytes 393216 | tf_op jit(solution)/shard_map/all_to_all | solution.py:184
  48.0 11.8 %collective-permute-start.5 = (f32[3,1,193,128]{3,2,1,0:T(8,128)S(1)}, f32[3,1,193,128]{3,2,1,0:T(8,128)S(1)}, u32[]{:S(2)}, u32[]{:S(2)}) collective-permute-start(f32[3,1,193,128]{3,2,1,0:T(8,128)S(1)} %slice.216), channel_id=1, source_target_pairs={{8,0},{16,8},{24,16},{32,24},{40,32},{48,40},{56,48},{64,56},{72,6... | collective-permute-start | bytes 889352 | tf_op jit(solution)/shard_map/ppermute | solution.py:32
  56.3 11.0 %all-to-all-start.2 = ((f32[6,32,256]{2,0,1:T(8,128)}), f32[6,32,256]{2,0,1:T(8,128)S(1)}, u32[]{:S(2)}, u32[]{:S(2)}) async-start(f32[6,32,256]{2,0,1:T(8,128)} %copy.151), calls=%async_computation.2 | async-start | bytes 524288 | tf_op jit(solution)/shard_map/all_to_all | solution.py:189
  67.5 0.7 copy-start.4
  68.2 9.0 %copy-start.7 = (f32[12,12]{1,0:T(8,128)S(1)}, f32[12,12]{1,0:T(8,128)}, u32[]{:S(2)}) copy-start(f32[12,12]{1,0:T(8,128)} %param.16) | copy-start | bytes 1732
  69.5 29.0 %all-to-all-start.3 = ((f32[8,96,2,256]{3,1,2,0:T(8,128)}), f32[8,96,2,256]{3,1,2,0:T(8,128)}, u32[]{:S(2)}, u32[]{:S(2)}) async-start(f32[8,96,2,256]{3,1,2,0:T(8,128)} %broadcast_in_dim.7), calls=%async_computation.3 | async-start | bytes 3145728 | tf_op jit(solution)/shard_map/all_to_all | solution.py:52
  77.2 4.8 copy-start.1
  77.2 4.8 copy-start.5
  84.1 10.5 %collective-permute-start.6 = (f32[3,3,1,128]{3,2,1,0:T(1,128)S(1)}, f32[3,3,1,128]{3,2,1,0:T(1,128)S(1)}, u32[]{:S(2)}, u32[]{:S(2)}) collective-permute-start(f32[3,3,1,128]{3,2,1,0:T(1,128)S(1)} %pad_add_fusion.5), channel_id=1, source_target_pairs={{7,0},{0,1},{1,2},{2,3},{3,4},{4,5},{5,6},{6,7},{15,8},{8,9},{9,10... | collective-permute-start | bytes 13832 | tf_op jit(solution)/shard_map/ppermute | solution.py:26
  94.6 0.9 copy-start.2
  95.6 7.5 %copy-start.12 = (f32[2]{0:T(128)S(1)}, f32[2]{0:T(128)}, u32[]{:S(2)}) copy-start(f32[2]{0:T(128)} %broadcast_multiply_fusion.1) | copy-start | bytes 28
  95.6 10.5 %collective-permute-start.7 = (f32[3,1,192,128]{3,2,1,0:T(8,128)S(1)}, f32[3,1,192,128]{3,2,1,0:T(8,128)}, u32[]{:S(2)}, u32[]{:S(2)}) collective-permute-start(f32[3,1,192,128]{3,2,1,0:T(8,128)S(1)} %slice.225), channel_id=1, source_target_pairs={{0,8},{8,16},{16,24},{24,32},{32,40},{40,48},{48,56},{56,64},{64,7... | collective-permute-start | bytes 884744 | tf_op jit(solution)/shard_map/ppermute | solution.py:32
  100.1 6.0 %copy-start.3 = (f32[3,3,192,128]{3,2,1,0:T(8,128)S(1)}, f32[3,3,192,128]{3,2,1,0:T(8,128)}, u32[]{:S(2)}) copy-start(f32[3,3,192,128]{3,2,1,0:T(8,128)} %copy-done.2) | copy-start | bytes 2654212
  100.1 6.0 %copy-start.6 = (f32[3,2,192,128]{3,2,1,0:T(8,128)S(1)}, f32[3,2,192,128]{3,2,1,0:T(8,128)}, u32[]{:S(2)}) copy-start(f32[3,2,192,128]{3,2,1,0:T(8,128)} %param.10) | copy-start | bytes 1769476
  107.1 4.1 collective-permute-start.8
  111.2 9.4 %collective-permute-start.9 = (f32[3,1,193,128]{3,2,1,0:T(8,128)S(1)}, f32[3,1,193,128]{3,2,1,0:T(8,128)S(1)}, u32[]{:S(2)}, u32[]{:S(2)}) collective-permute-start(f32[3,1,193,128]{3,2,1,0:T(8,128)S(1)} %pad_maximum_fusion.7), channel_id=1, source_target_pairs={{8,0},{16,8},{24,16},{32,24},{40,32},{48,40},{56,48},{64,56},{72,6... | collective-permute-start | bytes 889352 | tf_op jit(solution)/shard_map/ppermute | solution.py:32
  128.1 2.5 collective-permute-start.10
  130.7 6.1 %collective-permute-start.11 = (f32[3,1,192,128]{3,2,1,0:T(8,128)S(1)}, f32[3,1,192,128]{3,2,1,0:T(8,128)S(1)}, u32[]{:S(2)}, u32[]{:S(2)}) collective-permute-start(f32[3,1,192,128]{3,2,1,0:T(8,128)S(1)} %slice.239), channel_id=1, source_target_pairs={{0,8},{8,16},{16,24},{24,32},{32,40},{40,48},{48,56},{56,64},{64,7... | collective-permute-start | bytes 884744 | tf_op jit(solution)/shard_map/ppermute | solution.py:32
  178.4 3.0 collective-permute-start
  181.5 10.0 %collective-permute-start.1 = (f32[3,1,193,128]{3,2,1,0:T(8,128)S(1)}, f32[3,1,193,128]{3,2,1,0:T(8,128)S(1)}, u32[]{:S(2)}, u32[]{:S(2)}) collective-permute-start(f32[3,1,193,128]{3,2,1,0:T(8,128)S(1)} %pad_maximum_fusion.11), channel_id=1, source_target_pairs={{8,0},{16,8},{24,16},{32,24},{40,32},{48,40},{56,48},{64,56},{72,6... | collective-permute-start | bytes 889352 | tf_op jit(solution)/shard_map/while/body/eval_jaxpr/ppermute | solution.py:32
  197.7 1.7 copy-start
  199.5 2.2 collective-permute-start.2
  202.5 8.0 %collective-permute-start.3 = (f32[3,1,192,128]{3,2,1,0:T(8,128)}, f32[3,1,192,128]{3,2,1,0:T(8,128)S(1)}, u32[]{:S(2)}, u32[]{:S(2)}) collective-permute-start(f32[3,1,192,128]{3,2,1,0:T(8,128)} %slice.322), channel_id=1, source_target_pairs={{0,8},{8,16},{16,24},{24,32},{32,40},{40,48},{48,56},{56,64},{64,7... | collective-permute-start | bytes 884744 | tf_op jit(solution)/shard_map/while/body/eval_jaxpr/ppermute | solution.py:32
  258.2 3.0 collective-permute-start
  261.2 10.5 %collective-permute-start.1 = (f32[3,1,193,128]{3,2,1,0:T(8,128)S(1)}, f32[3,1,193,128]{3,2,1,0:T(8,128)S(1)}, u32[]{:S(2)}, u32[]{:S(2)}) collective-permute-start(f32[3,1,193,128]{3,2,1,0:T(8,128)S(1)} %pad_maximum_fusion.11), channel_id=1, source_target_pairs={{8,0},{16,8},{24,16},{32,24},{40,32},{48,40},{56,48},{64,56},{72,6... | collective-permute-start | bytes 889352 | tf_op jit(solution)/shard_map/while/body/eval_jaxpr/ppermute | solution.py:32
  278.0 1.7 copy-start
  279.8 2.2 collective-permute-start.2
  282.8 7.5 %collective-permute-start.3 = (f32[3,1,192,128]{3,2,1,0:T(8,128)}, f32[3,1,192,128]{3,2,1,0:T(8,128)S(1)}, u32[]{:S(2)}, u32[]{:S(2)}) collective-permute-start(f32[3,1,192,128]{3,2,1,0:T(8,128)} %slice.322), channel_id=1, source_target_pairs={{0,8},{8,16},{16,24},{24,32},{32,40},{40,48},{48,56},{56,64},{64,7... | collective-permute-start | bytes 884744 | tf_op jit(solution)/shard_map/while/body/eval_jaxpr/ppermute | solution.py:32
  337.8 3.0 collective-permute-start
  340.8 11.1 %collective-permute-start.1 = (f32[3,1,193,128]{3,2,1,0:T(8,128)S(1)}, f32[3,1,193,128]{3,2,1,0:T(8,128)S(1)}, u32[]{:S(2)}, u32[]{:S(2)}) collective-permute-start(f32[3,1,193,128]{3,2,1,0:T(8,128)S(1)} %pad_maximum_fusion.11), channel_id=1, source_target_pairs={{8,0},{16,8},{24,16},{32,24},{40,32},{48,40},{56,48},{64,56},{72,6... | collective-permute-start | bytes 889352 | tf_op jit(solution)/shard_map/while/body/eval_jaxpr/ppermute | solution.py:32
  358.1 1.7 copy-start
  360.0 1.4 collective-permute-start.2
  362.2 7.3 %collective-permute-start.3 = (f32[3,1,192,128]{3,2,1,0:T(8,128)}, f32[3,1,192,128]{3,2,1,0:T(8,128)S(1)}, u32[]{:S(2)}, u32[]{:S(2)}) collective-permute-start(f32[3,1,192,128]{3,2,1,0:T(8,128)} %slice.322), channel_id=1, source_target_pairs={{0,8},{8,16},{16,24},{24,32},{32,40},{40,48},{48,56},{56,64},{64,7... | collective-permute-start | bytes 884744 | tf_op jit(solution)/shard_map/while/body/eval_jaxpr/ppermute | solution.py:32
  417.6 3.1 collective-permute-start
  420.7 10.6 %collective-permute-start.1 = (f32[3,1,193,128]{3,2,1,0:T(8,128)S(1)}, f32[3,1,193,128]{3,2,1,0:T(8,128)S(1)}, u32[]{:S(2)}, u32[]{:S(2)}) collective-permute-start(f32[3,1,193,128]{3,2,1,0:T(8,128)S(1)} %pad_maximum_fusion.11), channel_id=1, source_target_pairs={{8,0},{16,8},{24,16},{32,24},{40,32},{48,40},{56,48},{64,56},{72,6... | collective-permute-start | bytes 889352 | tf_op jit(solution)/shard_map/while/body/eval_jaxpr/ppermute | solution.py:32
  437.5 1.7 copy-start
  439.3 1.7 collective-permute-start.2
  441.8 7.3 %collective-permute-start.3 = (f32[3,1,192,128]{3,2,1,0:T(8,128)}, f32[3,1,192,128]{3,2,1,0:T(8,128)S(1)}, u32[]{:S(2)}, u32[]{:S(2)}) collective-permute-start(f32[3,1,192,128]{3,2,1,0:T(8,128)} %slice.322), channel_id=1, source_target_pairs={{0,8},{8,16},{16,24},{24,32},{32,40},{40,48},{48,56},{56,64},{64,7... | collective-permute-start | bytes 884744 | tf_op jit(solution)/shard_map/while/body/eval_jaxpr/ppermute | solution.py:32
  497.6 3.0 collective-permute-start
  500.7 11.2 %collective-permute-start.1 = (f32[3,1,193,128]{3,2,1,0:T(8,128)S(1)}, f32[3,1,193,128]{3,2,1,0:T(8,128)S(1)}, u32[]{:S(2)}, u32[]{:S(2)}) collective-permute-start(f32[3,1,193,128]{3,2,1,0:T(8,128)S(1)} %pad_maximum_fusion.11), channel_id=1, source_target_pairs={{8,0},{16,8},{24,16},{32,24},{40,32},{48,40},{56,48},{64,56},{72,6... | collective-permute-start | bytes 889352 | tf_op jit(solution)/shard_map/while/body/eval_jaxpr/ppermute | solution.py:32
  518.0 1.7 copy-start
  519.9 1.4 collective-permute-start.2
  522.0 7.3 %collective-permute-start.3 = (f32[3,1,192,128]{3,2,1,0:T(8,128)}, f32[3,1,192,128]{3,2,1,0:T(8,128)S(1)}, u32[]{:S(2)}, u32[]{:S(2)}) collective-permute-start(f32[3,1,192,128]{3,2,1,0:T(8,128)} %slice.322), channel_id=1, source_target_pairs={{0,8},{8,16},{16,24},{24,32},{32,40},{40,48},{48,56},{56,64},{64,7... | collective-permute-start | bytes 884744 | tf_op jit(solution)/shard_map/while/body/eval_jaxpr/ppermute | solution.py:32
where the time goes:
time: 595 us; the launch traced here: 585 us
  blocking collectives  223 us (37%)
  waiting for transfers between devices  132 us (22%)
  starting transfers between devices  64.4 us (11%)
  other arithmetic  64.1 us (11%)
  matrix products  53.5 us (9%)
  local copies, waits for them, and re-layouts  28.4 us (5%)
  loops' own time  17.2 us (3%)
    psum x24, blocking collectives, by_axis(): return functools.reduce(lax.psum, axes, shard)  223 us
    ppermute x14, waiting for transfers between devices, from_behind_2(): return lax.ppermute(block, axis, route)  68.7 us
    dot_general x7, matrix products, element_forces(): jnp.einsum('ab,brhs->arhs', stiffness, values, precision=precise)  38.8 us
    add x5, other arithmetic, iterate(): elastic = elastic + step_size * direction_forces  35.8 us
    ppermute x14, waiting for transfers between devices, from_behind(): return lax.ppermute(block, axis, route)  31 us
    ppermute x14, starting transfers between devices, from_behind_2(): return lax.ppermute(block, axis, route)  30.3 us
    all_to_all x1, waiting for transfers between devices, sum_at_owner(): tiles = lax.all_to_all(split_up(shard, dim, length), axis, 0, 0, tiled=True)  19.5 us
    another operation x1, loops' own time, body(): final_state = lax.fori_loop(0, ITERS - 1, iterate, start_state)  17.2 us
  transfers between devices with their start and end apart: 32, of which 27 were waited for; matrix products, arithmetic and copies ran while one was open for 5% of the time, Pallas kernels for 0%

commit v1 on v0

v1 whole, which is shorter than its diff:
```python
import functools
import math

import jax
import jax.numpy as jnp
import ml_dtypes
import numpy as np
from jax import lax
from jax.experimental import pallas as pl
from jax.experimental.pallas import tpu as pltpu
from jax.sharding import Mesh
from jax.sharding import PartitionSpec as P

HRING = 1536
LDEG = 768
NR = 32
TILE = ("tile_0", "tile_1")
CAP = ("cap_0", "cap_1")
ALL = ("cap_0", "cap_1", "tile_0", "tile_1")
LANES = 128
COLS = 192
ROOT3H = math.sqrt(3.0) / 2.0
rotation_gain = 2.0
gravity_gain = 0.2

EFF_TILE = 21
TAIL_TILE = 24
IN_TILES = 26
OUT_TAIL = 12
OUT_TILES = 14

f32 = jnp.float32
bf16 = jnp.bfloat16


def split_table(table):
    high = table.astype(ml_dtypes.bfloat16)
    low = (table - high.astype(np.float64)).astype(ml_dtypes.bfloat16)
    return high, low


def transform_tables():
    q = np.arange(128)[None, :]
    b = np.arange(256)[:, None]
    angle = 2.0 * np.pi * ((q * b) % 256) / 256.0
    cosine, sine = np.cos(angle), np.sin(angle)
    table = np.concatenate(
        [np.concatenate([cosine, sine], 1), np.concatenate([sine, -cosine], 1)], 0
    )
    p = np.arange(8)[:, None]
    turn = 2.0 * np.pi * ((p * np.arange(256)[None, :]) % HRING) / HRING
    twiddle = np.stack([np.cos(turn), np.sin(turn)]).astype(np.float32)
    return split_table(table), split_table(np.ascontiguousarray(table.T)), twiddle


def radial_tables():
    radius = 1.0 - 0.45 * (np.arange(NR) + 0.5) / NR
    degree = 6.0 * np.arange(128)[None, :] + np.arange(8)[:, None]
    log_radius = np.log(radius)
    ratio = np.zeros((NR, 8, 128))
    for r in range(1, NR):
        ratio[r] = np.exp(-degree * (log_radius[r - 1] - log_radius[r]))
    scale = 1.0 / np.sqrt(2.0 * degree + 1.0)
    return ratio.astype(np.float32), scale.astype(np.float32), radius


def split(x):
    high = x.astype(bf16)
    return high, (x - high.astype(f32)).astype(bf16)


def mm(a, b):
    return jnp.dot(a, b, preferred_element_type=f32)


def lane_index(shape):
    return lax.broadcasted_iota(jnp.int32, shape, len(shape) - 1)


def row_index(shape):
    return lax.broadcasted_iota(jnp.int32, shape, 0)


def tile_of(k):
    return slice(k * LANES, (k + 1) * LANES)


def down_one(x):
    return jnp.where(row_index(x.shape) == 0, 0.0, pltpu.roll(x, 1, 0))


def up_one(x):
    n = x.shape[0]
    return jnp.where(row_index(x.shape) == n - 1, 0.0, pltpu.roll(x, n - 1, 0))


def pack_kernel(parity_ref, density_ref, load_ref, prev_ref, stress_ref, shear_ref, relax_ref,
                out_ref, acc_ref, tail_ref):
    comp = pl.program_id(0)
    parity = parity_ref[0]
    wide = pl.ds(pl.multiple_of(64 * parity, 64), 128)
    narrow = pl.ds(pl.multiple_of(128 * (1 - parity), 64), 64)

    def put(tile, block):
        start = pl.multiple_of(tile * LANES, LANES)
        out_ref[:, pl.ds(start, LANES)] = jnp.transpose(block)

    @pl.when(comp == 0)
    def _():
        acc_ref[:2] = shear_ref[...] / (1.0 + 0.5 * relax_ref[...])
        put(EFF_TILE, acc_ref[0, wide, :])
        put(EFF_TILE + 1, acc_ref[1, wide, :])
        put(EFF_TILE + 2, jnp.concatenate([acc_ref[0, narrow, :], acc_ref[1, narrow, :]], 0))
        tail_ref[192:256, :] = jnp.zeros((64, LANES), f32)
        for r in range(2):
            tail_ref[201 + r : 202 + r, :] = jnp.full((1, LANES), density_ref[r], f32)

    base = comp * 7
    put(base, prev_ref[0, 0, wide, :])
    put(base + 1, prev_ref[0, 1, wide, :])
    put(base + 2, jnp.concatenate([prev_ref[0, 0, narrow, :], prev_ref[0, 1, narrow, :]], 0))

    relax = relax_ref[...]
    carried = relax / (1.0 + 0.5 * relax)
    part = [[carried[r] * stress_ref[q, r] for r in range(2)] for q in range(4)]
    near = [part[0][0], part[0][1] + part[2][0], part[2][1]]
    far = [part[1][0], part[1][1] + part[3][0], part[3][1]]
    for r in range(3):
        total = near[r] + down_one(far[r])
        if r < 2:
            total = total + load_ref[0, r]
        acc_ref[r] = total
        tail_ref[pl.ds(192 + 3 * comp + r, 1), :] = far[r][COLS - 1 : COLS, :]
    for r in range(3):
        put(base + 3 + r, acc_ref[r, wide, :])
    put(base + 6, jnp.concatenate([acc_ref[0, narrow, :], acc_ref[1, narrow, :]], 0))
    tail_ref[pl.ds(pl.multiple_of(64 * comp, 64), 64), :] = acc_ref[2, narrow, :]

    @pl.when(comp == 2)
    def _():
        put(TAIL_TILE, tail_ref[:128, :])
        put(TAIL_TILE + 1, tail_ref[128:, :])


def section_kernel(stiff_ref, recv_ref, slots_ref, fh_ref, fl_ref, th_ref, tl_ref, twiddle_ref,
                   ratio_ref, scale_ref, basis_ref, send_ref,
                   eff_ref, matrix_ref, xh_ref, xl_ref, image_ref, coef_ref, pot_ref, stage_ref,
                   *, radius):
    lane = lane_index((16, LANES))
    for k in range(IN_TILES):
        stage_ref[tile_of(k), :] = recv_ref[:, tile_of(k)]

    def rows_of(t, tile):
        return stage_ref[pl.ds(LANES * tile + t, 16, stride=8), :]

    def unrolled(wide_tile, narrow_tile, half):
        for u in range(4):
            even, odd = rows_of(2 * u, narrow_tile), rows_of(2 * u + 1, narrow_tile)
            if half == 0:
                middle = jnp.where(lane < 64, even, pltpu.roll(odd, 64, 1))
            else:
                middle = jnp.where(lane < 64, pltpu.roll(even, 64, 1), odd)
            yield 3 * u, rows_of(2 * u, wide_tile)
            yield 3 * u + 1, middle
            yield 3 * u + 2, rows_of(2 * u + 1, wide_tile)

    tail = TAIL_TILE
    for c in range(3):
        for r in range(2):
            rows = slice(32 * c + 16 * r, 32 * c + 16 * r + 16)
            for k, block in unrolled(7 * c + r, 7 * c + 2, r):
                basis_ref[1, rows, tile_of(k)] = block
            for k, block in unrolled(7 * c + 3 + r, 7 * c + 6, r):
                basis_ref[0, rows, tile_of(k)] = block
        rows = slice(32 * c, 32 * c + 16)
        for k, block in unrolled(7 * c + 5, tail + c // 2, c % 2):
            basis_ref[0, rows, tile_of(k)] += down_one(block)
    for t in range(8):
        following = (t + 1) % 8
        k, target = 3 * (following // 2) + following % 2, 64 * (following % 2)
        block = rows_of(t, tail + 1)
        for c in range(3):
            for r in range(3):
                shift = (target - 64 - 3 * c - r) % LANES
                value = jnp.where(lane == target, pltpu.roll(block, shift, 1), 0.0)
                if r == 2:
                    value = down_one(value)
                start = 32 * c + 16 * (r % 2)
                basis_ref[0, start : start + 16, tile_of(k)] += value
    for r in range(2):
        for k, block in unrolled(EFF_TILE + r, EFF_TILE + 2, r):
            eff_ref[0, 16 * r : 16 * r + 16, tile_of(k)] = block
    eff_ref[1, 16:32, :] = eff_ref[0, 0:16, :]
    eff_ref[1, 0:16, :] = down_one(eff_ref[0, 16:32, :])
    eff_ref[2] = pltpu.roll(eff_ref[0], 1, 1)
    eff_ref[3] = pltpu.roll(eff_ref[1], 1, 1)

    density = jnp.concatenate(
        [jnp.sum(jnp.where(lane == 73 + r, rows_of(0, tail + 1), 0.0), 1, keepdims=True)
         for r in range(2)], 0
    )

    weight = density * math.sqrt(2.0 / HRING)
    w = [basis_ref[1, 0:32, 256 * a : 256 * a + 256] * weight for a in range(6)]
    s1, s2, d1, d2 = w[1] + w[5], w[2] + w[4], w[1] - w[5], w[2] - w[4]
    plus, minus = w[0] + w[3], w[0] - w[3]
    half = 0.5 * (s1 + s2)
    diff = 0.5 * (s1 - s2)
    real = [plus + 2.0 * half, minus + diff, plus - half, minus - 2.0 * diff]
    real += [real[2], real[1]]
    i1, i2 = -ROOT3H * (d1 + d2), -ROOT3H * (d1 - d2)
    imag = [None, i1, i2, None, -i2, -i1]
    for p in range(6):
        cosine, sine = twiddle_ref[0, p : p + 1, :], twiddle_ref[1, p : p + 1, :]
        rows = slice(32 * p, 32 * p + 32)
        re, im = real[p] * cosine, -real[p] * sine
        if imag[p] is not None:
            re, im = re + imag[p] * sine, im + imag[p] * cosine
        for k, x in ((0, re), (256, im)):
            high, low = split(x)
            xh_ref[rows, k : k + 256] = high
            xl_ref[rows, k : k + 256] = low
    high, low = xh_ref[0:192, 0:512], xl_ref[0:192, 0:512]
    coefs = mm(high, fh_ref[...]) + mm(low, fh_ref[...]) + mm(high, fl_ref[...])
    for k in range(2):
        coef_ref[256 * k : 256 * k + 192, :] = coefs[:, tile_of(k)]
        coef_ref[256 * k + 192 : 256 * k + 256, :] = jnp.zeros((64, LANES), f32)

    def place(r, k):
        return pl.ds(256 * k + 16 * (r % 2) + r // 2, 8, stride=32)

    zero = jnp.zeros((8, LANES), f32)
    for k in range(2):
        lanes = tile_of(k)
        rows = [coef_ref[place(r, k), :] for r in range(NR)]
        forward, moment = zero, zero
        for r in range(NR):
            forward = rows[r] + ratio_ref[r] * forward
            moment = moment + (radius[r] ** 4 / NR) * rows[r]
            pot_ref[r, :, lanes] = forward
        chosen = (lane_index((8, LANES)) == 0) & (row_index((8, LANES)) == 2)
        moment = jnp.where(chosen, rotation_gain * moment, 0.0)
        back = zero
        for r in reversed(range(NR)):
            if r + 1 < NR:
                back = ratio_ref[r + 1] * (rows[r + 1] + back)
            pot_ref[r, :, lanes] = (
                (pot_ref[r, :, lanes] + back) * scale_ref[...] + radius[r] ** 2 * moment
            )
    for k in range(2):
        for r in range(NR):
            coef_ref[place(r, k), :] = pot_ref[r, :, tile_of(k)]

    for k in range(2):
        for p in range(6):
            x = coef_ref[256 * k + 32 * p : 256 * k + 32 * p + 32, :]
            high, low = split(x)
            rest = (x - high.astype(f32) - low.astype(f32)).astype(bf16)
            for n, piece in enumerate((high, low, rest)):
                xl_ref[64 * n + 32 * k : 64 * n + 32 * k + 32, tile_of(p)] = piece
    degrees = slots_ref[...]
    for t in range(8):
        d = degrees[t : t + 1, :]
        where_from = (d % 6) * LANES + d // 6
        pick = jnp.where(row_index((LDEG, LANES)) == where_from, 1.0, 0.0).astype(bf16)
        chosen = mm(xl_ref[0:192, 0:LDEG], pick)
        chosen = chosen[0:64] + chosen[64:128] + chosen[128:192]
        for k in range(4):
            stage_ref[pl.ds(LANES * k + t, 16, stride=8), :] = chosen[16 * k : 16 * k + 16]
    for k in range(4):
        send_ref[:, tile_of(k)] = stage_ref[tile_of(k), :]

    high, low = split(jnp.concatenate([coef_ref[0:192, :], coef_ref[256:448, :]], 1))
    field = mm(high, th_ref[...]) + mm(low, th_ref[...]) + mm(high, tl_ref[...])
    re, im = [], []
    for p in range(6):
        cosine, sine = twiddle_ref[0, p : p + 1, :], twiddle_ref[1, p : p + 1, :]
        x, y = field[32 * p : 32 * p + 32, 0:256], field[32 * p : 32 * p + 32, 256:512]
        re.append(x * cosine - y * sine)
        im.append(x * sine + y * cosine)
    a1, a2, e1, e2 = re[1] + re[5], re[2] + re[4], im[1] - im[5], im[2] - im[4]
    plus, minus = re[0] + re[3], re[0] - re[3]
    half, diff = 0.5 * (a1 + a2), 0.5 * (a1 - a2)
    o1, o2 = ROOT3H * (e1 + e2), ROOT3H * (e1 - e2)
    parts = [plus + 2.0 * half, minus + diff - o1, plus - half - o2, minus - 2.0 * diff,
             plus - half + o2, minus + diff + o1]
    for a in range(6):
        basis_ref[0, 0:32, 256 * a : 256 * a + 256] += gravity_gain * density * parts[a]

    idx = row_index((32, LANES))
    lane32 = lane_index((32, LANES))
    after = jnp.where(idx < 16, idx + 16, jnp.where(idx == 31, -1000, idx - 15))
    before = jnp.where(idx >= 16, idx - 16, jnp.where(idx == 0, -1000, idx + 15))
    masks = {}
    for c in range(3):
        for name, index in ((0, idx), (1, after), (-1, before)):
            masks[c, name] = jnp.where(lane32 == index + 32 * c, 1.0, 0.0)
    for g in range(2):
        for n in range(2):
            for c in range(3):
                row = 4 * c + 2 * n + g
                start = 96 * n + 32 * c
                for dh in range(2):
                    block = jnp.zeros((32, LANES), f32)
                    for c2 in range(3):
                        for dr in range(2):
                            value = stiff_ref[12 * row + 4 * c2 + 2 * dr + dh]
                            block = block + value * masks[c2, dr - n]
                    high, low = split(block)
                    matrix_ref[g, start : start + 32, tile_of(dh)] = high
                    matrix_ref[g, 192 + start : 224 + start, tile_of(dh)] = low

    for k in range(3):
        pad = jnp.zeros((32, HRING), bf16)
        xh_ref[128 * k + 96 : 128 * k + 128, :] = pad
        xl_ref[128 * k + 96 : 128 * k + 128, :] = pad

    lane_row = lane_index((1, LANES))

    def step(j, state):
        moments, beta = state
        v = basis_ref[j + 1]
        for k, x in ((0, pltpu.roll(v, 1, 1)), (128, v), (256, pltpu.roll(v, HRING - 1, 1))):
            high, low = split(x)
            xh_ref[k : k + 96, :] = high
            xl_ref[k : k + 96, :] = low
        product = jnp.zeros((96, 256), f32)
        for n in range(6):
            cols = slice(256 * n, 256 * n + 256)
            total = None
            for g in range(2):
                rows = slice(128 * (1 - g), 128 * (1 - g) + 256)
                first = mm(matrix_ref[g], xh_ref[rows, cols])
                second = mm(matrix_ref[g, 0:192, :], xl_ref[rows, cols])
                force = first[0:192] + first[192:384] + second
                for i in range(2):
                    share = eff_ref[2 * g + i, :, cols]
                    term = force[96 * i : 96 * i + 96].reshape(3, 32, 256) * share[None]
                    total = term if total is None else total + term
            total = total.reshape(96, 256)
            image_ref[:, cols] = total
            product = product + total * basis_ref[j + 1, :, cols]
        inner = jnp.sum(jnp.sum(product, 0, keepdims=True), 1, keepdims=True)
        alpha = jnp.where(j == 0, 0.0, inner)
        moments = moments + jnp.where(lane_row == j - 1, alpha, 0.0)
        rest = image_ref[...] - alpha * basis_ref[j + 1] - beta * basis_ref[j]
        norm2 = jnp.sum(jnp.sum(rest * rest, 0, keepdims=True), 1, keepdims=True)
        inverse = jnp.where(norm2 > 0.0, lax.rsqrt(norm2), 0.0)
        norm = norm2 * inverse

        @pl.when(j < 6)
        def _():
            basis_ref[j + 2] = rest * jnp.where(j == 0, -inverse, inverse)

        slot = jnp.where(j == 0, 16, jnp.where(j < 6, 7 + j, 100))
        moments = moments + jnp.where(lane_row == slot, norm, 0.0)
        return moments, jnp.where(j == 0, 0.0, norm)

    moments, _ = lax.fori_loop(
        0, 7, step, (jnp.zeros((1, LANES), f32), jnp.ones((1, 1), f32))
    )
    send_ref[:, tile_of(4)] = jnp.broadcast_to(moments, (LANES, LANES))


def solve_kernel(place_ref, moments_ref, basis_ref, out_ref, x_ref, stage_ref):
    table = jnp.transpose(moments_ref[...])
    diagonal, beside, start = table[0:8], table[8:16], table[16:17]
    first = row_index((8, LANES)) == 0
    residual = jnp.where(first, start, 0.0)

    def total(x):
        return jnp.sum(jnp.sum(x, 0, keepdims=True), 1, keepdims=True)

    direction, y = residual, jnp.zeros((8, LANES), f32)
    rr = total(residual * residual)
    for i in range(6):
        image = (
            diagonal * direction
            + beside * pltpu.roll(direction, 7, 0)
            + pltpu.roll(beside * direction, 1, 0)
        )
        size = rr / total(direction * image)
        y = y + size * direction
        if i < 5:
            residual = residual - size * image
            new = total(residual * residual)
            direction = residual + (new / rr) * direction
            rr = new
    mine = lane_index((8, LANES)) == place_ref[0]
    own = jnp.sum(jnp.where(mine, y, 0.0), 1, keepdims=True)
    x = basis_ref[1]
    for i in range(6):
        x = x + own[i : i + 1, :] * basis_ref[2 + i]
    x_ref[...] = x

    lane = lane_index((16, LANES))

    def node_rows(c, r, k):
        block = x_ref[32 * c + 16 * (r % 2) : 32 * c + 16 * (r % 2) + 16, tile_of(k)]
        return up_one(block) if r == 2 else block

    def at(t, tile):
        return pl.ds(LANES * tile + t, 16, stride=8)

    for u in range(4):
        even, odd = 2 * u, 2 * u + 1
        for c in range(3):
            for r in range(3):
                stage_ref[at(even, 4 * c + r), :] = node_rows(c, r, 3 * u)
                stage_ref[at(odd, 4 * c + r), :] = node_rows(c, r, 3 * u + 2)
            low, high = node_rows(c, 0, 3 * u + 1), node_rows(c, 1, 3 * u + 1)
            stage_ref[at(even, 4 * c + 3), :] = jnp.where(lane < 64, low, pltpu.roll(high, 64, 1))
            stage_ref[at(odd, 4 * c + 3), :] = jnp.where(lane < 64, pltpu.roll(low, 64, 1), high)
        extra = [node_rows(c, 2, 3 * u + 1) for c in range(3)]
        stage_ref[at(even, OUT_TAIL), :] = jnp.where(
            lane < 64, extra[0], pltpu.roll(extra[1], 64, 1)
        )
        stage_ref[at(odd, OUT_TAIL), :] = jnp.where(
            lane < 64, pltpu.roll(extra[0], 64, 1), extra[1]
        )
        for parity, rows in ((0, even), (1, odd)):
            block = extra[2] if parity == 0 else pltpu.roll(extra[2], 64, 1)
            following = (2 * u + parity + 1) % 8
            k, source = 3 * (following // 2) + following % 2, 64 * (following % 2)
            for c in range(3):
                for r in range(3):
                    target = 64 + 3 * c + r
                    value = pltpu.roll(node_rows(c, r, k), (target - source) % LANES, 1)
                    block = jnp.where(lane == target, value, block)
            stage_ref[at(rows, OUT_TAIL + 1), :] = block
    for k in range(OUT_TILES):
        out_ref[:, tile_of(k)] = stage_ref[tile_of(k), :]


def finish_kernel(parity_ref, stiff_ref, recv_ref, stress_ref, shear_ref, relax_ref,
                  x_out_ref, stress_out_ref, x_ref, eff_ref, kept_ref):
    comp = pl.program_id(0)
    parity = parity_ref[0]
    wide = pl.ds(pl.multiple_of(64 * parity, 64), 128)
    narrow = pl.ds(pl.multiple_of(128 * (1 - parity), 64), 64)

    @pl.when(comp == 0)
    def _():
        relax = relax_ref[...]
        share = 1.0 / (1.0 + 0.5 * relax)
        eff_ref[...] = shear_ref[...] * share
        kept_ref[...] = (1.0 - 0.5 * relax) * share
        def block(k):
            return jnp.transpose(recv_ref[:, tile_of(k)])
        for c in range(3):
            for r in range(3):
                x_ref[c, r, wide, :] = block(4 * c + r)
            rest = block(4 * c + 3)
            x_ref[c, 0, narrow, :] = rest[0:64]
            x_ref[c, 1, narrow, :] = rest[64:128]
        rest = block(OUT_TAIL)
        x_ref[0, 2, narrow, :] = rest[0:64]
        x_ref[1, 2, narrow, :] = rest[64:128]
        rest = block(OUT_TAIL + 1)
        x_ref[2, 2, narrow, :] = rest[0:64]
        for c in range(3):
            for r in range(3):
                x_ref[c, r, COLS : COLS + 1, :] = rest[64 + 3 * c + r : 65 + 3 * c + r]
        for c in range(3):
            x_out_ref[c] = x_ref[c, 0:2, 0:COLS, :]

    chunk = 24
    for r in range(2):
        for n in range(COLS // chunk):
            start = n * chunk
            rows = slice(start, start + chunk)
            corners = []
            for c in range(3):
                for dr in range(2):
                    for dh in range(2):
                        corners.append(x_ref[c, r + dr, start + dh : start + dh + chunk, :])
            eff, kept = eff_ref[r, rows, :], kept_ref[r, rows, :]
            for q in range(4):
                row = (4 * comp + q) * 12
                force = stiff_ref[row] * corners[0]
                for k in range(1, 12):
                    force = force + stiff_ref[row + k] * corners[k]
                stress_out_ref[q, r, rows, :] = kept * stress_ref[q, r, rows, :] + eff * force


def potential_kernel(recv_ref, out_ref):
    for part in range(2):
        for r in range(2):
            block = jnp.transpose(recv_ref[:, tile_of(2 * part + r)])
            out_ref[:, r, tile_of(part)] = block[0:96]


def whole(shape):
    return pl.BlockSpec(shape, lambda *_: (0,) * len(shape))


smem = pl.BlockSpec(memory_space=pltpu.SMEM)


def params(mib):
    return pltpu.CompilerParams(vmem_limit_bytes=mib * 2**20)


def body(load, previous, stress_old, shear_modulus, relaxation, density_jump, element_stiffness,
         degree_slots):
    tile_place = lax.axis_index(TILE)
    place = (lax.axis_index(CAP) * 8 + tile_place).astype(jnp.int32).reshape(1)
    parity = (tile_place % 2).astype(jnp.int32).reshape(1)
    stiff = element_stiffness.reshape(144)
    slots = jnp.pad(degree_slots.reshape(8, 96), ((0, 0), (0, 32)), constant_values=-1)
    (fh, fl), (th, tl), twiddle = transform_tables()
    ratio, scale, radius = radial_tables()

    one = pl.BlockSpec((1, 2, COLS, LANES), lambda c: (c, 0, 0, 0))
    four = pl.BlockSpec((4, 2, COLS, LANES), lambda c: (c, 0, 0, 0))
    field = whole((2, COLS, LANES))
    packed = pl.pallas_call(
        pack_kernel,
        grid=(3,),
        in_specs=[smem, smem, one, one, four, field, field],
        out_specs=whole((LANES, IN_TILES * LANES)),
        out_shape=jax.ShapeDtypeStruct((LANES, IN_TILES * LANES), f32),
        scratch_shapes=[pltpu.VMEM((3, COLS, LANES), f32), pltpu.VMEM((256, LANES), f32)],
        compiler_params=params(24),
    )(parity, density_jump, load, previous, stress_old, shear_modulus, relaxation)
    received = lax.all_to_all(packed, ALL, 0, 0, tiled=True)

    basis, sent = pl.pallas_call(
        functools.partial(section_kernel, radius=[float(x) for x in radius]),
        in_specs=[smem] + [pl.BlockSpec(memory_space=pltpu.VMEM)] * 9,
        out_specs=[pl.BlockSpec(memory_space=pltpu.VMEM)] * 2,
        out_shape=[
            jax.ShapeDtypeStruct((8, 96, HRING), f32),
            jax.ShapeDtypeStruct((LANES, 5 * LANES), f32),
        ],
        scratch_shapes=[
            pltpu.VMEM((4, 32, HRING), f32),
            pltpu.VMEM((2, 384, 256), bf16),
            pltpu.VMEM((384, HRING), bf16),
            pltpu.VMEM((384, HRING), bf16),
            pltpu.VMEM((96, HRING), f32),
            pltpu.VMEM((512, LANES), f32),
            pltpu.VMEM((NR, 8, 256), f32),
            pltpu.VMEM((IN_TILES * LANES, LANES), f32),
        ],
        compiler_params=params(48),
    )(stiff, received, slots, fh, fl, th, tl, twiddle, ratio, scale)
    shared = lax.all_to_all(sent, ALL, 0, 0, tiled=True)

    back = pl.pallas_call(
        solve_kernel,
        grid=(1,),
        in_specs=[
            smem,
            pl.BlockSpec((LANES, LANES), lambda i: (0, 4)),
            whole((8, 96, HRING)),
        ],
        out_specs=whole((LANES, OUT_TILES * LANES)),
        out_shape=jax.ShapeDtypeStruct((LANES, OUT_TILES * LANES), f32),
        scratch_shapes=[
            pltpu.VMEM((96, HRING), f32),
            pltpu.VMEM((OUT_TILES * LANES, LANES), f32),
        ],
        compiler_params=params(32),
    )(place, shared, basis)
    returned = lax.all_to_all(back, ALL, 0, 0, tiled=True)

    potential = pl.pallas_call(
        potential_kernel,
        grid=(1,),
        in_specs=[pl.BlockSpec((LANES, 4 * LANES), lambda i: (0, 0))],
        out_specs=whole((96, 2, 256)),
        out_shape=jax.ShapeDtypeStruct((96, 2, 256), f32),
        compiler_params=params(16),
    )(shared)

    displacement, stress_new = pl.pallas_call(
        finish_kernel,
        grid=(3,),
        in_specs=[smem, smem, whole((LANES, OUT_TILES * LANES)), four, field, field],
        out_specs=[whole((3, 2, COLS, LANES)), four],
        out_shape=[
            jax.ShapeDtypeStruct((3, 2, COLS, LANES), f32),
            jax.ShapeDtypeStruct((12, 2, COLS, LANES), f32),
        ],
        scratch_shapes=[
            pltpu.VMEM((3, 3, COLS + 8, LANES), f32),
            pltpu.VMEM((2, COLS, LANES), f32),
            pltpu.VMEM((2, COLS, LANES), f32),
        ],
        compiler_params=params(24),
    )(parity, stiff, returned, stress_old, shear_modulus, relaxation)
    return displacement, stress_new, potential


def solution(mesh):
    torus = Mesh(mesh.devices.reshape(4, 4, 4, 2), ("cap_0", "cap_1", "tile_0", "tile_1"))
    return jax.shard_map(
        body,
        mesh=torus,
        in_specs=(
            P(None, CAP, TILE, None),
            P(None, CAP, TILE, None),
            P(None, CAP, TILE, None),
            P(CAP, TILE, None),
            P(CAP, TILE, None),
            P(CAP),
            P(),
            P(),
        ),
        out_specs=(P(None, CAP, TILE, None), P(None, CAP, TILE, None), P(TILE, CAP, None)),
        check_vma=False,
    )
```

time: 595 us -> 119 us (0.20); the launches traced: 585 us -> 118 us
  blocking collectives: 223 us -> 0 us
  waiting for transfers between devices: 132 us -> 54.2 us
  other arithmetic: 64.1 us -> 0 us
  matrix products: 53.5 us -> 0 us
  starting transfers between devices: 64.4 us -> 21.9 us
  Pallas kernels: 0 us -> 25.4 us
  loops' own time: 17.2 us -> 0 us
  local copies, waits for them, and re-layouts: 28.4 us -> 16.1 us
    psum x24 -> x0, blocking collectives: 223 us -> none  [by_axis(): return functools.reduce(lax.psum, axes, shard)]
    ppermute x28 -> x0, waiting for transfers between devices: 99.7 us -> none  [the longest x14 68.7 us: from_behind_2(): return lax.ppermute(block, axis, route)]
    dot_general x13 -> x0, matrix products: 53.5 us -> none  [the longest x7 38.8 us: element_forces(): jnp.einsum('ab,brhs->arhs', stiffness, values, precision=precise)]
    add x28 -> x0, other arithmetic: 47.7 us -> none  [the longest x5 35.8 us: iterate(): elastic = elastic + step_size * direction_forces]
    ppermute x28 -> x0, starting transfers between devices: 39.5 us -> none  [the longest x14 30.3 us: from_behind_2(): return lax.ppermute(block, axis, route)]
    pallas_call x0 -> x5, Pallas kernels: none -> 25.4 us  [the longest x1 16.7 us: body(): pl.pallas_call(functools.partial(section_kernel, radius=[float(x) for x i...]
    all_to_all x4 -> x3, waiting for transfers between devices: 32 us -> 54.2 us  [the longest x1 25.8 us: body(): received = lax.all_to_all(packed, ALL, 0, 0, tiled=True)]
    another operation x1 -> x0, loops' own time: 17.2 us -> none  [body(): final_state = lax.fori_loop(0, ITERS - 1, iterate, start_state)]
  transfers between devices with their start and end apart: 32 -> 3, of which waited for: 27 -> 3; matrix products, arithmetic and copies ran while one was open for 5% -> 0% of each run, Pallas kernels for 0% -> 1%
where the time goes in v1:
time: 119 us; the launch traced here: 118 us
  waiting for transfers between devices  54.2 us (46%)
  Pallas kernels  25.4 us (21%)
  starting transfers between devices  21.9 us (18%)
  local copies, waits for them, and re-layouts  16.1 us (14%)
    all_to_all x1, waiting for transfers between devices, body(): received = lax.all_to_all(packed, ALL, 0, 0, tiled=True)  25.8 us
    all_to_all x1, waiting for transfers between devices, body(): returned = lax.all_to_all(back, ALL, 0, 0, tiled=True)  16.7 us
    pallas_call x1, Pallas kernels, body(): pl.pallas_call(functools.partial(section_kernel, radius=[float(x) for x i...  16.7 us
    all_to_all x1, waiting for transfers between devices, body(): shared = lax.all_to_all(sent, ALL, 0, 0, tiled=True)  11.6 us
    all_to_all x1, starting transfers between devices, body(): received = lax.all_to_all(packed, ALL, 0, 0, tiled=True)  11.5 us
    unnamed x41, local copies, waits for them, and re-layouts  10.1 us
    all_to_all x1, starting transfers between devices, body(): returned = lax.all_to_all(back, ALL, 0, 0, tiled=True)  5.79 us
    all_to_all x1, starting transfers between devices, body(): shared = lax.all_to_all(sent, ALL, 0, 0, tiled=True)  4.66 us
  transfers between devices with their start and end apart: 3, of which 3 were waited for; matrix products, arithmetic and copies ran while one was open for 0% of the time, Pallas kernels for 1%

profile of v1, /device:TPU:1, one launch (start us, length us, event | category | flops | bytes accessed | tf_op | source)
XLA Modules:
  0.0 118.5 jit_solution(8139636880040315589)
XLA Ops:
  0.6 0.0 copy-start
  0.7 1.7 %copy-done = f32[12,2,192,128]{3,2,1,0:T(8,128)S(1)} copy-done((f32[12,2,192,128]{3,2,1,0:T(8,128)S(1)}, f32[12,2,192,128]{3,2,1,0:T(8,128)}, u32[]{:S(2)}) %copy-start) | copy-done | bytes 2359320
  2.3 0.0 copy-start.3
  2.3 0.9 copy-done.3
  3.2 0.0 copy-start.5
  3.2 0.9 copy-done.5
  4.2 0.0 copy-start.7
  4.2 1.1 copy-done.7
  5.2 0.0 copy-start.8
  5.2 1.1 copy-done.8
  6.3 0.0 copy-start.16
  6.3 0.7 copy-done.16
  7.0 1.7 %shard_map.166 = f32[128,3328]{1,0:T(8,128)S(1)} custom-call(s32[1]{0:T(128)} %bitcast.parity_ref, f32[2]{0:T(128)S(1)} %copy-done.16, f32[3,2,192,128]{3,2,1,0:T(8,128)S(1)} %copy-done.7, f32[3,2,192,128]{3,2,1,0:T(8,128)S(1)} %copy-done.8, f32[12,2,192,128]{3,2,1,0:T(8,128)S(1)} %copy-done, f32[2,192,128]{2,1,0:T(8,128)S(1)} %copy-done.3, ...), custom_call_target="tpu_custom_call" | custom-call | tf_op jit(solution)/shard_map/pallas_call | solution.py:517
  8.6 2.9 %copy.18 = f32[128,1,3328]{2,1,0:T(1,128)} copy(f32[128,1,3328]{2,0,1:T(8,128)S(1)} %bitcast.15) | data formatting | bytes 3407872 | tf_op jit(solution)/shard_map/all_to_all | solution.py:526
  11.6 0.0 copy-start.17
  11.6 0.0 copy-start.18
  11.6 11.5 %all-to-all-start = ((f32[128,1,3328]{2,1,0:T(1,128)}), f32[128,1,3328]{2,1,0:T(1,128)S(1)}, u32[]{:S(2)}, u32[]{:S(2)}) async-start(f32[128,1,3328]{2,1,0:T(1,128)} %copy.18), calls=%async_computation | async-start | bytes 3407872 | tf_op jit(solution)/shard_map/all_to_all | solution.py:526
  23.1 0.0 copy-done.17
  23.1 0.1 reshape.25.stiff_ref
  23.2 0.0 copy-done.18
  23.2 0.1 reshape.27
  23.3 0.0 copy-start.9
  23.3 0.0 copy-start.10
  23.3 0.0 copy-start.11
  23.3 0.0 copy-start.12
  23.3 0.0 copy-start.13
  23.3 0.0 copy-start.14
  23.3 0.0 copy-start.15
  23.3 25.8 %all-to-all-done = f32[128,1,3328]{2,1,0:T(1,128)S(1)} async-done(((f32[128,1,3328]{2,1,0:T(1,128)}), f32[128,1,3328]{2,1,0:T(1,128)S(1)}, u32[]{:S(2)}, u32[]{:S(2)}) %all-to-all-start) | async-done | bytes 1703968 | tf_op jit(solution)/shard_map/all_to_all | solution.py:526
  49.2 0.1 copy.27
  49.3 0.0 copy-done.9
  49.3 0.0 copy-done.10
  49.3 0.0 copy-done.11
  49.3 0.0 copy-done.12
  49.3 0.0 copy-done.13
  49.3 0.0 copy-done.14
  49.3 0.0 copy-done.15
  49.3 16.7 %shard_map.167 = (f32[8,96,1536]{2,1,0:T(8,128)}, f32[128,640]{1,0:T(8,128)S(1)}) custom-call(f32[144]{0:T(256)S(1)} %reshape.25.stiff_ref, f32[128,3328]{1,0:T(8,128)S(1)} %bitcast.14, s32[8,128]{1,0:T(8,128)S(1)} %pad.4.slots_ref, bf16[512,256]{1,0:T(8,128)(2,1)S(1)} %copy-done.12, bf16[512,256]{1,0:T(8,128)(2,1)S(1)} %copy-done.11, ...), custom_call_target="tpu_custom_call" | custom-call | tf_op jit(solution)/shard_map/pallas_call | solution.py:528
  66.1 1.1 copy.19
  67.1 4.7 %all-to-all-start.1 = ((f32[128,1,640]{2,1,0:T(1,128)}), f32[128,1,640]{2,1,0:T(1,128)S(1)}, u32[]{:S(2)}, u32[]{:S(2)}) async-start(f32[128,1,640]{2,1,0:T(1,128)} %copy.19), calls=%async_computation.1 | async-start | bytes 655360 | tf_op jit(solution)/shard_map/all_to_all | solution.py:548
  71.8 11.6 %all-to-all-done.1 = f32[128,1,640]{2,1,0:T(1,128)S(1)} async-done(((f32[128,1,640]{2,1,0:T(1,128)}), f32[128,1,640]{2,1,0:T(1,128)S(1)}, u32[]{:S(2)}, u32[]{:S(2)}) %all-to-all-start.1) | async-done | bytes 327712 | tf_op jit(solution)/shard_map/all_to_all | solution.py:548
  83.5 0.0 copy-start.2
  83.5 2.3 %copy-done.2 = f32[8,96,1536]{2,1,0:T(8,128)S(1)} copy-done((f32[8,96,1536]{2,1,0:T(8,128)S(1)}, f32[8,96,1536]{2,1,0:T(8,128)}, u32[]{:S(2)}) %copy-start.2) | copy-done | bytes 4718616
  85.8 1.7 %shard_map.168 = f32[128,1792]{1,0:T(8,128)S(1)} custom-call(s32[1]{0:T(128)} %bitcast.1.place_ref, f32[128,640]{1,0:T(8,128)S(1)} %bitcast.18, f32[8,96,1536]{2,1,0:T(8,128)S(1)} %copy-done.2), custom_call_target="tpu_custom_call" | custom-call | tf_op jit(solution)/shard_map/pallas_call | solution.py:550
  87.5 1.9 %copy.20 = f32[128,1,1792]{2,1,0:T(1,128)} copy(f32[128,1,1792]{2,0,1:T(8,128)S(1)} %bitcast.16) | data formatting | bytes 1835008 | tf_op jit(solution)/shard_map/all_to_all | solution.py:566
  89.3 0.0 copy-start.1
  89.3 0.0 copy-start.4
  89.4 0.0 copy-start.6
  89.4 5.8 %all-to-all-start.2 = ((f32[128,1,1792]{2,1,0:T(1,128)}), f32[128,1,1792]{2,1,0:T(1,128)}, u32[]{:S(2)}, u32[]{:S(2)}) async-start(f32[128,1,1792]{2,1,0:T(1,128)} %copy.20), calls=%async_computation.2 | async-start | bytes 1835008 | tf_op jit(solution)/shard_map/all_to_all | solution.py:566
  95.1 0.9 shard_map.170
  96.0 16.7 %all-to-all-done.2 = f32[128,1,1792]{2,1,0:T(1,128)} async-done(((f32[128,1,1792]{2,1,0:T(1,128)}), f32[128,1,1792]{2,1,0:T(1,128)}, u32[]{:S(2)}, u32[]{:S(2)}) %all-to-all-start.2) | async-done | bytes 917536 | tf_op jit(solution)/shard_map/all_to_all | solution.py:566
  112.7 1.2 %copy.28 = f32[128,1,1792]{2,0,1:T(8,128)S(1)} copy(f32[128,1,1792]{2,1,0:T(1,128)} %all-to-all-done.2) | data formatting | bytes 1835008
  114.0 0.0 copy-done.1
  114.0 0.0 copy-done.4
  114.0 0.0 copy-done.6
  114.0 4.5 %shard_map.169 = (f32[3,2,192,128]{3,2,1,0:T(8,128)}, f32[12,2,192,128]{3,2,1,0:T(8,128)}) custom-call(s32[1]{0:T(128)} %bitcast.parity_ref, f32[144]{0:T(256)S(1)} %reshape.25.stiff_ref, f32[128,1792]{1,0:T(8,128)S(1)} %bitcast.17, f32[12,2,192,128]{3,2,1,0:T(8,128)S(1)} %copy-done.1, f32[2,192,128]{2,1,0:T(8,128)S(1)} %copy-done.4, ...), custom_call_target="tpu_custom_call" | custom-call | tf_op jit(solution)/shard_map/pallas_call | solution.py:577
  (2 shorter events, 0.0 us)
Async XLA Ops:
  0.6 1.7 %copy-start = (f32[12,2,192,128]{3,2,1,0:T(8,128)S(1)}, f32[12,2,192,128]{3,2,1,0:T(8,128)}, u32[]{:S(2)}) copy-start(f32[12,2,192,128]{3,2,1,0:T(8,128)} %stress_ref.3) | copy-start | bytes 7077892
  2.3 0.9 copy-start.3
  3.2 0.9 copy-start.5
  4.2 1.1 copy-start.7
  5.2 1.1 copy-start.8
  6.3 0.7 copy-start.16
  11.6 11.5 %copy-start.17 = (f32[12,12]{1,0:T(8,128)S(1)}, f32[12,12]{1,0:T(8,128)}, u32[]{:S(2)}) copy-start(f32[12,12]{1,0:T(8,128)} %param.21) | copy-start | bytes 1732
  11.6 11.6 %copy-start.18 = (s32[768]{0:T(1024)S(1)}, s32[768]{0:T(1024)}, u32[]{:S(2)}) copy-start(s32[768]{0:T(1024)} %param.22) | copy-start | bytes 9220
  11.6 37.6 %all-to-all-start = ((f32[128,1,3328]{2,1,0:T(1,128)}), f32[128,1,3328]{2,1,0:T(1,128)S(1)}, u32[]{:S(2)}, u32[]{:S(2)}) async-start(f32[128,1,3328]{2,1,0:T(1,128)} %copy.18), calls=%async_computation | async-start | bytes 3407872 | tf_op jit(solution)/shard_map/all_to_all | solution.py:526
  23.3 26.0 %copy-start.9 = (bf16[256,512]{1,0:T(8,128)(2,1)S(1)}, bf16[256,512]{1,0:T(8,128)(2,1)}, u32[]{:S(2)}) copy-start(bf16[256,512]{1,0:T(8,128)(2,1)} %constant.51.clone.tl_ref) | copy-start | bytes 786436
  23.3 26.0 %copy-start.10 = (bf16[256,512]{1,0:T(8,128)(2,1)S(1)}, bf16[256,512]{1,0:T(8,128)(2,1)}, u32[]{:S(2)}) copy-start(bf16[256,512]{1,0:T(8,128)(2,1)} %constant.50.clone.th_ref) | copy-start | bytes 786436
  23.3 26.0 %copy-start.11 = (bf16[512,256]{1,0:T(8,128)(2,1)S(1)}, bf16[512,256]{1,0:T(8,128)(2,1)}, u32[]{:S(2)}) copy-start(bf16[512,256]{1,0:T(8,128)(2,1)} %constant.49.clone.fl_ref) | copy-start | bytes 786436
  23.3 26.0 %copy-start.12 = (bf16[512,256]{1,0:T(8,128)(2,1)S(1)}, bf16[512,256]{1,0:T(8,128)(2,1)}, u32[]{:S(2)}) copy-start(bf16[512,256]{1,0:T(8,128)(2,1)} %constant.48.clone.fh_ref) | copy-start | bytes 786436
  23.3 26.0 %copy-start.13 = (f32[32,8,128]{2,1,0:T(8,128)S(1)}, f32[32,8,128]{2,1,0:T(8,128)}, u32[]{:S(2)}) copy-start(f32[32,8,128]{2,1,0:T(8,128)} %constant.53.clone.ratio_ref) | copy-start | bytes 393220
  23.3 26.0 %copy-start.14 = (f32[2,8,256]{2,1,0:T(8,128)S(1)}, f32[2,8,256]{2,1,0:T(8,128)}, u32[]{:S(2)}) copy-start(f32[2,8,256]{2,1,0:T(8,128)} %constant.52.clone.twiddle_ref) | copy-start | bytes 49156
  23.3 26.0 %copy-start.15 = (f32[8,128]{1,0:T(8,128)S(1)}, f32[8,128]{1,0:T(8,128)}, u32[]{:S(2)}) copy-start(f32[8,128]{1,0:T(8,128)} %constant.54.clone.scale_ref) | copy-start | bytes 12292
  67.1 16.3 %all-to-all-start.1 = ((f32[128,1,640]{2,1,0:T(1,128)}), f32[128,1,640]{2,1,0:T(1,128)S(1)}, u32[]{:S(2)}, u32[]{:S(2)}) async-start(f32[128,1,640]{2,1,0:T(1,128)} %copy.19), calls=%async_computation.1 | async-start | bytes 655360 | tf_op jit(solution)/shard_map/all_to_all | solution.py:548
  83.5 2.3 %copy-start.2 = (f32[8,96,1536]{2,1,0:T(8,128)S(1)}, f32[8,96,1536]{2,1,0:T(8,128)}, u32[]{:S(2)}) copy-start(f32[8,96,1536]{2,1,0:T(8,128)} %get-tuple-element.8.basis_ref) | copy-start | bytes 14155780
  89.3 24.6 %copy-start.1 = (f32[12,2,192,128]{3,2,1,0:T(8,128)S(1)}, f32[12,2,192,128]{3,2,1,0:T(8,128)}, u32[]{:S(2)}) copy-start(f32[12,2,192,128]{3,2,1,0:T(8,128)} %stress_ref.3) | copy-start | bytes 7077892
  89.3 24.6 %copy-start.4 = (f32[2,192,128]{2,1,0:T(8,128)S(1)}, f32[2,192,128]{2,1,0:T(8,128)}, u32[]{:S(2)}) copy-start(f32[2,192,128]{2,1,0:T(8,128)} %shear_ref.3) | copy-start | bytes 589828
  89.4 24.7 %copy-start.6 = (f32[2,192,128]{2,1,0:T(8,128)S(1)}, f32[2,192,128]{2,1,0:T(8,128)}, u32[]{:S(2)}) copy-start(f32[2,192,128]{2,1,0:T(8,128)} %relax_ref.3) | copy-start | bytes 589828
  89.4 23.4 %all-to-all-start.2 = ((f32[128,1,1792]{2,1,0:T(1,128)}), f32[128,1,1792]{2,1,0:T(1,128)}, u32[]{:S(2)}, u32[]{:S(2)}) async-start(f32[128,1,1792]{2,1,0:T(1,128)} %copy.20), calls=%async_computation.2 | async-start | bytes 1835008 | tf_op jit(solution)/shard_map/all_to_all | solution.py:566

commit v2 on v1

--- a/solution.py
+++ b/solution.py
@@ -26,6 +26,7 @@
 EFF_TILE = 21
 TAIL_TILE = 24
 IN_TILES = 26
+MID_TILES = 4
 OUT_TAIL = 12
 OUT_TILES = 14
 
@@ -102,8 +103,7 @@
     narrow = pl.ds(pl.multiple_of(128 * (1 - parity), 64), 64)
 
     def put(tile, block):
-        start = pl.multiple_of(tile * LANES, LANES)
-        out_ref[:, pl.ds(start, LANES)] = jnp.transpose(block)
+        out_ref[pl.ds(tile, LANES, stride=IN_TILES), :] = jnp.transpose(block)
 
     @pl.when(comp == 0)
     def _():
@@ -143,15 +143,16 @@
 
 
 def section_kernel(stiff_ref, recv_ref, slots_ref, fh_ref, fl_ref, th_ref, tl_ref, twiddle_ref,
-                   ratio_ref, scale_ref, basis_ref, send_ref,
-                   eff_ref, matrix_ref, xh_ref, xl_ref, image_ref, coef_ref, pot_ref, stage_ref,
+                   ratio_ref, scale_ref, kept_ref, send_ref, basis_ref, sems,
+                   eff_ref, matrix_ref, xh_ref, xl_ref, image_ref, coef_ref, pot_ref,
                    *, radius):
     lane = lane_index((16, LANES))
-    for k in range(IN_TILES):
-        stage_ref[tile_of(k), :] = recv_ref[:, tile_of(k)]
+
+    def leaving(slot):
+        return pltpu.make_async_copy(basis_ref.at[slot + 1], kept_ref.at[slot], sems.at[slot])
 
     def rows_of(t, tile):
-        return stage_ref[pl.ds(LANES * tile + t, 16, stride=8), :]
+        return recv_ref[pl.ds(IN_TILES * t + tile, 16, stride=8 * IN_TILES), :]
 
     def unrolled(wide_tile, narrow_tile, half):
         for u in range(4):
@@ -175,6 +176,7 @@
         rows = slice(32 * c, 32 * c + 16)
         for k, block in unrolled(7 * c + 5, tail + c // 2, c % 2):
             basis_ref[0, rows, tile_of(k)] += down_one(block)
+    leaving(0).start()
     for t in range(8):
         following = (t + 1) % 8
         k, target = 3 * (following // 2) + following % 2, 64 * (following % 2)
@@ -265,10 +267,14 @@
         pick = jnp.where(row_index((LDEG, LANES)) == where_from, 1.0, 0.0).astype(bf16)
         chosen = mm(xl_ref[0:192, 0:LDEG], pick)
         chosen = chosen[0:64] + chosen[64:128] + chosen[128:192]
-        for k in range(4):
-            stage_ref[pl.ds(LANES * k + t, 16, stride=8), :] = chosen[16 * k : 16 * k + 16]
-    for k in range(4):
-        send_ref[:, tile_of(k)] = stage_ref[tile_of(k), :]
+        c0, c1, c2, c3 = [chosen[16 * k : 16 * k + 16] for k in range(4)]
+        joined = [
+            jnp.where(lane < 96, c0, pltpu.roll(c1, 96, 1)),
+            jnp.where(lane < 64, pltpu.roll(c1, 96, 1), pltpu.roll(c2, 64, 1)),
+            jnp.where(lane < 32, pltpu.roll(c2, 64, 1), pltpu.roll(c3, 32, 1)),
+        ]
+        for k, block in enumerate(joined):
+            send_ref[pl.ds(MID_TILES * t + k, 16, stride=8 * MID_TILES), :] = block
 
     high, low = split(jnp.concatenate([coef_ref[0:192, :], coef_ref[256:448, :]], 1))
     field = mm(high, th_ref[...]) + mm(low, th_ref[...]) + mm(high, tl_ref[...])
@@ -351,6 +357,7 @@
         @pl.when(j < 6)
         def _():
             basis_ref[j + 2] = rest * jnp.where(j == 0, -inverse, inverse)
+            leaving(j + 1).start()
 
         slot = jnp.where(j == 0, 16, jnp.where(j < 6, 7 + j, 100))
         moments = moments + jnp.where(lane_row == slot, norm, 0.0)
@@ -359,11 +366,18 @@
     moments, _ = lax.fori_loop(
         0, 7, step, (jnp.zeros((1, LANES), f32), jnp.ones((1, 1), f32))
     )
-    send_ref[:, tile_of(4)] = jnp.broadcast_to(moments, (LANES, LANES))
-
-
-def solve_kernel(place_ref, moments_ref, basis_ref, out_ref, x_ref, stage_ref):
-    table = jnp.transpose(moments_ref[...])
+    send_ref[pl.ds(3, LANES, stride=MID_TILES), :] = jnp.broadcast_to(moments, (LANES, LANES))
+    for slot in range(7):
+        leaving(slot).wait()
+
+
+def solve_kernel(place_ref, moments_ref, kept_ref, out_ref, x_ref, basis_ref, sems):
+    def arriving(slot):
+        return pltpu.make_async_copy(kept_ref.at[slot], basis_ref.at[slot], sems.at[slot])
+
+    for slot in range(7):
+        arriving(slot).start()
+    table = jnp.transpose(moments_ref[pl.ds(3, LANES, stride=MID_TILES), :])
     diagonal, beside, start = table[0:8], table[8:16], table[16:17]
     first = row_index((8, LANES)) == 0
     residual = jnp.where(first, start, 0.0)
@@ -388,9 +402,11 @@
             rr = new
     mine = lane_index((8, LANES)) == place_ref[0]
     own = jnp.sum(jnp.where(mine, y, 0.0), 1, keepdims=True)
-    x = basis_ref[1]
+    for slot in range(7):
+        arriving(slot).wait()
+    x = basis_ref[0]
     for i in range(6):
-        x = x + own[i : i + 1, :] * basis_ref[2 + i]
+        x = x + own[i : i + 1, :] * basis_ref[1 + i]
     x_ref[...] = x
 
     lane = lane_index((16, LANES))
@@ -400,22 +416,22 @@
         return up_one(block) if r == 2 else block
 
     def at(t, tile):
-        return pl.ds(LANES * tile + t, 16, stride=8)
+        return pl.ds(OUT_TILES * t + tile, 16, stride=8 * OUT_TILES)
 
     for u in range(4):
         even, odd = 2 * u, 2 * u + 1
         for c in range(3):
             for r in range(3):
-                stage_ref[at(even, 4 * c + r), :] = node_rows(c, r, 3 * u)
-                stage_ref[at(odd, 4 * c + r), :] = node_rows(c, r, 3 * u + 2)
+                out_ref[at(even, 4 * c + r), :] = node_rows(c, r, 3 * u)
+                out_ref[at(odd, 4 * c + r), :] = node_rows(c, r, 3 * u + 2)
             low, high = node_rows(c, 0, 3 * u + 1), node_rows(c, 1, 3 * u + 1)
-            stage_ref[at(even, 4 * c + 3), :] = jnp.where(lane < 64, low, pltpu.roll(high, 64, 1))
-            stage_ref[at(odd, 4 * c + 3), :] = jnp.where(lane < 64, pltpu.roll(low, 64, 1), high)
+            out_ref[at(even, 4 * c + 3), :] = jnp.where(lane < 64, low, pltpu.roll(high, 64, 1))
+            out_ref[at(odd, 4 * c + 3), :] = jnp.where(lane < 64, pltpu.roll(low, 64, 1), high)
         extra = [node_rows(c, 2, 3 * u + 1) for c in range(3)]
-        stage_ref[at(even, OUT_TAIL), :] = jnp.where(
+        out_ref[at(even, OUT_TAIL), :] = jnp.where(
             lane < 64, extra[0], pltpu.roll(extra[1], 64, 1)
         )
-        stage_ref[at(odd, OUT_TAIL), :] = jnp.where(
+        out_ref[at(odd, OUT_TAIL), :] = jnp.where(
             lane < 64, pltpu.roll(extra[0], 64, 1), extra[1]
         )
         for parity, rows in ((0, even), (1, odd)):
@@ -427,13 +443,11 @@
                     target = 64 + 3 * c + r
                     value = pltpu.roll(node_rows(c, r, k), (target - source) % LANES, 1)
                     block = jnp.where(lane == target, value, block)
-            stage_ref[at(rows, OUT_TAIL + 1), :] = block
-    for k in range(OUT_TILES):
-        out_ref[:, tile_of(k)] = stage_ref[tile_of(k), :]
-
-
-def finish_kernel(parity_ref, stiff_ref, recv_ref, stress_ref, shear_ref, relax_ref,
-                  x_out_ref, stress_out_ref, x_ref, eff_ref, kept_ref):
+            out_ref[at(rows, OUT_TAIL + 1), :] = block
+
+
+def finish_kernel(parity_ref, stiff_ref, recv_ref, stress_ref, eff_ref, kept_ref,
+                  x_out_ref, stress_out_ref, x_ref):
     comp = pl.program_id(0)
     parity = parity_ref[0]
     wide = pl.ds(pl.multiple_of(64 * parity, 64), 128)
@@ -441,12 +455,8 @@
 
     @pl.when(comp == 0)
     def _():
-        relax = relax_ref[...]
-        share = 1.0 / (1.0 + 0.5 * relax)
-        eff_ref[...] = shear_ref[...] * share
-        kept_ref[...] = (1.0 - 0.5 * relax) * share
         def block(k):
-            return jnp.transpose(recv_ref[:, tile_of(k)])
+            return jnp.transpose(recv_ref[pl.ds(k, LANES, stride=OUT_TILES), :])
         for c in range(3):
             for r in range(3):
                 x_ref[c, r, wide, :] = block(4 * c + r)
@@ -483,11 +493,17 @@
                 stress_out_ref[q, r, rows, :] = kept * stress_ref[q, r, rows, :] + eff * force
 
 
-def potential_kernel(recv_ref, out_ref):
+def potential_kernel(recv_ref, shear_ref, relax_ref, out_ref, eff_ref, kept_ref):
+    relax = relax_ref[...]
+    share = 1.0 / (1.0 + 0.5 * relax)
+    eff_ref[...] = shear_ref[...] * share
+    kept_ref[...] = (1.0 - 0.5 * relax) * share
+    blocks = [jnp.transpose(recv_ref[pl.ds(k, LANES, stride=MID_TILES), :]) for k in range(3)]
+    lines = jnp.concatenate(blocks, 0)
     for part in range(2):
         for r in range(2):
-            block = jnp.transpose(recv_ref[:, tile_of(2 * part + r)])
-            out_ref[:, r, tile_of(part)] = block[0:96]
+            start = 96 * (2 * part + r)
+            out_ref[:, r, tile_of(part)] = lines[start : start + 96]
 
 
 def whole(shape):
@@ -495,6 +511,16 @@
 
 
 smem = pl.BlockSpec(memory_space=pltpu.SMEM)
+
+
+def far_memory(x):
+    return pltpu.with_memory_space_constraint(x, pltpu.HBM)
+
+
+def exchanged(lines):
+    count = lines.shape[0]
+    rows = lines.reshape(LANES, 1, count)
+    return lax.all_to_all(rows, ALL, 0, 0, tiled=True).reshape(count, LANES)
 
 
 def params(mib):
@@ -518,22 +544,24 @@
         pack_kernel,
         grid=(3,),
         in_specs=[smem, smem, one, one, four, field, field],
-        out_specs=whole((LANES, IN_TILES * LANES)),
-        out_shape=jax.ShapeDtypeStruct((LANES, IN_TILES * LANES), f32),
+        out_specs=whole((IN_TILES * LANES, LANES)),
+        out_shape=pltpu.HBM((IN_TILES * LANES, LANES), f32),
         scratch_shapes=[pltpu.VMEM((3, COLS, LANES), f32), pltpu.VMEM((256, LANES), f32)],
-        compiler_params=params(24),
-    )(parity, density_jump, load, previous, stress_old, shear_modulus, relaxation)
-    received = lax.all_to_all(packed, ALL, 0, 0, tiled=True)
+        compiler_params=params(12),
+    )(parity, *[far_memory(x) for x in (density_jump, load, previous, stress_old, shear_modulus, relaxation)])
+    received = exchanged(packed)
 
     basis, sent = pl.pallas_call(
         functools.partial(section_kernel, radius=[float(x) for x in radius]),
         in_specs=[smem] + [pl.BlockSpec(memory_space=pltpu.VMEM)] * 9,
-        out_specs=[pl.BlockSpec(memory_space=pltpu.VMEM)] * 2,
+        out_specs=[pl.BlockSpec(memory_space=pl.ANY), pl.BlockSpec(memory_space=pltpu.VMEM)],
         out_shape=[
-            jax.ShapeDtypeStruct((8, 96, HRING), f32),
-            jax.ShapeDtypeStruct((LANES, 5 * LANES), f32),
+            pltpu.HBM((7, 96, HRING), f32),
+            pltpu.HBM((MID_TILES * LANES, LANES), f32),
         ],
         scratch_shapes=[
+            pltpu.VMEM((8, 96, HRING), f32),
+            pltpu.SemaphoreType.DMA((7,)),
             pltpu.VMEM((4, 32, HRING), f32),
             pltpu.VMEM((2, 384, 256), bf16),
             pltpu.VMEM((384, HRING), bf16),
@@ -541,43 +569,44 @@
             pltpu.VMEM((96, HRING), f32),
             pltpu.VMEM((512, LANES), f32),
             pltpu.VMEM((NR, 8, 256), f32),
-            pltpu.VMEM((IN_TILES * LANES, LANES), f32),
         ],
-        compiler_params=params(48),
+        compiler_params=params(20),
     )(stiff, received, slots, fh, fl, th, tl, twiddle, ratio, scale)
-    shared = lax.all_to_all(sent, ALL, 0, 0, tiled=True)
+    shared = exchanged(sent)
 
     back = pl.pallas_call(
         solve_kernel,
         grid=(1,),
         in_specs=[
             smem,
-            pl.BlockSpec((LANES, LANES), lambda i: (0, 4)),
-            whole((8, 96, HRING)),
+            whole((MID_TILES * LANES, LANES)),
+            pl.BlockSpec(memory_space=pl.ANY),
         ],
-        out_specs=whole((LANES, OUT_TILES * LANES)),
-        out_shape=jax.ShapeDtypeStruct((LANES, OUT_TILES * LANES), f32),
+        out_specs=whole((OUT_TILES * LANES, LANES)),
+        out_shape=pltpu.HBM((OUT_TILES * LANES, LANES), f32),
         scratch_shapes=[
             pltpu.VMEM((96, HRING), f32),
-            pltpu.VMEM((OUT_TILES * LANES, LANES), f32),
+            pltpu.VMEM((7, 96, HRING), f32),
+            pltpu.SemaphoreType.DMA((7,)),
         ],
-        compiler_params=params(32),
-    )(place, shared, basis)
-    returned = lax.all_to_all(back, ALL, 0, 0, tiled=True)
-
-    potential = pl.pallas_call(
+        compiler_params=params(12),
+    )(place, shared, far_memory(basis))
+    returned = exchanged(back)
+
+    potential, effective, kept = pl.pallas_call(
         potential_kernel,
         grid=(1,),
-        in_specs=[pl.BlockSpec((LANES, 4 * LANES), lambda i: (0, 0))],
-        out_specs=whole((96, 2, 256)),
-        out_shape=jax.ShapeDtypeStruct((96, 2, 256), f32),
-        compiler_params=params(16),
-    )(shared)
+        in_specs=[whole((MID_TILES * LANES, LANES)), field, field],
+        out_specs=[whole((96, 2, 256)), field, field],
+        out_shape=[jax.ShapeDtypeStruct((96, 2, 256), f32)]
+        + [pltpu.HBM((2, COLS, LANES), f32)] * 2,
+        compiler_params=params(4),
+    )(shared, far_memory(shear_modulus), far_memory(relaxation))
 
     displacement, stress_new = pl.pallas_call(
         finish_kernel,
         grid=(3,),
-        in_specs=[smem, smem, whole((LANES, OUT_TILES * LANES)), four, field, field],
+        in_specs=[smem, smem, whole((OUT_TILES * LANES, LANES)), four, field, field],
         out_specs=[whole((3, 2, COLS, LANES)), four],
         out_shape=[
             jax.ShapeDtypeStruct((3, 2, COLS, LANES), f32),
@@ -585,11 +614,9 @@
         ],
         scratch_shapes=[
             pltpu.VMEM((3, 3, COLS + 8, LANES), f32),
-            pltpu.VMEM((2, COLS, LANES), f32),
-            pltpu.VMEM((2, COLS, LANES), f32),
         ],
-        compiler_params=params(24),
-    )(parity, stiff, returned, stress_old, shear_modulus, relaxation)
+        compiler_params=params(12),
+    )(parity, stiff, returned, stress_old, far_memory(effective), far_memory(kept))
     return displacement, stress_new, potential
 
 

time: 119 us -> 106 us (0.89)
  local copies, waits for them, and re-layouts: 16.1 us -> 0.22 us
  Pallas kernels: 25.4 us -> 31.1 us
  waiting for transfers between devices: 54.2 us -> 52.8 us
    unnamed x41 -> x20, local copies, waits for them, and re-layouts: 10.1 us -> 0.06 us
    all_to_all x3 -> x0, local copies, waits for them, and re-layouts: 5.87 us -> none  [the longest x1 2.94 us: body(): received = lax.all_to_all(packed, ALL, 0, 0, tiled=True)]
    pallas_call x3, Pallas kernels: 6.99 us -> 10.7 us  [the longest x1 4.9 us: body(): pl.pallas_call(finish_kernel, grid=(3,), in_specs=[smem, smem, whole((OUT...]
    pallas_call x1, Pallas kernels: 1.67 us -> 4.84 us  [body(): pl.pallas_call(pack_kernel, grid=(3,), in_specs=[smem, smem, one, one, fo...]
    all_to_all x3, waiting for transfers between devices: 54.2 us -> 52.8 us  [exchanged(): return lax.all_to_all(rows, ALL, 0, 0, tiled=True).reshape(count, LANES)]
  transfers between devices with their start and end apart: 3 -> 3, of which waited for: 3 -> 3; matrix products, arithmetic and copies ran while one was open for 0% -> 0% of each run, Pallas kernels for 1% -> 2%
where the time goes in v2:
time: 106 us
  waiting for transfers between devices  52.8 us (50%)
  Pallas kernels  31.1 us (29%)
  starting transfers between devices  20.9 us (20%)
    all_to_all x3, waiting for transfers between devices, exchanged(): return lax.all_to_all(rows, ALL, 0, 0, tiled=True).reshape(count, LANES)  52.8 us
    all_to_all x3, starting transfers between devices, exchanged(): return lax.all_to_all(rows, ALL, 0, 0, tiled=True).reshape(count, LANES)  20.9 us
    pallas_call x1, Pallas kernels, body(): pl.pallas_call(functools.partial(section_kernel, radius=[float(x) for x i...  15.6 us
    pallas_call x1, Pallas kernels, body(): pl.pallas_call(finish_kernel, grid=(3,), in_specs=[smem, smem, whole((OUT...  4.9 us
    pallas_call x1, Pallas kernels, body(): pl.pallas_call(pack_kernel, grid=(3,), in_specs=[smem, smem, one, one, fo...  4.84 us
    pallas_call x1, Pallas kernels, body(): pl.pallas_call(solve_kernel, grid=(1,), in_specs=[smem, whole((MID_TILES...  3.74 us
  transfers between devices with their start and end apart: 3, of which 3 were waited for; matrix products, arithmetic and copies ran while one was open for 0% of the time, Pallas kernels for 2%

profile of v2, /device:TPU:1, one launch (start us, length us, event | category | flops | bytes accessed | tf_op | source)
XLA Modules:
  0.0 105.8 jit_solution(16050623874459887831)
XLA Ops:
  0.6 4.8 %shard_map.166 = f32[3328,128]{1,0:T(8,128)} custom-call(s32[1]{0:T(128)} %bitcast.parity_ref, f32[2]{0:T(128)} %density_ref.1, f32[3,2,192,128]{3,2,1,0:T(8,128)} %load_ref.1, f32[3,2,192,128]{3,2,1,0:T(8,128)} %prev_ref.1, f32[12,2,192,128]{3,2,1,0:T(8,128)} %stress_ref.3, f32[2,192,128]{2,1,0:T(8,128)} %shear_ref.3, f32[2,192,128]{2,1,0:T(8,128)} %relax_ref.3), custom_call_target="tpu_custom_call" | custom-call | tf_op jit(solution)/shard_map/pallas_call | solution.py:543
  5.5 0.0 copy-start.8
  5.5 0.0 copy-start.9
  5.5 0.0 copy-start.1
  5.5 0.0 copy-start.2
  5.5 0.0 copy-start.3
  5.5 0.0 copy-start.4
  5.5 0.0 copy-start.5
  5.5 0.0 copy-start.6
  5.6 0.0 copy-start.7
  5.6 11.5 %all-to-all-start = ((f32[128,1,3328]{2,1,0:T(1,128)}), f32[128,1,3328]{2,1,0:T(1,128)S(1)}, u32[]{:S(2)}, u32[]{:S(2)}) async-start(f32[128,1,3328]{2,1,0:T(1,128)} %bitcast.12), calls=%async_computation | async-start | bytes 3407872 | tf_op jit(solution)/shard_map/all_to_all | solution.py:523
  17.1 0.0 copy-done.8
  17.1 0.1 reshape.37.stiff_ref
  17.2 0.0 copy-done.9
  17.2 0.1 reshape.41
  17.3 25.9 %all-to-all-done = f32[128,1,3328]{2,1,0:T(1,128)S(1)} async-done(((f32[128,1,3328]{2,1,0:T(1,128)}), f32[128,1,3328]{2,1,0:T(1,128)S(1)}, u32[]{:S(2)}, u32[]{:S(2)}) %all-to-all-start) | async-done | bytes 1703968 | tf_op jit(solution)/shard_map/all_to_all | solution.py:523
  43.2 0.0 copy-done.1
  43.2 0.0 copy-done.2
  43.2 0.0 copy-done.3
  43.2 0.0 copy-done.4
  43.2 0.0 copy-done.5
  43.2 0.0 copy-done.6
  43.2 0.0 copy-done.7
  43.2 15.6 %shard_map.167 = (f32[7,96,1536]{2,1,0:T(8,128)}, f32[512,128]{1,0:T(8,128)}) custom-call(f32[144]{0:T(256)S(1)} %reshape.37.stiff_ref, f32[3328,128]{1,0:T(8,128)S(1)} %bitcast.8, s32[8,128]{1,0:T(8,128)S(1)} %pad.4.slots_ref, bf16[512,256]{1,0:T(8,128)(2,1)S(1)} %copy-done.4, bf16[512,256]{1,0:T(8,128)(2,1)S(1)} %copy-done.3, ...), custom_call_target="tpu_custom_call" | custom-call | tf_op jit(solution)/shard_map/pallas_call | solution.py:554
  58.8 4.7 %all-to-all-start.1 = ((f32[128,1,512]{2,1,0:T(1,128)}), f32[128,1,512]{2,1,0:T(1,128)S(1)}, u32[]{:S(2)}, u32[]{:S(2)}) async-start(f32[128,1,512]{2,1,0:T(1,128)} %bitcast.14), calls=%async_computation.1 | async-start | bytes 524288 | tf_op jit(solution)/shard_map/all_to_all | solution.py:523
  63.5 11.0 %all-to-all-done.1 = f32[128,1,512]{2,1,0:T(1,128)S(1)} async-done(((f32[128,1,512]{2,1,0:T(1,128)}), f32[128,1,512]{2,1,0:T(1,128)S(1)}, u32[]{:S(2)}, u32[]{:S(2)}) %all-to-all-start.1) | async-done | bytes 262176 | tf_op jit(solution)/shard_map/all_to_all | solution.py:523
  74.5 3.7 %shard_map.168 = f32[1792,128]{1,0:T(8,128)} custom-call(s32[1]{0:T(128)} %bitcast.1.place_ref, f32[512,128]{1,0:T(8,128)S(1)} %bitcast.10, f32[7,96,1536]{2,1,0:T(8,128)} %get-tuple-element.11.kept_ref), custom_call_target="tpu_custom_call" | custom-call | tf_op jit(solution)/shard_map/pallas_call | solution.py:577
  78.3 0.0 copy-start
  78.3 4.7 %all-to-all-start.2 = ((f32[128,1,1792]{2,1,0:T(1,128)}), f32[128,1,1792]{2,1,0:T(1,128)S(1)}, u32[]{:S(2)}, u32[]{:S(2)}) async-start(f32[128,1,1792]{2,1,0:T(1,128)} %bitcast.13), calls=%async_computation.2 | async-start | bytes 1835008 | tf_op jit(solution)/shard_map/all_to_all | solution.py:523
  83.0 2.0 %shard_map.169 = (f32[96,2,256]{2,1,0:T(2,128)}, f32[2,192,128]{2,1,0:T(8,128)}, f32[2,192,128]{2,1,0:T(8,128)}) custom-call(f32[512,128]{1,0:T(8,128)S(1)} %bitcast.11, f32[2,192,128]{2,1,0:T(8,128)} %shear_ref.3, f32[2,192,128]{2,1,0:T(8,128)} %relax_ref.3), custom_call_target="tpu_custom_call" | custom-call | tf_op jit(solution)/shard_map/pallas_call | solution.py:596
  85.0 15.9 %all-to-all-done.2 = f32[128,1,1792]{2,1,0:T(1,128)S(1)} async-done(((f32[128,1,1792]{2,1,0:T(1,128)}), f32[128,1,1792]{2,1,0:T(1,128)S(1)}, u32[]{:S(2)}, u32[]{:S(2)}) %all-to-all-start.2) | async-done | bytes 917536 | tf_op jit(solution)/shard_map/all_to_all | solution.py:523
  100.9 0.0 copy-done
  100.9 4.9 %shard_map.170 = (f32[3,2,192,128]{3,2,1,0:T(8,128)}, f32[12,2,192,128]{3,2,1,0:T(8,128)}) custom-call(s32[1]{0:T(128)} %bitcast.parity_ref, f32[144]{0:T(256)S(1)} %reshape.37.stiff_ref, f32[1792,128]{1,0:T(8,128)S(1)} %bitcast.9, f32[12,2,192,128]{3,2,1,0:T(8,128)S(1)} %copy-done, f32[2,192,128]{2,1,0:T(8,128)} %get-tuple-element.12.eff_ref, ...), custom_call_target="tpu_custom_call" | custom-call | tf_op jit(solution)/shard_map/pallas_call | solution.py:606
  (1 shorter events, 0.0 us)
Async XLA Ops:
  5.5 11.6 %copy-start.8 = (f32[12,12]{1,0:T(8,128)S(1)}, f32[12,12]{1,0:T(8,128)}, u32[]{:S(2)}) copy-start(f32[12,12]{1,0:T(8,128)} %param.21) | copy-start | bytes 1732
  5.5 11.7 %copy-start.9 = (s32[768]{0:T(1024)S(1)}, s32[768]{0:T(1024)}, u32[]{:S(2)}) copy-start(s32[768]{0:T(1024)} %param.22) | copy-start | bytes 9220
  5.5 37.7 %copy-start.1 = (bf16[256,512]{1,0:T(8,128)(2,1)S(1)}, bf16[256,512]{1,0:T(8,128)(2,1)}, u32[]{:S(2)}) copy-start(bf16[256,512]{1,0:T(8,128)(2,1)} %constant.51.clone.tl_ref) | copy-start | bytes 786436
  5.5 37.7 %copy-start.2 = (bf16[256,512]{1,0:T(8,128)(2,1)S(1)}, bf16[256,512]{1,0:T(8,128)(2,1)}, u32[]{:S(2)}) copy-start(bf16[256,512]{1,0:T(8,128)(2,1)} %constant.50.clone.th_ref) | copy-start | bytes 786436
  5.5 37.7 %copy-start.3 = (bf16[512,256]{1,0:T(8,128)(2,1)S(1)}, bf16[512,256]{1,0:T(8,128)(2,1)}, u32[]{:S(2)}) copy-start(bf16[512,256]{1,0:T(8,128)(2,1)} %constant.49.clone.fl_ref) | copy-start | bytes 786436
  5.5 37.7 %copy-start.4 = (bf16[512,256]{1,0:T(8,128)(2,1)S(1)}, bf16[512,256]{1,0:T(8,128)(2,1)}, u32[]{:S(2)}) copy-start(bf16[512,256]{1,0:T(8,128)(2,1)} %constant.48.clone.fh_ref) | copy-start | bytes 786436
  5.5 37.6 %copy-start.5 = (f32[32,8,128]{2,1,0:T(8,128)S(1)}, f32[32,8,128]{2,1,0:T(8,128)}, u32[]{:S(2)}) copy-start(f32[32,8,128]{2,1,0:T(8,128)} %constant.53.clone.ratio_ref) | copy-start | bytes 393220
  5.5 37.6 %copy-start.6 = (f32[2,8,256]{2,1,0:T(8,128)S(1)}, f32[2,8,256]{2,1,0:T(8,128)}, u32[]{:S(2)}) copy-start(f32[2,8,256]{2,1,0:T(8,128)} %constant.52.clone.twiddle_ref) | copy-start | bytes 49156
  5.6 37.6 %copy-start.7 = (f32[8,128]{1,0:T(8,128)S(1)}, f32[8,128]{1,0:T(8,128)}, u32[]{:S(2)}) copy-start(f32[8,128]{1,0:T(8,128)} %constant.54.clone.scale_ref) | copy-start | bytes 12292
  5.6 37.6 %all-to-all-start = ((f32[128,1,3328]{2,1,0:T(1,128)}), f32[128,1,3328]{2,1,0:T(1,128)S(1)}, u32[]{:S(2)}, u32[]{:S(2)}) async-start(f32[128,1,3328]{2,1,0:T(1,128)} %bitcast.12), calls=%async_computation | async-start | bytes 3407872 | tf_op jit(solution)/shard_map/all_to_all | solution.py:523
  58.8 15.7 %all-to-all-start.1 = ((f32[128,1,512]{2,1,0:T(1,128)}), f32[128,1,512]{2,1,0:T(1,128)S(1)}, u32[]{:S(2)}, u32[]{:S(2)}) async-start(f32[128,1,512]{2,1,0:T(1,128)} %bitcast.14), calls=%async_computation.1 | async-start | bytes 524288 | tf_op jit(solution)/shard_map/all_to_all | solution.py:523
  78.3 22.6 %copy-start = (f32[12,2,192,128]{3,2,1,0:T(8,128)S(1)}, f32[12,2,192,128]{3,2,1,0:T(8,128)}, u32[]{:S(2)}) copy-start(f32[12,2,192,128]{3,2,1,0:T(8,128)} %stress_ref.3) | copy-start | bytes 7077892
  78.3 22.6 %all-to-all-start.2 = ((f32[128,1,1792]{2,1,0:T(1,128)}), f32[128,1,1792]{2,1,0:T(1,128)S(1)}, u32[]{:S(2)}, u32[]{:S(2)}) async-start(f32[128,1,1792]{2,1,0:T(1,128)} %bitcast.13), calls=%async_computation.2 | async-start | bytes 1835008 | tf_op jit(solution)/shard_map/all_to_all | solution.py:523

commit v3 on v2

--- a/solution.py
+++ b/solution.py
@@ -194,8 +194,6 @@
             eff_ref[0, 16 * r : 16 * r + 16, tile_of(k)] = block
     eff_ref[1, 16:32, :] = eff_ref[0, 0:16, :]
     eff_ref[1, 0:16, :] = down_one(eff_ref[0, 16:32, :])
-    eff_ref[2] = pltpu.roll(eff_ref[0], 1, 1)
-    eff_ref[3] = pltpu.roll(eff_ref[1], 1, 1)
 
     density = jnp.concatenate(
         [jnp.sum(jnp.where(lane == 73 + r, rows_of(0, tail + 1), 0.0), 1, keepdims=True)
@@ -301,71 +299,102 @@
     for c in range(3):
         for name, index in ((0, idx), (1, after), (-1, before)):
             masks[c, name] = jnp.where(lane32 == index + 32 * c, 1.0, 0.0)
-    for g in range(2):
-        for n in range(2):
-            for c in range(3):
-                row = 4 * c + 2 * n + g
-                start = 96 * n + 32 * c
-                for dh in range(2):
-                    block = jnp.zeros((32, LANES), f32)
-                    for c2 in range(3):
-                        for dr in range(2):
-                            value = stiff_ref[12 * row + 4 * c2 + 2 * dr + dh]
-                            block = block + value * masks[c2, dr - n]
-                    high, low = split(block)
-                    matrix_ref[g, start : start + 32, tile_of(dh)] = high
-                    matrix_ref[g, 192 + start : 224 + start, tile_of(dh)] = low
-
-    for k in range(3):
+    for q in range(4):
+        for c in range(3):
+            row, start = 4 * c + q, 96 * q + 32 * c
+            for dh in range(2):
+                block = jnp.zeros((32, LANES), f32)
+                for c2 in range(3):
+                    for dr in range(2):
+                        value = stiff_ref[12 * row + 4 * c2 + 2 * dr + dh]
+                        block = block + value * masks[c2, dr - q // 2]
+                high, low = split(block)
+                matrix_ref[start : start + 32, tile_of(dh)] = high
+                matrix_ref[384 + start : 416 + start, tile_of(dh)] = low
+
+    for k in range(2):
         pad = jnp.zeros((32, HRING), bf16)
         xh_ref[128 * k + 96 : 128 * k + 128, :] = pad
         xl_ref[128 * k + 96 : 128 * k + 128, :] = pad
 
     lane_row = lane_index((1, LANES))
 
-    def step(j, state):
-        moments, beta = state
-        v = basis_ref[j + 1]
-        for k, x in ((0, pltpu.roll(v, 1, 1)), (128, v), (256, pltpu.roll(v, HRING - 1, 1))):
+    def total(x):
+        return jnp.sum(jnp.sum(x, 0, keepdims=True), 1, keepdims=True)
+
+    def spread(v):
+        for k, x in ((0, v), (128, pltpu.roll(v, HRING - 1, 1))):
             high, low = split(x)
             xh_ref[k : k + 96, :] = high
             xl_ref[k : k + 96, :] = low
-        product = jnp.zeros((96, 256), f32)
+
+    first_lane = lane_index((96, 256)) == 0
+
+    def products(n, image, j):
+        cols = slice(256 * n, 256 * n + 256)
+        v, before = basis_ref[j + 1, :, cols], basis_ref[j, :, cols]
+        return image * v, image * image, image * before
+
+    def apply(j):
+        carry, sums = None, None
         for n in range(6):
             cols = slice(256 * n, 256 * n + 256)
-            total = None
-            for g in range(2):
-                rows = slice(128 * (1 - g), 128 * (1 - g) + 256)
-                first = mm(matrix_ref[g], xh_ref[rows, cols])
-                second = mm(matrix_ref[g, 0:192, :], xl_ref[rows, cols])
-                force = first[0:192] + first[192:384] + second
-                for i in range(2):
-                    share = eff_ref[2 * g + i, :, cols]
-                    term = force[96 * i : 96 * i + 96].reshape(3, 32, 256) * share[None]
-                    total = term if total is None else total + term
-            total = total.reshape(96, 256)
-            image_ref[:, cols] = total
-            product = product + total * basis_ref[j + 1, :, cols]
-        inner = jnp.sum(jnp.sum(product, 0, keepdims=True), 1, keepdims=True)
-        alpha = jnp.where(j == 0, 0.0, inner)
-        moments = moments + jnp.where(lane_row == j - 1, alpha, 0.0)
-        rest = image_ref[...] - alpha * basis_ref[j + 1] - beta * basis_ref[j]
-        norm2 = jnp.sum(jnp.sum(rest * rest, 0, keepdims=True), 1, keepdims=True)
-        inverse = jnp.where(norm2 > 0.0, lax.rsqrt(norm2), 0.0)
-        norm = norm2 * inverse
-
-        @pl.when(j < 6)
-        def _():
-            basis_ref[j + 2] = rest * jnp.where(j == 0, -inverse, inverse)
-            leaving(j + 1).start()
-
-        slot = jnp.where(j == 0, 16, jnp.where(j < 6, 7 + j, 100))
-        moments = moments + jnp.where(lane_row == slot, norm, 0.0)
-        return moments, jnp.where(j == 0, 0.0, norm)
-
-    moments, _ = lax.fori_loop(
-        0, 7, step, (jnp.zeros((1, LANES), f32), jnp.ones((1, 1), f32))
-    )
+            first = mm(matrix_ref[...], xh_ref[:, cols])
+            second = mm(matrix_ref[0:384, :], xl_ref[:, cols])
+            force = (first[0:384] + first[384:768] + second).reshape(4, 3, 32, 256)
+            here, above = eff_ref[0, :, cols][None], eff_ref[1, :, cols][None]
+            image = (force[0] * here + force[2] * above).reshape(96, 256)
+            passed = pltpu.roll((force[1] * here + force[3] * above).reshape(96, 256), 1, 1)
+            if n == 0:
+                image_ref[:, cols] = image + jnp.where(first_lane, 0.0, passed)
+            else:
+                image = image + jnp.where(first_lane, carry, passed)
+                image_ref[:, cols] = image
+                terms = products(n, image, j)
+                sums = terms if sums is None else [x + y for x, y in zip(sums, terms)]
+            carry = passed
+        image = image_ref[:, 0:256] + jnp.where(first_lane, carry, 0.0)
+        image_ref[:, 0:256] = image
+        return [total(x + y) for x, y in zip(sums, products(0, image, j))]
+
+    def inverted(x):
+        return jnp.where(x > 0.0, 1.0 / x, 0.0)
+
+    def root(x):
+        return jnp.where(x > 0.0, x * lax.rsqrt(x), 0.0)
+
+    spread(basis_ref[1])
+    load_norm = total(basis_ref[0] * basis_ref[0])
+    _, image_norm, cross = apply(0)
+    rough = jnp.maximum(image_norm - 2.0 * cross + load_norm, 1e-6 * (image_norm + load_norm))
+    scale = jnp.where(rough > 0.0, lax.rsqrt(rough), 0.0)
+
+    def step(j, state):
+        moments, a, b, scale, norm_before = state
+        v = scale * (image_ref[...] - a * basis_ref[j] - b * basis_ref[j - 1])
+        basis_ref[j + 1] = v
+        leaving(j).start()
+        norm = total(v * v)
+        spread(v)
+        inner, image_norm, cross = apply(j)
+        inverse = inverted(norm)
+        a = inner * inverse
+        b = jnp.where(j == 1, 0.0, cross * inverted(norm_before))
+        beside = root(norm) * inverted(jnp.abs(scale) * root(norm_before))
+        moments = (
+            moments
+            + jnp.where(lane_row == j - 1, a, 0.0)
+            + jnp.where(lane_row == jnp.where(j == 1, 16, 6 + j), beside, 0.0)
+            + jnp.where(lane_row == 23 + j, root(inverse), 0.0)
+        )
+        rough = jnp.maximum(image_norm - a * inner - b * cross, 1e-6 * image_norm)
+        scale = jnp.where(rough > 0.0, lax.rsqrt(rough), 0.0)
+        return moments, a, b, scale, norm
+
+    one = jnp.ones((1, 1), f32)
+    moments = lax.fori_loop(
+        1, 7, step, (jnp.zeros((1, LANES), f32), 0.0 * one, one, -scale, one)
+    )[0]
     send_ref[pl.ds(3, LANES, stride=MID_TILES), :] = jnp.broadcast_to(moments, (LANES, LANES))
     for slot in range(7):
         leaving(slot).wait()
@@ -385,29 +414,35 @@
     def total(x):
         return jnp.sum(jnp.sum(x, 0, keepdims=True), 1, keepdims=True)
 
-    direction, y = residual, jnp.zeros((8, LANES), f32)
-    rr = total(residual * residual)
-    for i in range(6):
-        image = (
-            diagonal * direction
-            + beside * pltpu.roll(direction, 7, 0)
-            + pltpu.roll(beside * direction, 1, 0)
+    def applied(v):
+        return (
+            diagonal * v
+            + beside * pltpu.roll(v, 7, 0)
+            + pltpu.roll(beside * v, 1, 0)
         )
-        size = rr / total(direction * image)
-        y = y + size * direction
-        if i < 5:
-            residual = residual - size * image
-            new = total(residual * residual)
-            direction = residual + (new / rr) * direction
-            rr = new
+
+    image = applied(residual)
+    norm, product = total(residual * residual), total(residual * image)
+    size = norm / product
+    direction, along, y = residual, image, size * residual
+    for i in range(5):
+        residual = residual - size * along
+        image = applied(residual)
+        new, product = total(residual * residual), total(residual * image)
+        growth = new / norm
+        size = new / (product - growth * new / size)
+        direction, along = residual + growth * direction, image + growth * along
+        y, norm = y + size * direction, new
     mine = lane_index((8, LANES)) == place_ref[0]
-    own = jnp.sum(jnp.where(mine, y, 0.0), 1, keepdims=True)
-    for slot in range(7):
-        arriving(slot).wait()
-    x = basis_ref[0]
-    for i in range(6):
-        x = x + own[i : i + 1, :] * basis_ref[1 + i]
-    x_ref[...] = x
+    own = jnp.sum(jnp.where(mine, y * table[24:32], 0.0), 1, keepdims=True)
+    for group in ((0, 1, 2), (3, 4), (5, 6)):
+        for slot in group:
+            arriving(slot).wait()
+        x = basis_ref[0] if group[0] == 0 else x_ref[...]
+        for slot in group:
+            if slot:
+                x = x + own[slot - 1 : slot, :] * basis_ref[slot]
+        x_ref[...] = x
 
     lane = lane_index((16, LANES))
 
@@ -446,58 +481,102 @@
             out_ref[at(rows, OUT_TAIL + 1), :] = block
 
 
-def finish_kernel(parity_ref, stiff_ref, recv_ref, stress_ref, eff_ref, kept_ref,
-                  x_out_ref, stress_out_ref, x_ref):
-    comp = pl.program_id(0)
+def finish_kernel(parity_ref, stiff_ref, recv_ref, stress_ref, shear_far_ref, relax_far_ref,
+                  x_out_ref, stress_out_ref, x_ref, new_ref, matrix_ref, shear_ref, relax_ref,
+                  first_ref, x_sems, sems):
+    shear_arriving = pltpu.make_async_copy(shear_far_ref, shear_ref, sems.at[3])
+    relax_arriving = pltpu.make_async_copy(relax_far_ref, relax_ref, sems.at[4])
+    shear_arriving.start()
+    relax_arriving.start()
     parity = parity_ref[0]
     wide = pl.ds(pl.multiple_of(64 * parity, 64), 128)
     narrow = pl.ds(pl.multiple_of(128 * (1 - parity), 64), 64)
 
-    @pl.when(comp == 0)
-    def _():
-        def block(k):
-            return jnp.transpose(recv_ref[pl.ds(k, LANES, stride=OUT_TILES), :])
+    def block(k):
+        return jnp.transpose(recv_ref[pl.ds(k, LANES, stride=OUT_TILES), :])
+
+    def x_leaving(c):
+        return pltpu.make_async_copy(x_ref.at[c, 0:2, 0:COLS], x_out_ref.at[c], x_sems.at[c])
+
+    def leaving(part):
+        rows = pl.ds(64 * part, 64)
+        return pltpu.make_async_copy(
+            new_ref.at[:, :, rows], stress_out_ref.at[:, :, rows], sems.at[part]
+        )
+
+    for c in range(3):
+        for r in range(3):
+            x_ref[c, r, wide, :] = block(4 * c + r)
+        rest = block(4 * c + 3)
+        x_ref[c, 0, narrow, :] = rest[0:64]
+        x_ref[c, 1, narrow, :] = rest[64:128]
+        x_leaving(c).start()
+    rest = block(OUT_TAIL)
+    x_ref[0, 2, narrow, :] = rest[0:64]
+    x_ref[1, 2, narrow, :] = rest[64:128]
+    rest = block(OUT_TAIL + 1)
+    x_ref[2, 2, narrow, :] = rest[0:64]
+    for c in range(3):
+        for r in range(3):
+            x_ref[c, r, COLS : COLS + 1, :] = rest[64 + 3 * c + r : 65 + 3 * c + r]
+
+    lane = lane_index((16, 192))
+    same = (lane % 16) == row_index((16, 192))
+    for a in range(12):
+        line = jnp.zeros((16, 192), f32)
+        for b in range(12):
+            line = jnp.where(lane // 16 == b, stiff_ref[12 * a + b], line)
+        high, low = split(jnp.where(same, line, 0.0))
+        for k, piece in enumerate((high, high, low)):
+            matrix_ref[16 * a : 16 * a + 16, 256 * k : 256 * k + 192] = piece
+            matrix_ref[16 * a : 16 * a + 16, 256 * k + 192 : 256 * k + 256] = jnp.zeros(
+                (16, 64), bf16
+            )
+
+    pad = jnp.zeros((64, 2 * LANES), bf16)
+
+    def forces(n):
+        corners = []
         for c in range(3):
-            for r in range(3):
-                x_ref[c, r, wide, :] = block(4 * c + r)
-            rest = block(4 * c + 3)
-            x_ref[c, 0, narrow, :] = rest[0:64]
-            x_ref[c, 1, narrow, :] = rest[64:128]
-        rest = block(OUT_TAIL)
-        x_ref[0, 2, narrow, :] = rest[0:64]
-        x_ref[1, 2, narrow, :] = rest[64:128]
-        rest = block(OUT_TAIL + 1)
-        x_ref[2, 2, narrow, :] = rest[0:64]
-        for c in range(3):
-            for r in range(3):
-                x_ref[c, r, COLS : COLS + 1, :] = rest[64 + 3 * c + r : 65 + 3 * c + r]
-        for c in range(3):
-            x_out_ref[c] = x_ref[c, 0:2, 0:COLS, :]
-
-    chunk = 24
-    for r in range(2):
-        for n in range(COLS // chunk):
-            start = n * chunk
-            rows = slice(start, start + chunk)
-            corners = []
-            for c in range(3):
-                for dr in range(2):
-                    for dh in range(2):
-                        corners.append(x_ref[c, r + dr, start + dh : start + dh + chunk, :])
-            eff, kept = eff_ref[r, rows, :], kept_ref[r, rows, :]
-            for q in range(4):
-                row = (4 * comp + q) * 12
-                force = stiff_ref[row] * corners[0]
-                for k in range(1, 12):
-                    force = force + stiff_ref[row + k] * corners[k]
-                stress_out_ref[q, r, rows, :] = kept * stress_ref[q, r, rows, :] + eff * force
-
-
-def potential_kernel(recv_ref, shear_ref, relax_ref, out_ref, eff_ref, kept_ref):
-    relax = relax_ref[...]
-    share = 1.0 / (1.0 + 0.5 * relax)
-    eff_ref[...] = shear_ref[...] * share
-    kept_ref[...] = (1.0 - 0.5 * relax) * share
+            for dr in range(2):
+                for dh in range(2):
+                    span = slice(16 * n + dh, 16 * n + dh + 16)
+                    corners.append(
+                        jnp.concatenate([x_ref[c, dr, span, :], x_ref[c, 1 + dr, span, :]], 1)
+                    )
+        high, low = split(jnp.concatenate(corners, 0))
+        return mm(matrix_ref[...], jnp.concatenate([high, pad, low, pad, high, pad], 0))
+
+    def store(n, force):
+        rows = slice(16 * n, 16 * n + 16)
+        for r in range(2):
+            relax = relax_ref[r, rows, :]
+            share = 1.0 / (1.0 + 0.5 * relax)
+            eff, kept = shear_ref[r, rows, :] * share, (1.0 - 0.5 * relax) * share
+            for a in range(12):
+                new_ref[a, r, rows, :] = (
+                    kept * stress_ref[a, r, rows, :]
+                    + eff * force[16 * a : 16 * a + 16, tile_of(r)]
+                )
+
+    for n in range(4):
+        first_ref[n] = forces(n)
+    shear_arriving.wait()
+    relax_arriving.wait()
+    for n in range(4):
+        store(n, first_ref[n])
+    leaving(0).start()
+    for n in range(4, COLS // 16):
+        store(n, forces(n))
+        if n % 4 == 3:
+            leaving(n // 4).start()
+    for c in range(3):
+        x_leaving(c).wait()
+    for part in range(3):
+        leaving(part).wait()
+
+
+def potential_kernel(recv_ref, out_ref):
     blocks = [jnp.transpose(recv_ref[pl.ds(k, LANES, stride=MID_TILES), :]) for k in range(3)]
     lines = jnp.concatenate(blocks, 0)
     for part in range(2):
@@ -562,10 +641,10 @@
         scratch_shapes=[
             pltpu.VMEM((8, 96, HRING), f32),
             pltpu.SemaphoreType.DMA((7,)),
-            pltpu.VMEM((4, 32, HRING), f32),
-            pltpu.VMEM((2, 384, 256), bf16),
-            pltpu.VMEM((384, HRING), bf16),
-            pltpu.VMEM((384, HRING), bf16),
+            pltpu.VMEM((2, 32, HRING), f32),
+            pltpu.VMEM((768, 256), bf16),
+            pltpu.VMEM((256, HRING), bf16),
+            pltpu.VMEM((256, HRING), bf16),
             pltpu.VMEM((96, HRING), f32),
             pltpu.VMEM((512, LANES), f32),
             pltpu.VMEM((NR, 8, 256), f32),
@@ -593,30 +672,37 @@
     )(place, shared, far_memory(basis))
     returned = exchanged(back)
 
-    potential, effective, kept = pl.pallas_call(
+    potential = pl.pallas_call(
         potential_kernel,
         grid=(1,),
-        in_specs=[whole((MID_TILES * LANES, LANES)), field, field],
-        out_specs=[whole((96, 2, 256)), field, field],
-        out_shape=[jax.ShapeDtypeStruct((96, 2, 256), f32)]
-        + [pltpu.HBM((2, COLS, LANES), f32)] * 2,
+        in_specs=[whole((MID_TILES * LANES, LANES))],
+        out_specs=whole((96, 2, 256)),
+        out_shape=jax.ShapeDtypeStruct((96, 2, 256), f32),
         compiler_params=params(4),
-    )(shared, far_memory(shear_modulus), far_memory(relaxation))
+    )(shared)
 
     displacement, stress_new = pl.pallas_call(
         finish_kernel,
-        grid=(3,),
-        in_specs=[smem, smem, whole((OUT_TILES * LANES, LANES)), four, field, field],
-        out_specs=[whole((3, 2, COLS, LANES)), four],
+        in_specs=[smem, smem]
+        + [pl.BlockSpec(memory_space=pltpu.VMEM)] * 2
+        + [pl.BlockSpec(memory_space=pl.ANY)] * 2,
+        out_specs=[pl.BlockSpec(memory_space=pl.ANY)] * 2,
         out_shape=[
             jax.ShapeDtypeStruct((3, 2, COLS, LANES), f32),
             jax.ShapeDtypeStruct((12, 2, COLS, LANES), f32),
         ],
         scratch_shapes=[
             pltpu.VMEM((3, 3, COLS + 8, LANES), f32),
+            pltpu.VMEM((12, 2, COLS, LANES), f32),
+            pltpu.VMEM((192, 768), bf16),
+            pltpu.VMEM((2, COLS, LANES), f32),
+            pltpu.VMEM((2, COLS, LANES), f32),
+            pltpu.VMEM((4, COLS, 2 * LANES), f32),
+            pltpu.SemaphoreType.DMA((3,)),
+            pltpu.SemaphoreType.DMA((5,)),
         ],
         compiler_params=params(12),
-    )(parity, stiff, returned, stress_old, far_memory(effective), far_memory(kept))
+    )(parity, stiff, returned, stress_old, far_memory(shear_modulus), far_memory(relaxation))
     return displacement, stress_new, potential
 
 

time: 106 us -> 104 us (0.981)
  Pallas kernels: 31.1 us -> 28.3 us
  waiting for transfers between devices: 52.8 us -> 53.9 us
    pallas_call x1, Pallas kernels: 2.01 us -> 0.85 us  [body(): pl.pallas_call(potential_kernel, grid=(1,), in_specs=[whole((MID_TILES *...]
    all_to_all x3, waiting for transfers between devices: 52.8 us -> 53.9 us  [exchanged(): return lax.all_to_all(rows, ALL, 0, 0, tiled=True).reshape(count, LANES)]
    pallas_call x1, Pallas kernels: 4.9 us -> 3.76 us  [body(): pl.pallas_call(finish_kernel, in_specs=[smem, smem] + [pl.BlockSpec(memor...]
  transfers between devices with their start and end apart: 3 -> 3, of which waited for: 3 -> 3; matrix products, arithmetic and copies ran while one was open for 0% -> 0% of each run, Pallas kernels for 2% -> 1%
where the time goes in v3:
time: 104 us
  waiting for transfers between devices  53.9 us (52%)
  Pallas kernels  28.3 us (27%)
  starting transfers between devices  20.7 us (20%)
    all_to_all x3, waiting for transfers between devices, exchanged(): return lax.all_to_all(rows, ALL, 0, 0, tiled=True).reshape(count, LANES)  53.9 us
    all_to_all x3, starting transfers between devices, exchanged(): return lax.all_to_all(rows, ALL, 0, 0, tiled=True).reshape(count, LANES)  20.7 us
    pallas_call x1, Pallas kernels, body(): pl.pallas_call(functools.partial(section_kernel, radius=[float(x) for x i...  15.1 us
    pallas_call x1, Pallas kernels, body(): pl.pallas_call(pack_kernel, grid=(3,), in_specs=[smem, smem, one, one, fo...  4.86 us
    pallas_call x1, Pallas kernels, body(): pl.pallas_call(finish_kernel, in_specs=[smem, smem] + [pl.BlockSpec(memor...  3.76 us
    pallas_call x1, Pallas kernels, body(): pl.pallas_call(solve_kernel, grid=(1,), in_specs=[smem, whole((MID_TILES...  3.7 us
  transfers between devices with their start and end apart: 3, of which 3 were waited for; matrix products, arithmetic and copies ran while one was open for 0% of the time, Pallas kernels for 1%

profile of v3, /device:TPU:1, one launch (start us, length us, event | category | flops | bytes accessed | tf_op | source)
XLA Modules:
  0.0 104.0 jit_solution(5758267073572810290)
XLA Ops:
  0.6 4.9 %shard_map.166 = f32[3328,128]{1,0:T(8,128)} custom-call(s32[1]{0:T(128)} %bitcast.parity_ref, f32[2]{0:T(128)} %density_ref.1, f32[3,2,192,128]{3,2,1,0:T(8,128)} %load_ref.1, f32[3,2,192,128]{3,2,1,0:T(8,128)} %prev_ref.1, f32[12,2,192,128]{3,2,1,0:T(8,128)} %stress_ref.3, f32[2,192,128]{2,1,0:T(8,128)} %shear_far_ref.1, f32[2,192,128]{2,1,0:T(8,128)} %relax_far_ref.1), custom_call_target="tpu_custom_call" | custom-call | tf_op jit(solution)/shard_map/pallas_call | solution.py:622
  5.5 0.0 copy-start.8
  5.5 0.0 copy-start.9
  5.5 0.0 copy-start.1
  5.5 0.0 copy-start.2
  5.5 0.0 copy-start.3
  5.5 0.0 copy-start.4
  5.6 0.0 copy-start.5
  5.6 0.0 copy-start.6
  5.6 0.0 copy-start.7
  5.6 11.5 %all-to-all-start = ((f32[128,1,3328]{2,1,0:T(1,128)}), f32[128,1,3328]{2,1,0:T(1,128)S(1)}, u32[]{:S(2)}, u32[]{:S(2)}) async-start(f32[128,1,3328]{2,1,0:T(1,128)} %bitcast.12), calls=%async_computation | async-start | bytes 3407872 | tf_op jit(solution)/shard_map/all_to_all | solution.py:602
  17.1 0.0 copy-done.8
  17.1 0.1 reshape.37.stiff_ref
  17.2 0.0 copy-done.9
  17.2 0.1 reshape.41
  17.3 25.9 %all-to-all-done = f32[128,1,3328]{2,1,0:T(1,128)S(1)} async-done(((f32[128,1,3328]{2,1,0:T(1,128)}), f32[128,1,3328]{2,1,0:T(1,128)S(1)}, u32[]{:S(2)}, u32[]{:S(2)}) %all-to-all-start) | async-done | bytes 1703968 | tf_op jit(solution)/shard_map/all_to_all | solution.py:602
  43.2 0.0 copy-done.1
  43.2 0.0 copy-done.2
  43.2 0.0 copy-done.3
  43.2 0.0 copy-done.4
  43.2 0.0 copy-done.5
  43.2 0.0 copy-done.6
  43.2 0.0 copy-done.7
  43.2 15.1 %shard_map.167 = (f32[7,96,1536]{2,1,0:T(8,128)}, f32[512,128]{1,0:T(8,128)}) custom-call(f32[144]{0:T(256)S(1)} %reshape.37.stiff_ref, f32[3328,128]{1,0:T(8,128)S(1)} %bitcast.8, s32[8,128]{1,0:T(8,128)S(1)} %pad.4.slots_ref, bf16[512,256]{1,0:T(8,128)(2,1)S(1)} %copy-done.4, bf16[512,256]{1,0:T(8,128)(2,1)S(1)} %copy-done.3, ...), custom_call_target="tpu_custom_call" | custom-call | tf_op jit(solution)/shard_map/pallas_call | solution.py:633
  58.4 4.7 %all-to-all-start.1 = ((f32[128,1,512]{2,1,0:T(1,128)}), f32[128,1,512]{2,1,0:T(1,128)S(1)}, u32[]{:S(2)}, u32[]{:S(2)}) async-start(f32[128,1,512]{2,1,0:T(1,128)} %bitcast.14), calls=%async_computation.1 | async-start | bytes 524288 | tf_op jit(solution)/shard_map/all_to_all | solution.py:602
  63.1 11.0 %all-to-all-done.1 = f32[128,1,512]{2,1,0:T(1,128)S(1)} async-done(((f32[128,1,512]{2,1,0:T(1,128)}), f32[128,1,512]{2,1,0:T(1,128)S(1)}, u32[]{:S(2)}, u32[]{:S(2)}) %all-to-all-start.1) | async-done | bytes 262176 | tf_op jit(solution)/shard_map/all_to_all | solution.py:602
  74.1 0.0 copy-start
  74.1 3.7 %shard_map.168 = f32[1792,128]{1,0:T(8,128)} custom-call(s32[1]{0:T(128)} %bitcast.1.place_ref, f32[512,128]{1,0:T(8,128)S(1)} %bitcast.10, f32[7,96,1536]{2,1,0:T(8,128)} %get-tuple-element.8.kept_ref), custom_call_target="tpu_custom_call" | custom-call | tf_op jit(solution)/shard_map/pallas_call | solution.py:656
  77.8 4.6 %all-to-all-start.2 = ((f32[128,1,1792]{2,1,0:T(1,128)}), f32[128,1,1792]{2,1,0:T(1,128)S(1)}, u32[]{:S(2)}, u32[]{:S(2)}) async-start(f32[128,1,1792]{2,1,0:T(1,128)} %bitcast.13), calls=%async_computation.2 | async-start | bytes 1835008 | tf_op jit(solution)/shard_map/all_to_all | solution.py:602
  82.3 0.9 shard_map.170
  83.2 17.0 %all-to-all-done.2 = f32[128,1,1792]{2,1,0:T(1,128)S(1)} async-done(((f32[128,1,1792]{2,1,0:T(1,128)}), f32[128,1,1792]{2,1,0:T(1,128)S(1)}, u32[]{:S(2)}, u32[]{:S(2)}) %all-to-all-start.2) | async-done | bytes 917536 | tf_op jit(solution)/shard_map/all_to_all | solution.py:602
  100.2 0.0 copy-done
  100.2 3.8 %shard_map.169 = (f32[3,2,192,128]{3,2,1,0:T(8,128)}, f32[12,2,192,128]{3,2,1,0:T(8,128)}) custom-call(s32[1]{0:T(128)} %bitcast.parity_ref, f32[144]{0:T(256)S(1)} %reshape.37.stiff_ref, f32[1792,128]{1,0:T(8,128)S(1)} %bitcast.9, f32[12,2,192,128]{3,2,1,0:T(8,128)S(1)} %copy-done, f32[2,192,128]{2,1,0:T(8,128)} %shear_far_ref.1, f32[2,192,128]{2,1,0:T(8,128)} %relax_far_ref.1), custom_call_target="tpu_custom_call" | custom-call | tf_op jit(solution)/shard_map/pallas_call | solution.py:684
  (1 shorter events, 0.0 us)
Async XLA Ops:
  5.5 11.6 %copy-start.8 = (f32[12,12]{1,0:T(8,128)S(1)}, f32[12,12]{1,0:T(8,128)}, u32[]{:S(2)}) copy-start(f32[12,12]{1,0:T(8,128)} %param.21) | copy-start | bytes 1732
  5.5 11.7 %copy-start.9 = (s32[768]{0:T(1024)S(1)}, s32[768]{0:T(1024)}, u32[]{:S(2)}) copy-start(s32[768]{0:T(1024)} %param.22) | copy-start | bytes 9220
  5.5 37.7 %copy-start.1 = (bf16[256,512]{1,0:T(8,128)(2,1)S(1)}, bf16[256,512]{1,0:T(8,128)(2,1)}, u32[]{:S(2)}) copy-start(bf16[256,512]{1,0:T(8,128)(2,1)} %constant.51.clone.tl_ref) | copy-start | bytes 786436
  5.5 37.7 %copy-start.2 = (bf16[256,512]{1,0:T(8,128)(2,1)S(1)}, bf16[256,512]{1,0:T(8,128)(2,1)}, u32[]{:S(2)}) copy-start(bf16[256,512]{1,0:T(8,128)(2,1)} %constant.50.clone.th_ref) | copy-start | bytes 786436
  5.5 37.7 %copy-start.3 = (bf16[512,256]{1,0:T(8,128)(2,1)S(1)}, bf16[512,256]{1,0:T(8,128)(2,1)}, u32[]{:S(2)}) copy-start(bf16[512,256]{1,0:T(8,128)(2,1)} %constant.49.clone.fl_ref) | copy-start | bytes 786436
  5.5 37.7 %copy-start.4 = (bf16[512,256]{1,0:T(8,128)(2,1)S(1)}, bf16[512,256]{1,0:T(8,128)(2,1)}, u32[]{:S(2)}) copy-start(bf16[512,256]{1,0:T(8,128)(2,1)} %constant.48.clone.fh_ref) | copy-start | bytes 786436
  5.6 37.6 %copy-start.5 = (f32[32,8,128]{2,1,0:T(8,128)S(1)}, f32[32,8,128]{2,1,0:T(8,128)}, u32[]{:S(2)}) copy-start(f32[32,8,128]{2,1,0:T(8,128)} %constant.53.clone.ratio_ref) | copy-start | bytes 393220
  5.6 37.6 %copy-start.6 = (f32[2,8,256]{2,1,0:T(8,128)S(1)}, f32[2,8,256]{2,1,0:T(8,128)}, u32[]{:S(2)}) copy-start(f32[2,8,256]{2,1,0:T(8,128)} %constant.52.clone.twiddle_ref) | copy-start | bytes 49156
  5.6 37.6 %copy-start.7 = (f32[8,128]{1,0:T(8,128)S(1)}, f32[8,128]{1,0:T(8,128)}, u32[]{:S(2)}) copy-start(f32[8,128]{1,0:T(8,128)} %constant.54.clone.scale_ref) | copy-start | bytes 12292
  5.6 37.6 %all-to-all-start = ((f32[128,1,3328]{2,1,0:T(1,128)}), f32[128,1,3328]{2,1,0:T(1,128)S(1)}, u32[]{:S(2)}, u32[]{:S(2)}) async-start(f32[128,1,3328]{2,1,0:T(1,128)} %bitcast.12), calls=%async_computation | async-start | bytes 3407872 | tf_op jit(solution)/shard_map/all_to_all | solution.py:602
  58.4 15.7 %all-to-all-start.1 = ((f32[128,1,512]{2,1,0:T(1,128)}), f32[128,1,512]{2,1,0:T(1,128)S(1)}, u32[]{:S(2)}, u32[]{:S(2)}) async-start(f32[128,1,512]{2,1,0:T(1,128)} %bitcast.14), calls=%async_computation.1 | async-start | bytes 524288 | tf_op jit(solution)/shard_map/all_to_all | solution.py:602
  74.1 26.2 %copy-start = (f32[12,2,192,128]{3,2,1,0:T(8,128)S(1)}, f32[12,2,192,128]{3,2,1,0:T(8,128)}, u32[]{:S(2)}) copy-start(f32[12,2,192,128]{3,2,1,0:T(8,128)} %stress_ref.3) | copy-start | bytes 7077892
  77.8 22.4 %all-to-all-start.2 = ((f32[128,1,1792]{2,1,0:T(1,128)}), f32[128,1,1792]{2,1,0:T(1,128)S(1)}, u32[]{:S(2)}, u32[]{:S(2)}) async-start(f32[128,1,1792]{2,1,0:T(1,128)} %bitcast.13), calls=%async_computation.2 | async-start | bytes 1835008 | tf_op jit(solution)/shard_map/all_to_all | solution.py:602

commit v4 on v3

--- a/solution.py
+++ b/solution.py
@@ -144,7 +144,7 @@
 
 def section_kernel(stiff_ref, recv_ref, slots_ref, fh_ref, fl_ref, th_ref, tl_ref, twiddle_ref,
                    ratio_ref, scale_ref, kept_ref, send_ref, basis_ref, sems,
-                   eff_ref, matrix_ref, xh_ref, xl_ref, image_ref, coef_ref, pot_ref,
+                   eff_ref, matrix_ref, xh_ref, xl_ref, xs_ref, halo_ref, image_ref, coef_ref, pot_ref,
                    *, radius):
     lane = lane_index((16, LANES))
 
@@ -166,16 +166,23 @@
             yield 3 * u + 2, rows_of(2 * u + 1, wide_tile)
 
     tail = TAIL_TILE
+
+    def halves(c, r):
+        for h in range(2):
+            yield slice(8 * h, 8 * h + 8), slice(32 * c + 16 * h + 8 * r, 32 * c + 16 * h + 8 * r + 8)
+
     for c in range(3):
         for r in range(2):
-            rows = slice(32 * c + 16 * r, 32 * c + 16 * r + 16)
             for k, block in unrolled(7 * c + r, 7 * c + 2, r):
-                basis_ref[1, rows, tile_of(k)] = block
+                for part, rows in halves(c, r):
+                    basis_ref[1, rows, tile_of(k)] = block[part]
             for k, block in unrolled(7 * c + 3 + r, 7 * c + 6, r):
-                basis_ref[0, rows, tile_of(k)] = block
-        rows = slice(32 * c, 32 * c + 16)
+                for part, rows in halves(c, r):
+                    basis_ref[0, rows, tile_of(k)] = block[part]
         for k, block in unrolled(7 * c + 5, tail + c // 2, c % 2):
-            basis_ref[0, rows, tile_of(k)] += down_one(block)
+            block = down_one(block)
+            for part, rows in halves(c, 0):
+                basis_ref[0, rows, tile_of(k)] += block[part]
     leaving(0).start()
     for t in range(8):
         following = (t + 1) % 8
@@ -187,17 +194,22 @@
                 value = jnp.where(lane == target, pltpu.roll(block, shift, 1), 0.0)
                 if r == 2:
                     value = down_one(value)
-                start = 32 * c + 16 * (r % 2)
-                basis_ref[0, start : start + 16, tile_of(k)] += value
+                for part, rows in halves(c, r % 2):
+                    basis_ref[0, rows, tile_of(k)] += value[part]
     for r in range(2):
         for k, block in unrolled(EFF_TILE + r, EFF_TILE + 2, r):
-            eff_ref[0, 16 * r : 16 * r + 16, tile_of(k)] = block
-    eff_ref[1, 16:32, :] = eff_ref[0, 0:16, :]
-    eff_ref[1, 0:16, :] = down_one(eff_ref[0, 16:32, :])
-
+            above = block if r == 0 else down_one(block)
+            for part, rows in halves(0, r):
+                eff_ref[0, rows, tile_of(k)] = block[part]
+            for part, rows in halves(0, 1 - r):
+                eff_ref[1, rows, tile_of(k)] = above[part]
+
+    density = [
+        jnp.sum(jnp.where(lane == 73 + r, rows_of(0, tail + 1), 0.0), 1, keepdims=True)
+        for r in range(2)
+    ]
     density = jnp.concatenate(
-        [jnp.sum(jnp.where(lane == 73 + r, rows_of(0, tail + 1), 0.0), 1, keepdims=True)
-         for r in range(2)], 0
+        [density[0][0:8], density[1][0:8], density[0][8:16], density[1][8:16]], 0
     )
 
     weight = density * math.sqrt(2.0 / HRING)
@@ -227,7 +239,7 @@
         coef_ref[256 * k + 192 : 256 * k + 256, :] = jnp.zeros((64, LANES), f32)
 
     def place(r, k):
-        return pl.ds(256 * k + 16 * (r % 2) + r // 2, 8, stride=32)
+        return pl.ds(256 * k + 16 * (r // 16) + 8 * (r % 2) + r // 2 % 8, 8, stride=32)
 
     zero = jnp.zeros((8, LANES), f32)
     for k in range(2):
@@ -265,7 +277,10 @@
         pick = jnp.where(row_index((LDEG, LANES)) == where_from, 1.0, 0.0).astype(bf16)
         chosen = mm(xl_ref[0:192, 0:LDEG], pick)
         chosen = chosen[0:64] + chosen[64:128] + chosen[128:192]
-        c0, c1, c2, c3 = [chosen[16 * k : 16 * k + 16] for k in range(4)]
+        c0, c1, c2, c3 = [
+            jnp.concatenate([chosen[k : k + 8], chosen[k + 16 : k + 24]], 0)
+            for k in (0, 8, 32, 40)
+        ]
         joined = [
             jnp.where(lane < 96, c0, pltpu.roll(c1, 96, 1)),
             jnp.where(lane < 64, pltpu.roll(c1, 96, 1), pltpu.roll(c2, 64, 1)),
@@ -291,31 +306,40 @@
     for a in range(6):
         basis_ref[0, 0:32, 256 * a : 256 * a + 256] += gravity_gain * density * parts[a]
 
-    idx = row_index((32, LANES))
-    lane32 = lane_index((32, LANES))
-    after = jnp.where(idx < 16, idx + 16, jnp.where(idx == 31, -1000, idx - 15))
-    before = jnp.where(idx >= 16, idx - 16, jnp.where(idx == 0, -1000, idx + 15))
-    masks = {}
-    for c in range(3):
-        for name, index in ((0, idx), (1, after), (-1, before)):
-            masks[c, name] = jnp.where(lane32 == index + 32 * c, 1.0, 0.0)
-    for q in range(4):
+    idx = row_index((16, 256))
+    wide_lane = lane_index((16, 256))
+    after = jnp.where(idx < 8, idx + 8, jnp.where(idx == 15, -1000, idx - 7))
+    before = jnp.where(idx >= 8, idx - 8, jnp.where(idx == 0, -1000, idx + 7))
+    is_high = (wide_lane < 96) | ((wide_lane >= 192) & (wide_lane < 200))
+    for half in range(2):
+        masks = {}
         for c in range(3):
-            row, start = 4 * c + q, 96 * q + 32 * c
-            for dh in range(2):
-                block = jnp.zeros((32, LANES), f32)
+            for dr, index in ((0, idx), (1, after), (-1, before)):
+                for dh in range(2):
+                    base = 48 * dh + 16 * c
+                    hit = (wide_lane == index + base) | (wide_lane == index + base + 96)
+                    if dr == 1 - 2 * half:
+                        edge = 15 if half == 0 else 0
+                        beyond = 192 + 3 * dh + c
+                        hit |= (idx == edge) & (
+                            (wide_lane == beyond) | (wide_lane == beyond + 8)
+                        )
+                    masks[c, dr, dh] = jnp.where(hit, 1.0, 0.0)
+        for q in range(4):
+            for c in range(3):
+                row, start = 4 * c + q, 48 * q + 16 * c
+                block = jnp.zeros((16, 256), f32)
                 for c2 in range(3):
                     for dr in range(2):
-                        value = stiff_ref[12 * row + 4 * c2 + 2 * dr + dh]
-                        block = block + value * masks[c2, dr - q // 2]
-                high, low = split(block)
-                matrix_ref[start : start + 32, tile_of(dh)] = high
-                matrix_ref[384 + start : 416 + start, tile_of(dh)] = low
-
-    for k in range(2):
-        pad = jnp.zeros((32, HRING), bf16)
-        xh_ref[128 * k + 96 : 128 * k + 128, :] = pad
-        xl_ref[128 * k + 96 : 128 * k + 128, :] = pad
+                        for dh in range(2):
+                            value = stiff_ref[12 * row + 4 * c2 + 2 * dr + dh]
+                            block = block + value * masks[c2, dr - q // 2, dh]
+                high = block.astype(bf16)
+                low = jnp.where(is_high, block - high.astype(f32), 0.0).astype(bf16)
+                matrix_ref[half, start : start + 16, :] = high
+                matrix_ref[half, 192 + start : 208 + start, :] = low
+        xs_ref[half, 208:256, :] = jnp.zeros((48, HRING), bf16)
+        halo_ref[half, 6:8, :] = jnp.zeros((2, HRING), f32)
 
     lane_row = lane_index((1, LANES))
 
@@ -323,10 +347,20 @@
         return jnp.sum(jnp.sum(x, 0, keepdims=True), 1, keepdims=True)
 
     def spread(v):
-        for k, x in ((0, v), (128, pltpu.roll(v, HRING - 1, 1))):
+        for dh, x in ((0, v), (1, pltpu.roll(v, HRING - 1, 1))):
             high, low = split(x)
-            xh_ref[k : k + 96, :] = high
-            xl_ref[k : k + 96, :] = low
+            for c in range(3):
+                for half in range(2):
+                    rows = slice(32 * c + 16 * half, 32 * c + 16 * half + 16)
+                    start = 48 * dh + 16 * c
+                    xs_ref[half, start : start + 16, :] = high[rows]
+                    xs_ref[half, 96 + start : 112 + start, :] = low[rows]
+                    edge = 32 * c + 16 - half
+                    halo_ref[half, 3 * dh + c : 3 * dh + c + 1, :] = x[edge : edge + 1]
+        for half in range(2):
+            x = halo_ref[half]
+            high = x.astype(bf16).astype(f32)
+            xs_ref[half, 192:208, :] = jnp.concatenate([high, x - high], 0).astype(bf16)
 
     first_lane = lane_index((96, 256)) == 0
 
@@ -339,12 +373,20 @@
         carry, sums = None, None
         for n in range(6):
             cols = slice(256 * n, 256 * n + 256)
-            first = mm(matrix_ref[...], xh_ref[:, cols])
-            second = mm(matrix_ref[0:384, :], xl_ref[:, cols])
-            force = (first[0:384] + first[384:768] + second).reshape(4, 3, 32, 256)
-            here, above = eff_ref[0, :, cols][None], eff_ref[1, :, cols][None]
-            image = (force[0] * here + force[2] * above).reshape(96, 256)
-            passed = pltpu.roll((force[1] * here + force[3] * above).reshape(96, 256), 1, 1)
+            images, passes = [], []
+            for half in range(2):
+                rows = slice(16 * half, 16 * half + 16)
+                force = mm(matrix_ref[half], xs_ref[half, :, cols])
+                force = (force[0:192] + force[192:384]).reshape(4, 3, 16, 256)
+                here, above = eff_ref[0, rows, cols][None], eff_ref[1, rows, cols][None]
+                images.append(force[0] * here + force[2] * above)
+                passes.append(force[1] * here + force[3] * above)
+
+            def joined(parts):
+                return jnp.concatenate([parts[h][c] for c in range(3) for h in range(2)], 0)
+
+            image = joined(images)
+            passed = pltpu.roll(joined(passes), 1, 1)
             if n == 0:
                 image_ref[:, cols] = image + jnp.where(first_lane, 0.0, passed)
             else:
@@ -447,7 +489,10 @@
     lane = lane_index((16, LANES))
 
     def node_rows(c, r, k):
-        block = x_ref[32 * c + 16 * (r % 2) : 32 * c + 16 * (r % 2) + 16, tile_of(k)]
+        start = 32 * c + 8 * (r % 2)
+        block = jnp.concatenate(
+            [x_ref[start : start + 8, tile_of(k)], x_ref[start + 16 : start + 24, tile_of(k)]], 0
+        )
         return up_one(block) if r == 2 else block
 
     def at(t, tile):
@@ -642,9 +687,11 @@
             pltpu.VMEM((8, 96, HRING), f32),
             pltpu.SemaphoreType.DMA((7,)),
             pltpu.VMEM((2, 32, HRING), f32),
-            pltpu.VMEM((768, 256), bf16),
-            pltpu.VMEM((256, HRING), bf16),
-            pltpu.VMEM((256, HRING), bf16),
+            pltpu.VMEM((2, 384, 256), bf16),
+            pltpu.VMEM((192, LDEG), bf16),
+            pltpu.VMEM((192, LDEG), bf16),
+            pltpu.VMEM((2, 256, HRING), bf16),
+            pltpu.VMEM((2, 8, HRING), f32),
             pltpu.VMEM((96, HRING), f32),
             pltpu.VMEM((512, LANES), f32),
             pltpu.VMEM((NR, 8, 256), f32),

time: 104 us -> 103 us (level)
  Pallas kernels: 28.3 us -> 26.7 us
    pallas_call x1, Pallas kernels: 15.1 us -> 13.5 us  [body(): pl.pallas_call(functools.partial(section_kernel, radius=[float(x) for x i...]
where the time goes in v4:
time: 103 us; the launch traced here: 102 us
  waiting for transfers between devices  53.9 us (52%)
  Pallas kernels  26.7 us (26%)
  starting transfers between devices  20.7 us (20%)
    all_to_all x3, waiting for transfers between devices, exchanged(): return lax.all_to_all(rows, ALL, 0, 0, tiled=True).reshape(count, LANES)  53.9 us
    all_to_all x3, starting transfers between devices, exchanged(): return lax.all_to_all(rows, ALL, 0, 0, tiled=True).reshape(count, LANES)  20.7 us
    pallas_call x1, Pallas kernels, body(): pl.pallas_call(functools.partial(section_kernel, radius=[float(x) for x i...  13.5 us
    pallas_call x1, Pallas kernels, body(): pl.pallas_call(pack_kernel, grid=(3,), in_specs=[smem, smem, one, one, fo...  4.86 us
    pallas_call x1, Pallas kernels, body(): pl.pallas_call(finish_kernel, in_specs=[smem, smem] + [pl.BlockSpec(memor...  3.76 us
    pallas_call x1, Pallas kernels, body(): pl.pallas_call(solve_kernel, grid=(1,), in_specs=[smem, whole((MID_TILES...  3.7 us
  transfers between devices with their start and end apart: 3, of which 3 were waited for; matrix products, arithmetic and copies ran while one was open for 0% of the time, Pallas kernels for 1%

profile of v4, /device:TPU:1, one launch (start us, length us, event | category | flops | bytes accessed | tf_op | source)
XLA Modules:
  0.0 102.3 jit_solution(16110264574769221413)
XLA Ops:
  0.6 4.9 %shard_map.166 = f32[3328,128]{1,0:T(8,128)} custom-call(s32[1]{0:T(128)} %bitcast.parity_ref, f32[2]{0:T(128)} %density_ref.1, f32[3,2,192,128]{3,2,1,0:T(8,128)} %load_ref.1, f32[3,2,192,128]{3,2,1,0:T(8,128)} %prev_ref.1, f32[12,2,192,128]{3,2,1,0:T(8,128)} %stress_ref.3, f32[2,192,128]{2,1,0:T(8,128)} %shear_far_ref.1, f32[2,192,128]{2,1,0:T(8,128)} %relax_far_ref.1), custom_call_target="tpu_custom_call" | custom-call | tf_op jit(solution)/shard_map/pallas_call | solution.py:667
  5.5 0.0 copy-start.8
  5.5 0.0 copy-start.9
  5.5 0.0 copy-start.1
  5.5 0.0 copy-start.2
  5.5 0.0 copy-start.3
  5.5 0.0 copy-start.4
  5.6 0.0 copy-start.5
  5.6 0.0 copy-start.6
  5.6 0.0 copy-start.7
  5.6 11.5 %all-to-all-start = ((f32[128,1,3328]{2,1,0:T(1,128)}), f32[128,1,3328]{2,1,0:T(1,128)S(1)}, u32[]{:S(2)}, u32[]{:S(2)}) async-start(f32[128,1,3328]{2,1,0:T(1,128)} %bitcast.12), calls=%async_computation | async-start | bytes 3407872 | tf_op jit(solution)/shard_map/all_to_all | solution.py:647
  17.1 0.0 copy-done.8
  17.1 0.1 reshape.37.stiff_ref
  17.2 0.0 copy-done.9
  17.2 0.1 reshape.41
  17.3 25.9 %all-to-all-done = f32[128,1,3328]{2,1,0:T(1,128)S(1)} async-done(((f32[128,1,3328]{2,1,0:T(1,128)}), f32[128,1,3328]{2,1,0:T(1,128)S(1)}, u32[]{:S(2)}, u32[]{:S(2)}) %all-to-all-start) | async-done | bytes 1703968 | tf_op jit(solution)/shard_map/all_to_all | solution.py:647
  43.2 0.0 copy-done.1
  43.2 0.0 copy-done.2
  43.2 0.0 copy-done.3
  43.2 0.0 copy-done.4
  43.2 0.0 copy-done.5
  43.2 0.0 copy-done.6
  43.2 0.0 copy-done.7
  43.2 13.5 %shard_map.167 = (f32[7,96,1536]{2,1,0:T(8,128)}, f32[512,128]{1,0:T(8,128)}) custom-call(f32[144]{0:T(256)S(1)} %reshape.37.stiff_ref, f32[3328,128]{1,0:T(8,128)S(1)} %bitcast.8, s32[8,128]{1,0:T(8,128)S(1)} %pad.4.slots_ref, bf16[512,256]{1,0:T(8,128)(2,1)S(1)} %copy-done.4, bf16[512,256]{1,0:T(8,128)(2,1)S(1)} %copy-done.3, ...), custom_call_target="tpu_custom_call" | custom-call | tf_op jit(solution)/shard_map/pallas_call | solution.py:678
  56.7 4.7 %all-to-all-start.1 = ((f32[128,1,512]{2,1,0:T(1,128)}), f32[128,1,512]{2,1,0:T(1,128)S(1)}, u32[]{:S(2)}, u32[]{:S(2)}) async-start(f32[128,1,512]{2,1,0:T(1,128)} %bitcast.14), calls=%async_computation.1 | async-start | bytes 524288 | tf_op jit(solution)/shard_map/all_to_all | solution.py:647
  61.4 11.0 %all-to-all-done.1 = f32[128,1,512]{2,1,0:T(1,128)S(1)} async-done(((f32[128,1,512]{2,1,0:T(1,128)}), f32[128,1,512]{2,1,0:T(1,128)S(1)}, u32[]{:S(2)}, u32[]{:S(2)}) %all-to-all-start.1) | async-done | bytes 262176 | tf_op jit(solution)/shard_map/all_to_all | solution.py:647
  72.4 0.0 copy-start
  72.4 3.7 %shard_map.168 = f32[1792,128]{1,0:T(8,128)} custom-call(s32[1]{0:T(128)} %bitcast.1.place_ref, f32[512,128]{1,0:T(8,128)S(1)} %bitcast.10, f32[7,96,1536]{2,1,0:T(8,128)} %get-tuple-element.8.kept_ref), custom_call_target="tpu_custom_call" | custom-call | tf_op jit(solution)/shard_map/pallas_call | solution.py:703
  76.1 4.6 %all-to-all-start.2 = ((f32[128,1,1792]{2,1,0:T(1,128)}), f32[128,1,1792]{2,1,0:T(1,128)S(1)}, u32[]{:S(2)}, u32[]{:S(2)}) async-start(f32[128,1,1792]{2,1,0:T(1,128)} %bitcast.13), calls=%async_computation.2 | async-start | bytes 1835008 | tf_op jit(solution)/shard_map/all_to_all | solution.py:647
  80.7 0.9 shard_map.170
  81.5 17.0 %all-to-all-done.2 = f32[128,1,1792]{2,1,0:T(1,128)S(1)} async-done(((f32[128,1,1792]{2,1,0:T(1,128)}), f32[128,1,1792]{2,1,0:T(1,128)S(1)}, u32[]{:S(2)}, u32[]{:S(2)}) %all-to-all-start.2) | async-done | bytes 917536 | tf_op jit(solution)/shard_map/all_to_all | solution.py:647
  98.6 0.0 copy-done
  98.6 3.8 %shard_map.169 = (f32[3,2,192,128]{3,2,1,0:T(8,128)}, f32[12,2,192,128]{3,2,1,0:T(8,128)}) custom-call(s32[1]{0:T(128)} %bitcast.parity_ref, f32[144]{0:T(256)S(1)} %reshape.37.stiff_ref, f32[1792,128]{1,0:T(8,128)S(1)} %bitcast.9, f32[12,2,192,128]{3,2,1,0:T(8,128)S(1)} %copy-done, f32[2,192,128]{2,1,0:T(8,128)} %shear_far_ref.1, f32[2,192,128]{2,1,0:T(8,128)} %relax_far_ref.1), custom_call_target="tpu_custom_call" | custom-call | tf_op jit(solution)/shard_map/pallas_call | solution.py:731
  (1 shorter events, 0.0 us)
Async XLA Ops:
  5.5 11.6 %copy-start.8 = (f32[12,12]{1,0:T(8,128)S(1)}, f32[12,12]{1,0:T(8,128)}, u32[]{:S(2)}) copy-start(f32[12,12]{1,0:T(8,128)} %param.21) | copy-start | bytes 1732
  5.5 11.7 %copy-start.9 = (s32[768]{0:T(1024)S(1)}, s32[768]{0:T(1024)}, u32[]{:S(2)}) copy-start(s32[768]{0:T(1024)} %param.22) | copy-start | bytes 9220
  5.5 37.7 %copy-start.1 = (bf16[256,512]{1,0:T(8,128)(2,1)S(1)}, bf16[256,512]{1,0:T(8,128)(2,1)}, u32[]{:S(2)}) copy-start(bf16[256,512]{1,0:T(8,128)(2,1)} %constant.51.clone.tl_ref) | copy-start | bytes 786436
  5.5 37.7 %copy-start.2 = (bf16[256,512]{1,0:T(8,128)(2,1)S(1)}, bf16[256,512]{1,0:T(8,128)(2,1)}, u32[]{:S(2)}) copy-start(bf16[256,512]{1,0:T(8,128)(2,1)} %constant.50.clone.th_ref) | copy-start | bytes 786436
  5.5 37.7 %copy-start.3 = (bf16[512,256]{1,0:T(8,128)(2,1)S(1)}, bf16[512,256]{1,0:T(8,128)(2,1)}, u32[]{:S(2)}) copy-start(bf16[512,256]{1,0:T(8,128)(2,1)} %constant.49.clone.fl_ref) | copy-start | bytes 786436
  5.5 37.7 %copy-start.4 = (bf16[512,256]{1,0:T(8,128)(2,1)S(1)}, bf16[512,256]{1,0:T(8,128)(2,1)}, u32[]{:S(2)}) copy-start(bf16[512,256]{1,0:T(8,128)(2,1)} %constant.48.clone.fh_ref) | copy-start | bytes 786436
  5.6 37.6 %copy-start.5 = (f32[32,8,128]{2,1,0:T(8,128)S(1)}, f32[32,8,128]{2,1,0:T(8,128)}, u32[]{:S(2)}) copy-start(f32[32,8,128]{2,1,0:T(8,128)} %constant.53.clone.ratio_ref) | copy-start | bytes 393220
  5.6 37.6 %copy-start.6 = (f32[2,8,256]{2,1,0:T(8,128)S(1)}, f32[2,8,256]{2,1,0:T(8,128)}, u32[]{:S(2)}) copy-start(f32[2,8,256]{2,1,0:T(8,128)} %constant.52.clone.twiddle_ref) | copy-start | bytes 49156
  5.6 37.6 %copy-start.7 = (f32[8,128]{1,0:T(8,128)S(1)}, f32[8,128]{1,0:T(8,128)}, u32[]{:S(2)}) copy-start(f32[8,128]{1,0:T(8,128)} %constant.54.clone.scale_ref) | copy-start | bytes 12292
  5.6 37.6 %all-to-all-start = ((f32[128,1,3328]{2,1,0:T(1,128)}), f32[128,1,3328]{2,1,0:T(1,128)S(1)}, u32[]{:S(2)}, u32[]{:S(2)}) async-start(f32[128,1,3328]{2,1,0:T(1,128)} %bitcast.12), calls=%async_computation | async-start | bytes 3407872 | tf_op jit(solution)/shard_map/all_to_all | solution.py:647
  56.7 15.7 %all-to-all-start.1 = ((f32[128,1,512]{2,1,0:T(1,128)}), f32[128,1,512]{2,1,0:T(1,128)S(1)}, u32[]{:S(2)}, u32[]{:S(2)}) async-start(f32[128,1,512]{2,1,0:T(1,128)} %bitcast.14), calls=%async_computation.1 | async-start | bytes 524288 | tf_op jit(solution)/shard_map/all_to_all | solution.py:647
  72.4 26.2 %copy-start = (f32[12,2,192,128]{3,2,1,0:T(8,128)S(1)}, f32[12,2,192,128]{3,2,1,0:T(8,128)}, u32[]{:S(2)}) copy-start(f32[12,2,192,128]{3,2,1,0:T(8,128)} %stress_ref.3) | copy-start | bytes 7077892
  76.1 22.4 %all-to-all-start.2 = ((f32[128,1,1792]{2,1,0:T(1,128)}), f32[128,1,1792]{2,1,0:T(1,128)S(1)}, u32[]{:S(2)}, u32[]{:S(2)}) async-start(f32[128,1,1792]{2,1,0:T(1,128)} %bitcast.13), calls=%async_computation.2 | async-start | bytes 1835008 | tf_op jit(solution)/shard_map/all_to_all | solution.py:647

commit v5 on v4

--- a/solution.py
+++ b/solution.py
@@ -95,51 +95,71 @@
     return jnp.where(row_index(x.shape) == n - 1, 0.0, pltpu.roll(x, n - 1, 0))
 
 
-def pack_kernel(parity_ref, density_ref, load_ref, prev_ref, stress_ref, shear_ref, relax_ref,
-                out_ref, acc_ref, tail_ref):
-    comp = pl.program_id(0)
+def pack_kernel(parity_ref, density_ref, load_far, prev_far, stress_far, shear_far, relax_far,
+                out_ref, load_ref, prev_ref, stress_ref, shear_ref, relax_ref, acc_ref, tail_ref,
+                sems):
     parity = parity_ref[0]
     wide = pl.ds(pl.multiple_of(64 * parity, 64), 128)
     narrow = pl.ds(pl.multiple_of(128 * (1 - parity), 64), 64)
+    copies = [
+        pltpu.make_async_copy(relax_far, relax_ref, sems.at[0]),
+        pltpu.make_async_copy(shear_far, shear_ref, sems.at[1]),
+    ]
+    for comp in range(3):
+        four = pl.ds(4 * comp, 4)
+        for far, near in (
+            (prev_far.at[comp], prev_ref.at[comp]),
+            (stress_far.at[four], stress_ref.at[four]),
+            (load_far.at[comp], load_ref.at[comp]),
+        ):
+            copies.append(pltpu.make_async_copy(far, near, sems.at[len(copies)]))
+    for copy in copies:
+        copy.start()
 
     def put(tile, block):
         out_ref[pl.ds(tile, LANES, stride=IN_TILES), :] = jnp.transpose(block)
 
-    @pl.when(comp == 0)
-    def _():
-        acc_ref[:2] = shear_ref[...] / (1.0 + 0.5 * relax_ref[...])
-        put(EFF_TILE, acc_ref[0, wide, :])
-        put(EFF_TILE + 1, acc_ref[1, wide, :])
-        put(EFF_TILE + 2, jnp.concatenate([acc_ref[0, narrow, :], acc_ref[1, narrow, :]], 0))
-        tail_ref[192:256, :] = jnp.zeros((64, LANES), f32)
-        for r in range(2):
-            tail_ref[201 + r : 202 + r, :] = jnp.full((1, LANES), density_ref[r], f32)
-
-    base = comp * 7
-    put(base, prev_ref[0, 0, wide, :])
-    put(base + 1, prev_ref[0, 1, wide, :])
-    put(base + 2, jnp.concatenate([prev_ref[0, 0, narrow, :], prev_ref[0, 1, narrow, :]], 0))
-
-    relax = relax_ref[...]
-    carried = relax / (1.0 + 0.5 * relax)
-    part = [[carried[r] * stress_ref[q, r] for r in range(2)] for q in range(4)]
-    near = [part[0][0], part[0][1] + part[2][0], part[2][1]]
-    far = [part[1][0], part[1][1] + part[3][0], part[3][1]]
-    for r in range(3):
-        total = near[r] + down_one(far[r])
-        if r < 2:
-            total = total + load_ref[0, r]
-        acc_ref[r] = total
-        tail_ref[pl.ds(192 + 3 * comp + r, 1), :] = far[r][COLS - 1 : COLS, :]
-    for r in range(3):
-        put(base + 3 + r, acc_ref[r, wide, :])
-    put(base + 6, jnp.concatenate([acc_ref[0, narrow, :], acc_ref[1, narrow, :]], 0))
-    tail_ref[pl.ds(pl.multiple_of(64 * comp, 64), 64), :] = acc_ref[2, narrow, :]
-
-    @pl.when(comp == 2)
-    def _():
-        put(TAIL_TILE, tail_ref[:128, :])
-        put(TAIL_TILE + 1, tail_ref[128:, :])
+    copies[0].wait()
+    copies[1].wait()
+    acc_ref[:2] = shear_ref[...] / (1.0 + 0.5 * relax_ref[...])
+    put(EFF_TILE, acc_ref[0, wide, :])
+    put(EFF_TILE + 1, acc_ref[1, wide, :])
+    put(EFF_TILE + 2, jnp.concatenate([acc_ref[0, narrow, :], acc_ref[1, narrow, :]], 0))
+    tail_ref[192:256, :] = jnp.zeros((64, LANES), f32)
+    for r in range(2):
+        tail_ref[201 + r : 202 + r, :] = jnp.full((1, LANES), density_ref[r], f32)
+
+    for comp in range(3):
+        base = comp * 7
+        copies[2 + 3 * comp].wait()
+        put(base, prev_ref[comp, 0, wide, :])
+        put(base + 1, prev_ref[comp, 1, wide, :])
+        rest = [prev_ref[comp, r, narrow, :] for r in range(2)]
+        put(base + 2, jnp.concatenate(rest, 0))
+
+        copies[3 + 3 * comp].wait()
+        copies[4 + 3 * comp].wait()
+        relax = relax_ref[...]
+        carried = relax / (1.0 + 0.5 * relax)
+        part = [
+            [carried[r] * stress_ref[4 * comp + q, r] for r in range(2)] for q in range(4)
+        ]
+        near = [part[0][0], part[0][1] + part[2][0], part[2][1]]
+        far = [part[1][0], part[1][1] + part[3][0], part[3][1]]
+        for r in range(3):
+            total = near[r] + down_one(far[r])
+            if r < 2:
+                total = total + load_ref[comp, r]
+            acc_ref[r] = total
+            place = 192 + 3 * comp + r
+            tail_ref[place : place + 1, :] = far[r][COLS - 1 : COLS, :]
+        for r in range(3):
+            put(base + 3 + r, acc_ref[r, wide, :])
+        put(base + 6, jnp.concatenate([acc_ref[0, narrow, :], acc_ref[1, narrow, :]], 0))
+        tail_ref[64 * comp : 64 * comp + 64, :] = acc_ref[2, narrow, :]
+
+    put(TAIL_TILE, tail_ref[:128, :])
+    put(TAIL_TILE + 1, tail_ref[128:, :])
 
 
 def section_kernel(stiff_ref, recv_ref, slots_ref, fh_ref, fl_ref, th_ref, tl_ref, twiddle_ref,
@@ -442,12 +462,16 @@
         leaving(slot).wait()
 
 
-def solve_kernel(place_ref, moments_ref, kept_ref, out_ref, x_ref, basis_ref, sems):
-    def arriving(slot):
-        return pltpu.make_async_copy(kept_ref.at[slot], basis_ref.at[slot], sems.at[slot])
-
-    for slot in range(7):
-        arriving(slot).start()
+def solve_kernel(place_ref, moments_ref, kept_ref, out_ref, x_ref, basis_ref, packed_ref, sems,
+                 out_sems):
+    def arriving(slot, half):
+        return pltpu.make_async_copy(
+            kept_ref.at[slot, :, half], basis_ref.at[slot, :, half], sems.at[half, slot]
+        )
+
+    for half in (1, 0):
+        for slot in range(7):
+            arriving(slot, half).start()
     table = jnp.transpose(moments_ref[pl.ds(3, LANES, stride=MID_TILES), :])
     diagonal, beside, start = table[0:8], table[8:16], table[16:17]
     first = row_index((8, LANES)) == 0
@@ -477,60 +501,64 @@
         y, norm = y + size * direction, new
     mine = lane_index((8, LANES)) == place_ref[0]
     own = jnp.sum(jnp.where(mine, y * table[24:32], 0.0), 1, keepdims=True)
-    for group in ((0, 1, 2), (3, 4), (5, 6)):
-        for slot in group:
-            arriving(slot).wait()
-        x = basis_ref[0] if group[0] == 0 else x_ref[...]
-        for slot in group:
-            if slot:
-                x = x + own[slot - 1 : slot, :] * basis_ref[slot]
-        x_ref[...] = x
-
-    lane = lane_index((16, LANES))
-
-    def node_rows(c, r, k):
-        start = 32 * c + 8 * (r % 2)
-        block = jnp.concatenate(
-            [x_ref[start : start + 8, tile_of(k)], x_ref[start + 16 : start + 24, tile_of(k)]], 0
-        )
-        return up_one(block) if r == 2 else block
-
-    def at(t, tile):
-        return pl.ds(OUT_TILES * t + tile, 16, stride=8 * OUT_TILES)
-
-    for u in range(4):
-        even, odd = 2 * u, 2 * u + 1
-        for c in range(3):
-            for r in range(3):
-                out_ref[at(even, 4 * c + r), :] = node_rows(c, r, 3 * u)
-                out_ref[at(odd, 4 * c + r), :] = node_rows(c, r, 3 * u + 2)
-            low, high = node_rows(c, 0, 3 * u + 1), node_rows(c, 1, 3 * u + 1)
-            out_ref[at(even, 4 * c + 3), :] = jnp.where(lane < 64, low, pltpu.roll(high, 64, 1))
-            out_ref[at(odd, 4 * c + 3), :] = jnp.where(lane < 64, pltpu.roll(low, 64, 1), high)
-        extra = [node_rows(c, 2, 3 * u + 1) for c in range(3)]
-        out_ref[at(even, OUT_TAIL), :] = jnp.where(
-            lane < 64, extra[0], pltpu.roll(extra[1], 64, 1)
-        )
-        out_ref[at(odd, OUT_TAIL), :] = jnp.where(
-            lane < 64, pltpu.roll(extra[0], 64, 1), extra[1]
-        )
-        for parity, rows in ((0, even), (1, odd)):
-            block = extra[2] if parity == 0 else pltpu.roll(extra[2], 64, 1)
-            following = (2 * u + parity + 1) % 8
-            k, source = 3 * (following // 2) + following % 2, 64 * (following % 2)
+    lane = lane_index((8, LANES))
+    last_row = row_index((8, LANES)) == 7
+
+    def leaving(half):
+        rows = pl.ds(64 * OUT_TILES * half, 64 * OUT_TILES)
+        return pltpu.make_async_copy(packed_ref.at[rows], out_ref.at[rows], out_sems.at[half])
+
+    for half in (1, 0):
+        for slot in range(7):
+            arriving(slot, half).wait()
+        x = basis_ref[0, :, half]
+        for i in range(6):
+            x = x + own[i : i + 1, :][None] * basis_ref[1 + i, :, half]
+        x_ref[:, half] = x
+
+        def node_rows(c, r, k):
+            block = x_ref[c, half, 8 * (r % 2) : 8 * (r % 2) + 8, tile_of(k)]
+            if r < 2:
+                return block
+            beyond = x_ref[c, 1, 0:1, tile_of(k)] if half == 0 else 0.0
+            return jnp.where(last_row, beyond, pltpu.roll(block, 7, 0))
+
+        def put(t, tile, block):
+            start = OUT_TILES * (64 * half + t) + tile
+            packed_ref[pl.ds(start, 8, stride=8 * OUT_TILES), :] = block
+
+        for u in range(4):
+            even, odd = 2 * u, 2 * u + 1
             for c in range(3):
                 for r in range(3):
-                    target = 64 + 3 * c + r
-                    value = pltpu.roll(node_rows(c, r, k), (target - source) % LANES, 1)
-                    block = jnp.where(lane == target, value, block)
-            out_ref[at(rows, OUT_TAIL + 1), :] = block
+                    put(even, 4 * c + r, node_rows(c, r, 3 * u))
+                    put(odd, 4 * c + r, node_rows(c, r, 3 * u + 2))
+                low, high = node_rows(c, 0, 3 * u + 1), node_rows(c, 1, 3 * u + 1)
+                put(even, 4 * c + 3, jnp.where(lane < 64, low, pltpu.roll(high, 64, 1)))
+                put(odd, 4 * c + 3, jnp.where(lane < 64, pltpu.roll(low, 64, 1), high))
+            extra = [node_rows(c, 2, 3 * u + 1) for c in range(3)]
+            put(even, OUT_TAIL, jnp.where(lane < 64, extra[0], pltpu.roll(extra[1], 64, 1)))
+            put(odd, OUT_TAIL, jnp.where(lane < 64, pltpu.roll(extra[0], 64, 1), extra[1]))
+            for parity, t in ((0, even), (1, odd)):
+                block = extra[2] if parity == 0 else pltpu.roll(extra[2], 64, 1)
+                following = (t + 1) % 8
+                k, source = 3 * (following // 2) + following % 2, 64 * (following % 2)
+                for c in range(3):
+                    for r in range(3):
+                        target = 64 + 3 * c + r
+                        value = pltpu.roll(node_rows(c, r, k), (target - source) % LANES, 1)
+                        block = jnp.where(lane == target, value, block)
+                put(t, OUT_TAIL + 1, block)
+        leaving(half).start()
+    for half in range(2):
+        leaving(half).wait()
 
 
 def finish_kernel(parity_ref, stiff_ref, recv_ref, stress_ref, shear_far_ref, relax_far_ref,
                   x_out_ref, stress_out_ref, x_ref, new_ref, matrix_ref, shear_ref, relax_ref,
                   first_ref, x_sems, sems):
-    shear_arriving = pltpu.make_async_copy(shear_far_ref, shear_ref, sems.at[3])
-    relax_arriving = pltpu.make_async_copy(relax_far_ref, relax_ref, sems.at[4])
+    shear_arriving = pltpu.make_async_copy(shear_far_ref, shear_ref, sems.at[4])
+    relax_arriving = pltpu.make_async_copy(relax_far_ref, relax_ref, sems.at[5])
     shear_arriving.start()
     relax_arriving.start()
     parity = parity_ref[0]
@@ -544,7 +572,7 @@
         return pltpu.make_async_copy(x_ref.at[c, 0:2, 0:COLS], x_out_ref.at[c], x_sems.at[c])
 
     def leaving(part):
-        rows = pl.ds(64 * part, 64)
+        rows = pl.ds((0, 64, 128, 160)[part], (64, 64, 32, 32)[part])
         return pltpu.make_async_copy(
             new_ref.at[:, :, rows], stress_out_ref.at[:, :, rows], sems.at[part]
         )
@@ -613,11 +641,11 @@
     leaving(0).start()
     for n in range(4, COLS // 16):
         store(n, forces(n))
-        if n % 4 == 3:
-            leaving(n // 4).start()
+        if n in (7, 9, 11):
+            leaving((n - 5) // 2).start()
     for c in range(3):
         x_leaving(c).wait()
-    for part in range(3):
+    for part in range(4):
         leaving(part).wait()
 
 
@@ -661,16 +689,21 @@
     (fh, fl), (th, tl), twiddle = transform_tables()
     ratio, scale, radius = radial_tables()
 
-    one = pl.BlockSpec((1, 2, COLS, LANES), lambda c: (c, 0, 0, 0))
-    four = pl.BlockSpec((4, 2, COLS, LANES), lambda c: (c, 0, 0, 0))
-    field = whole((2, COLS, LANES))
     packed = pl.pallas_call(
         pack_kernel,
-        grid=(3,),
-        in_specs=[smem, smem, one, one, four, field, field],
-        out_specs=whole((IN_TILES * LANES, LANES)),
+        in_specs=[smem, smem] + [pl.BlockSpec(memory_space=pl.ANY)] * 5,
+        out_specs=pl.BlockSpec(memory_space=pltpu.VMEM),
         out_shape=pltpu.HBM((IN_TILES * LANES, LANES), f32),
-        scratch_shapes=[pltpu.VMEM((3, COLS, LANES), f32), pltpu.VMEM((256, LANES), f32)],
+        scratch_shapes=[
+            pltpu.VMEM((3, 2, COLS, LANES), f32),
+            pltpu.VMEM((3, 2, COLS, LANES), f32),
+            pltpu.VMEM((12, 2, COLS, LANES), f32),
+            pltpu.VMEM((2, COLS, LANES), f32),
+            pltpu.VMEM((2, COLS, LANES), f32),
+            pltpu.VMEM((3, COLS, LANES), f32),
+            pltpu.VMEM((256, LANES), f32),
+            pltpu.SemaphoreType.DMA((11,)),
+        ],
         compiler_params=params(12),
     )(parity, *[far_memory(x) for x in (density_jump, load, previous, stress_old, shear_modulus, relaxation)])
     received = exchanged(packed)
@@ -708,15 +741,17 @@
             whole((MID_TILES * LANES, LANES)),
             pl.BlockSpec(memory_space=pl.ANY),
         ],
-        out_specs=whole((OUT_TILES * LANES, LANES)),
+        out_specs=pl.BlockSpec(memory_space=pl.ANY),
         out_shape=pltpu.HBM((OUT_TILES * LANES, LANES), f32),
         scratch_shapes=[
-            pltpu.VMEM((96, HRING), f32),
-            pltpu.VMEM((7, 96, HRING), f32),
-            pltpu.SemaphoreType.DMA((7,)),
+            pltpu.VMEM((3, 2, 16, HRING), f32),
+            pltpu.VMEM((7, 3, 2, 16, HRING), f32),
+            pltpu.VMEM((OUT_TILES * LANES, LANES), f32),
+            pltpu.SemaphoreType.DMA((2, 7)),
+            pltpu.SemaphoreType.DMA((2,)),
         ],
         compiler_params=params(12),
-    )(place, shared, far_memory(basis))
+    )(place, shared, far_memory(basis.reshape(7, 3, 2, 16, HRING)))
     returned = exchanged(back)
 
     potential = pl.pallas_call(
@@ -746,7 +781,7 @@
             pltpu.VMEM((2, COLS, LANES), f32),
             pltpu.VMEM((4, COLS, 2 * LANES), f32),
             pltpu.SemaphoreType.DMA((3,)),
-            pltpu.SemaphoreType.DMA((5,)),
+            pltpu.SemaphoreType.DMA((6,)),
         ],
         compiler_params=params(12),
     )(parity, stiff, returned, stress_old, far_memory(shear_modulus), far_memory(relaxation))

time: 103 us -> 102 us (level)
  no operation moved by 1% of the time
where the time goes in v5:
time: 102 us
  waiting for transfers between devices  53.9 us (53%)
  Pallas kernels  26.1 us (26%)
  starting transfers between devices  20.7 us (20%)
    all_to_all x3, waiting for transfers between devices, exchanged(): return lax.all_to_all(rows, ALL, 0, 0, tiled=True).reshape(count, LANES)  53.9 us
    all_to_all x3, starting transfers between devices, exchanged(): return lax.all_to_all(rows, ALL, 0, 0, tiled=True).reshape(count, LANES)  20.7 us
    pallas_call x1, Pallas kernels, body(): pl.pallas_call(functools.partial(section_kernel, radius=[float(x) for x i...  13.5 us
    pallas_call x1, Pallas kernels, body(): pl.pallas_call(pack_kernel, in_specs=[smem, smem] + [pl.BlockSpec(memory_...  4.54 us
    pallas_call x1, Pallas kernels, body(): pl.pallas_call(finish_kernel, in_specs=[smem, smem] + [pl.BlockSpec(memor...  3.77 us
    pallas_call x1, Pallas kernels, body(): pl.pallas_call(solve_kernel, grid=(1,), in_specs=[smem, whole((MID_TILES...  3.43 us
  transfers between devices with their start and end apart: 3, of which 3 were waited for; matrix products, arithmetic and copies ran while one was open for 0% of the time, Pallas kernels for 1%

profile of v5, /device:TPU:1, one launch (start us, length us, event | category | flops | bytes accessed | tf_op | source)
XLA Modules:
  0.0 101.8 jit_solution(4844941996787070188)
XLA Ops:
  0.6 4.5 %shard_map.166 = f32[3328,128]{1,0:T(8,128)} custom-call(s32[1]{0:T(128)} %bitcast.parity_ref, f32[2]{0:T(128)} %density_ref.1, f32[3,2,192,128]{3,2,1,0:T(8,128)} %load_far.1, f32[3,2,192,128]{3,2,1,0:T(8,128)} %prev_far.1, f32[12,2,192,128]{3,2,1,0:T(8,128)} %stress_ref.1, f32[2,192,128]{2,1,0:T(8,128)} %shear_far_ref.1, f32[2,192,128]{2,1,0:T(8,128)} %relax_far_ref.1), custom_call_target="tpu_custom_call" | custom-call | tf_op jit(solution)/shard_map/pallas_call | solution.py:692
  5.2 0.0 copy-start.8
  5.2 0.0 copy-start.9
  5.2 0.0 copy-start.1
  5.2 0.0 copy-start.2
  5.2 0.0 copy-start.3
  5.3 0.0 copy-start.4
  5.3 0.0 copy-start.5
  5.3 0.0 copy-start.6
  5.3 0.0 copy-start.7
  5.3 11.5 %all-to-all-start = ((f32[128,1,3328]{2,1,0:T(1,128)}), f32[128,1,3328]{2,1,0:T(1,128)S(1)}, u32[]{:S(2)}, u32[]{:S(2)}) async-start(f32[128,1,3328]{2,1,0:T(1,128)} %bitcast.13), calls=%async_computation | async-start | bytes 3407872 | tf_op jit(solution)/shard_map/all_to_all | solution.py:675
  16.8 0.0 copy-done.8
  16.8 0.1 reshape.40.stiff_ref
  16.9 0.0 copy-done.9
  16.9 0.1 reshape.44
  17.0 25.9 %all-to-all-done = f32[128,1,3328]{2,1,0:T(1,128)S(1)} async-done(((f32[128,1,3328]{2,1,0:T(1,128)}), f32[128,1,3328]{2,1,0:T(1,128)S(1)}, u32[]{:S(2)}, u32[]{:S(2)}) %all-to-all-start) | async-done | bytes 1703968 | tf_op jit(solution)/shard_map/all_to_all | solution.py:675
  42.9 0.0 copy-done.1
  42.9 0.0 copy-done.2
  42.9 0.0 copy-done.3
  42.9 0.0 copy-done.4
  42.9 0.0 copy-done.5
  42.9 0.0 copy-done.6
  42.9 0.0 copy-done.7
  43.0 13.5 %shard_map.167 = (f32[7,96,1536]{2,1,0:T(8,128)}, f32[512,128]{1,0:T(8,128)}) custom-call(f32[144]{0:T(256)S(1)} %reshape.40.stiff_ref, f32[3328,128]{1,0:T(8,128)S(1)} %bitcast.9, s32[8,128]{1,0:T(8,128)S(1)} %pad.4.slots_ref, bf16[512,256]{1,0:T(8,128)(2,1)S(1)} %copy-done.4, bf16[512,256]{1,0:T(8,128)(2,1)S(1)} %copy-done.3, ...), custom_call_target="tpu_custom_call" | custom-call | tf_op jit(solution)/shard_map/pallas_call | solution.py:711
  56.4 4.7 %all-to-all-start.1 = ((f32[128,1,512]{2,1,0:T(1,128)}), f32[128,1,512]{2,1,0:T(1,128)S(1)}, u32[]{:S(2)}, u32[]{:S(2)}) async-start(f32[128,1,512]{2,1,0:T(1,128)} %bitcast.16), calls=%async_computation.1 | async-start | bytes 524288 | tf_op jit(solution)/shard_map/all_to_all | solution.py:675
  61.1 11.0 %all-to-all-done.1 = f32[128,1,512]{2,1,0:T(1,128)S(1)} async-done(((f32[128,1,512]{2,1,0:T(1,128)}), f32[128,1,512]{2,1,0:T(1,128)S(1)}, u32[]{:S(2)}, u32[]{:S(2)}) %all-to-all-start.1) | async-done | bytes 262176 | tf_op jit(solution)/shard_map/all_to_all | solution.py:675
  72.1 0.0 copy-start
  72.1 3.4 %shard_map.168 = f32[1792,128]{1,0:T(8,128)} custom-call(s32[1]{0:T(128)} %bitcast.1.place_ref, f32[512,128]{1,0:T(8,128)S(1)} %bitcast.11, f32[7,3,2,16,1536]{4,3,2,1,0:T(8,128)} %bitcast.14), custom_call_target="tpu_custom_call" | custom-call | tf_op jit(solution)/shard_map/pallas_call | solution.py:736
  75.6 4.6 %all-to-all-start.2 = ((f32[128,1,1792]{2,1,0:T(1,128)}), f32[128,1,1792]{2,1,0:T(1,128)S(1)}, u32[]{:S(2)}, u32[]{:S(2)}) async-start(f32[128,1,1792]{2,1,0:T(1,128)} %bitcast.15), calls=%async_computation.2 | async-start | bytes 1835008 | tf_op jit(solution)/shard_map/all_to_all | solution.py:675
  80.1 0.9 shard_map.170
  81.0 17.0 %all-to-all-done.2 = f32[128,1,1792]{2,1,0:T(1,128)S(1)} async-done(((f32[128,1,1792]{2,1,0:T(1,128)}), f32[128,1,1792]{2,1,0:T(1,128)S(1)}, u32[]{:S(2)}, u32[]{:S(2)}) %all-to-all-start.2) | async-done | bytes 917536 | tf_op jit(solution)/shard_map/all_to_all | solution.py:675
  98.0 0.0 copy-done
  98.0 3.8 %shard_map.169 = (f32[3,2,192,128]{3,2,1,0:T(8,128)}, f32[12,2,192,128]{3,2,1,0:T(8,128)}) custom-call(s32[1]{0:T(128)} %bitcast.parity_ref, f32[144]{0:T(256)S(1)} %reshape.40.stiff_ref, f32[1792,128]{1,0:T(8,128)S(1)} %bitcast.10, f32[12,2,192,128]{3,2,1,0:T(8,128)S(1)} %copy-done, f32[2,192,128]{2,1,0:T(8,128)} %shear_far_ref.1, f32[2,192,128]{2,1,0:T(8,128)} %relax_far_ref.1), custom_call_target="tpu_custom_call" | custom-call | tf_op jit(solution)/shard_map/pallas_call | solution.py:766
  (1 shorter events, 0.0 us)
Async XLA Ops:
  5.2 11.6 %copy-start.8 = (f32[12,12]{1,0:T(8,128)S(1)}, f32[12,12]{1,0:T(8,128)}, u32[]{:S(2)}) copy-start(f32[12,12]{1,0:T(8,128)} %param.21) | copy-start | bytes 1732
  5.2 11.7 %copy-start.9 = (s32[768]{0:T(1024)S(1)}, s32[768]{0:T(1024)}, u32[]{:S(2)}) copy-start(s32[768]{0:T(1024)} %param.22) | copy-start | bytes 9220
  5.2 37.7 %copy-start.1 = (bf16[256,512]{1,0:T(8,128)(2,1)S(1)}, bf16[256,512]{1,0:T(8,128)(2,1)}, u32[]{:S(2)}) copy-start(bf16[256,512]{1,0:T(8,128)(2,1)} %constant.51.clone.tl_ref) | copy-start | bytes 786436
  5.2 37.7 %copy-start.2 = (bf16[256,512]{1,0:T(8,128)(2,1)S(1)}, bf16[256,512]{1,0:T(8,128)(2,1)}, u32[]{:S(2)}) copy-start(bf16[256,512]{1,0:T(8,128)(2,1)} %constant.50.clone.th_ref) | copy-start | bytes 786436
  5.2 37.7 %copy-start.3 = (bf16[512,256]{1,0:T(8,128)(2,1)S(1)}, bf16[512,256]{1,0:T(8,128)(2,1)}, u32[]{:S(2)}) copy-start(bf16[512,256]{1,0:T(8,128)(2,1)} %constant.49.clone.fl_ref) | copy-start | bytes 786436
  5.3 37.7 %copy-start.4 = (bf16[512,256]{1,0:T(8,128)(2,1)S(1)}, bf16[512,256]{1,0:T(8,128)(2,1)}, u32[]{:S(2)}) copy-start(bf16[512,256]{1,0:T(8,128)(2,1)} %constant.48.clone.fh_ref) | copy-start | bytes 786436
  5.3 37.7 %copy-start.5 = (f32[32,8,128]{2,1,0:T(8,128)S(1)}, f32[32,8,128]{2,1,0:T(8,128)}, u32[]{:S(2)}) copy-start(f32[32,8,128]{2,1,0:T(8,128)} %constant.53.clone.ratio_ref) | copy-start | bytes 393220
  5.3 37.7 %copy-start.6 = (f32[2,8,256]{2,1,0:T(8,128)S(1)}, f32[2,8,256]{2,1,0:T(8,128)}, u32[]{:S(2)}) copy-start(f32[2,8,256]{2,1,0:T(8,128)} %constant.52.clone.twiddle_ref) | copy-start | bytes 49156
  5.3 37.6 %copy-start.7 = (f32[8,128]{1,0:T(8,128)S(1)}, f32[8,128]{1,0:T(8,128)}, u32[]{:S(2)}) copy-start(f32[8,128]{1,0:T(8,128)} %constant.54.clone.scale_ref) | copy-start | bytes 12292
  5.3 37.6 %all-to-all-start = ((f32[128,1,3328]{2,1,0:T(1,128)}), f32[128,1,3328]{2,1,0:T(1,128)S(1)}, u32[]{:S(2)}, u32[]{:S(2)}) async-start(f32[128,1,3328]{2,1,0:T(1,128)} %bitcast.13), calls=%async_computation | async-start | bytes 3407872 | tf_op jit(solution)/shard_map/all_to_all | solution.py:675
  56.4 15.7 %all-to-all-start.1 = ((f32[128,1,512]{2,1,0:T(1,128)}), f32[128,1,512]{2,1,0:T(1,128)S(1)}, u32[]{:S(2)}, u32[]{:S(2)}) async-start(f32[128,1,512]{2,1,0:T(1,128)} %bitcast.16), calls=%async_computation.1 | async-start | bytes 524288 | tf_op jit(solution)/shard_map/all_to_all | solution.py:675
  72.1 25.9 %copy-start = (f32[12,2,192,128]{3,2,1,0:T(8,128)S(1)}, f32[12,2,192,128]{3,2,1,0:T(8,128)}, u32[]{:S(2)}) copy-start(f32[12,2,192,128]{3,2,1,0:T(8,128)} %stress_ref.1) | copy-start | bytes 7077892
  75.6 22.4 %all-to-all-start.2 = ((f32[128,1,1792]{2,1,0:T(1,128)}), f32[128,1,1792]{2,1,0:T(1,128)S(1)}, u32[]{:S(2)}, u32[]{:S(2)}) async-start(f32[128,1,1792]{2,1,0:T(1,128)} %bitcast.15), calls=%async_computation.2 | async-start | bytes 1835008 | tf_op jit(solution)/shard_map/all_to_all | solution.py:675
